TPU v7x, 32 devices: a whole 2x2x4 slice. The times are simulated.
32 devices in a mesh: pa: 8 (over y, x, core), pb: 4 (over z).
Axes of the slice: x: 2, y: 2, z: 4, core: 2. Of those that a mesh axis runs over, the one named last changes fastest.
Arguments:
- queries: bfloat16 [4096, 1024], P(('pa', 'pb')), may hold values from -900 to 900
- batch_hidden: bfloat16 [512, 1024], P(('pa', 'pb')), may hold values from -6 to 6
- pool_hidden: bfloat16 [16384, 1024], P(('pa', 'pb')), may hold values from -6 to 6
- projection: bfloat16 [1024, 1024], replicated, may hold values from -0.1875 to 0.1875
- hard_ids: int32 [4096, 16], P(('pa', 'pb')), may hold values from 0 to 2047, as said below
- query_group: int32 [4096], P(('pa', 'pb')), may hold values from 0 to 63
- labels: int32 [4096], P(('pa', 'pb')), may hold values from 0 to 63
- group_lists: int32 [64, 64], replicated, may hold values from 0 to 127, as said below
Outputs:
- query_grad: bfloat16 [4096, 1024], P(('pa', 'pb'))
- batch_hidden_grad: bfloat16 [512, 1024], P(('pa', 'pb'))
- pool_hidden_grad: bfloat16 [16384, 1024], P(('pa', 'pb'))
Inputs may be any that keep to these rules, and one draw needn't show every extreme that they name: `hard_ids`: entry k of a query's list lies in [(k % 4) * 512, (k % 4 + 1) * 512); entries may repeat. `group_lists`: each row holds 64 different values.
All inputs are finite; a program needn't handle non-finite values.
Results may differ from a plain program's by a relative error of at most 0.017.
The roundings to bfloat16 on the way count: a program that leaves them out, or rounds other values in their place, can miss the bound.
Values may be sent and summed in bfloat16 or wider, within the bound.
No kernel may reach another device: no remote copies, remote signals or barrier semaphores. Data moves between devices by JAX's collectives and lax.ppermute only.
A program may use at most 128 MiB of HBM per device.

v0:
```python
import math

import jax
import jax.numpy as jnp
from jax import lax
from jax.sharding import PartitionSpec as P

D = 1024


def pick_rows(table, wanted):
    flat = wanted.reshape(-1)
    table_iota = lax.broadcasted_iota(jnp.int32, (flat.shape[0], table.shape[0]), 1)
    selector = (flat[:, None] == table_iota).astype(jnp.bfloat16)
    found = jnp.dot(selector, table, preferred_element_type=jnp.float32).astype(table.dtype)
    return found.reshape(wanted.shape + (table.shape[1],))


def add_rows(wanted, values, count):
    flat = wanted.reshape(-1)
    row_iota = lax.broadcasted_iota(jnp.int32, (count, flat.shape[0]), 0)
    selector = (row_iota == flat[None, :]).astype(jnp.bfloat16)
    return jnp.dot(selector, values.reshape(flat.shape[0], -1), preferred_element_type=jnp.float32)


def shards(
    queries, batch_hidden, pool_hidden, projection, hard_ids, query_group, labels, group_lists
):
    score_scale = 1.0 / math.sqrt(D)
    owners = lax.axis_size("pb")
    query_rows = queries.shape[0]
    pool_count = pool_hidden.shape[0]
    hard_count = hard_ids.shape[1]
    per_owner = hard_count // owners
    group_size = group_lists.shape[1]
    group_total = group_lists.shape[0]
    dims = (((1,), (1,)), ((), ()))
    batch_proj = jnp.dot(batch_hidden, projection, preferred_element_type=jnp.float32).astype(
        jnp.bfloat16
    )
    pool_proj = jnp.dot(pool_hidden, projection, preferred_element_type=jnp.float32).astype(
        jnp.bfloat16
    )
    column = lax.all_gather(batch_proj, "pa", axis=0, tiled=True)
    column_count = column.shape[0]
    dense = lax.dot_general(queries, column, dims, preferred_element_type=jnp.float32) * score_scale
    group_iota = lax.broadcasted_iota(jnp.int32, (query_rows, group_total, group_size), 1)
    chosen = jnp.sum(
        jnp.where(query_group[:, None, None] == group_iota, group_lists[None, :, :], 0), axis=1
    )
    column_iota = lax.broadcasted_iota(jnp.int32, (query_rows, group_size, column_count), 2)
    member = chosen[:, :, None] == column_iota
    group_scores = jnp.sum(jnp.where(member, dense[:, None, :], 0.0), axis=2)
    owner_of = lax.broadcasted_iota(jnp.int32, hard_ids.shape, 1) % owners
    local_rows = hard_ids - owner_of * pool_count
    requests = (
        local_rows.reshape(query_rows, per_owner, owners)
        .transpose(2, 0, 1)
        .reshape(owners, query_rows * per_owner)
    )
    received = lax.all_to_all(requests, "pb", split_axis=0, concat_axis=0, tiled=True)
    copies = lax.all_gather(queries, "pb", axis=0, tiled=True).reshape(owners, query_rows, D)
    picked = pick_rows(pool_proj, received).reshape(owners, query_rows, per_owner, D)
    owner_scores = (
        jnp.einsum("sid,sijd->sij", copies, picked, preferred_element_type=jnp.float32)
        * score_scale
    )
    returned = lax.all_to_all(owner_scores, "pb", split_axis=0, concat_axis=0, tiled=True)
    hard_scores = returned.transpose(1, 2, 0).reshape(query_rows, hard_count)
    scores = jnp.concatenate([group_scores, hard_scores], axis=1)
    likely = jax.nn.softmax(scores, axis=1)
    positions = lax.broadcasted_iota(jnp.int32, scores.shape, 1)
    target = (positions == labels[:, None]).astype(jnp.float32)
    dscore = (likely - target).astype(jnp.bfloat16)
    grad_group = dscore[:, :group_size]
    grad_hard = dscore[:, group_size:].reshape(query_rows, per_owner, owners).transpose(2, 0, 1)
    dense_grad = jnp.einsum(
        "ic,icr->ir", grad_group, member.astype(jnp.bfloat16), preferred_element_type=jnp.float32
    ).astype(jnp.bfloat16)
    group_term = jnp.dot(dense_grad, column, preferred_element_type=jnp.float32)
    batch_part = (
        lax.dot_general(
            dense_grad, queries, (((0,), (0,)), ((), ())), preferred_element_type=jnp.float32
        )
        * score_scale
    )
    batch_grad = lax.psum_scatter(batch_part, "pa", scatter_dimension=0, tiled=True)
    sent_back = lax.all_to_all(grad_hard, "pb", split_axis=0, concat_axis=0, tiled=True)
    contrib = (
        score_scale
        * sent_back.astype(jnp.float32)[..., None]
        * copies.astype(jnp.float32)[:, :, None, :]
    )
    contrib = contrib.astype(jnp.bfloat16)
    pool_grad = add_rows(received, contrib, pool_count)
    owner_term = jnp.einsum("sij,sijd->sid", sent_back, picked, preferred_element_type=jnp.float32)
    gathered_terms = lax.all_to_all(owner_term, "pb", split_axis=0, concat_axis=0, tiled=True)
    hard_term = jnp.sum(gathered_terms, axis=0)
    query_grad = (score_scale * (group_term + hard_term)).astype(jnp.bfloat16)
    batch_hidden_grad = lax.dot_general(
        batch_grad.astype(jnp.bfloat16), projection, dims, preferred_element_type=jnp.float32
    ).astype(jnp.bfloat16)
    pool_hidden_grad = lax.dot_general(
        pool_grad.astype(jnp.bfloat16), projection, dims, preferred_element_type=jnp.float32
    ).astype(jnp.bfloat16)
    return (query_grad, batch_hidden_grad, pool_hidden_grad)


def solution(mesh):
    return jax.shard_map(
        shards,
        mesh=mesh,
        in_specs=(
            P(("pa", "pb"), None),
            P(("pa", "pb"), None),
            P(("pa", "pb"), None),
            P(),
            P(("pa", "pb"), None),
            P(("pa", "pb")),
            P(("pa", "pb")),
            P(),
        ),
        out_specs=(P(("pa", "pb"), None), P(("pa", "pb"), None), P(("pa", "pb"), None)),
        check_vma=False,
    )
```

profile of v0, /device:TPU:0, one launch (start us, length us, event | category | flops | bytes accessed | tf_op | source)
XLA Modules:
  0.0 145.6 jit_solution(15382826161694779296)
XLA Ops:
  7.2 0.7 all-gather.2.cloned.1.call-update
  7.9 0.8 multiply_subtract_fusion
  8.7 0.2 copy.23
  8.9 0.8 all_to_all.20
  9.7 6.3 %all-to-all-start = ((s32[4,1,512]{2,1,0:T(1,128)}), s32[4,1,512]{2,1,0:T(1,128)S(1)}, u32[]{:S(2)}, u32[]{:S(2)}) async-start(s32[4,1,512]{2,1,0:T(1,128)} %all_to_all.20), calls=%async_computation | async-start | bytes 16384 | tf_op jit(solution)/shard_map/all_to_all | solution.py:61
  16.0 1.1 convolution_convert_fusion.3
  17.1 9.3 %all_gather.6 = bf16[128,1024]{1,0:T(8,128)(2,1)S(1)} all-gather(bf16[16,1024]{1,0:T(8,128)(2,1)S(1)} %convolution_convert_fusion.3), channel_id=1, replica_groups=mesh['pa'=8,'pb'=4] {'pa'}, dimensions={0}, use_global_device_ids=true | all-gather | bytes 294912 | tf_op jit(solution)/shard_map/all_gather | solution.py:44
  26.4 1.2 fusion.13
  27.6 1.4 select_reduce_fusion.1
  29.3 6.6 %fusion.4 = bf16[2048,1024]{1,0:T(8,128)(2,1)} fusion(s32[2048]{0:T(1024)S(1)} %bitcast.47, bf16[512,1024]{1,0:T(8,128)(2,1)} %param.10, bf16[1024,1024]{1,0:T(8,128)(2,1)S(1)} %copy-done), kind=kOutput, calls=%fused_computation.9 | convolution fusion | flops 3224895488 | bytes 7348224 | tf_op jit(solution)/shard_map/dot_general | solution.py:15
  35.8 7.2 %reshape_reshape.3 = bf16[4,128,4,1024]{3,2,1,0:T(4,128)(2,1)} reshape(bf16[2048,1024]{1,0:T(8,128)(2,1)} %fusion.4) | data formatting | bytes 8388608 | tf_op jit(solution)/shard_map/reshape;reshape | solution.py:63
  43.0 6.8 %fusion.8 = f32[4,128,1,4]{3,2,1,0:T(1,128)S(1)} fusion(bf16[4,128,4,1024]{3,2,1,0:T(4,128)(2,1)} %reshape_reshape.3, bf16[4,128,1024,1]{2,1,0,3:T(8,128)(2,1)} %bitcast.37), kind=kOutput, calls=%fused_computation.16 | convolution fusion | flops 4194304 | bytes 5251072 | tf_op jit(solution)/shard_map/sid,sijd->sij/dot_general | solution.py:65
  49.9 0.6 bitcast_multiply_fusion
  50.6 5.1 %all-to-all-start.1 = ((f32[4,128,4]{1,2,0:T(4,128)}), f32[4,128,4]{1,2,0:T(4,128)S(1)}, u32[]{:S(2)}, u32[]{:S(2)}) async-start(f32[4,128,4]{1,2,0:T(4,128)} %bitcast_multiply_fusion), calls=%async_computation.1 | async-start | bytes 16384 | tf_op jit(solution)/shard_map/all_to_all | solution.py:68
  55.6 2.6 %select_reduce_fusion = f32[128,64]{1,0:T(8,128)S(1)} fusion(f32[128,128]{1,0:T(8,128)S(1)} %copy.22, s32[128,64]{1,0:T(8,128)S(1)} %copy.21), kind=kLoop, calls=%fused_computation.5 | loop fusion | flops 3137536 | bytes 131072 | tf_op jit(solution)/shard_map/reduce_sum | solution.py:53
  58.3 2.9 %all-to-all-done.1 = f32[4,128,4]{1,2,0:T(4,128)S(1)} async-done(((f32[4,128,4]{1,2,0:T(4,128)}), f32[4,128,4]{1,2,0:T(4,128)S(1)}, u32[]{:S(2)}, u32[]{:S(2)}) %all-to-all-start.1) | async-done | bytes 8224 | tf_op jit(solution)/shard_map/all_to_all | solution.py:68
  61.4 0.2 fusion.19
  61.9 7.9 %all_to_all.25 = bf16[4,128,4]{1,2,0:T(4,128)(2,1)S(1)} all-to-all(bf16[4,128,4]{1,2,0:T(4,128)(2,1)S(1)} %copy.28), channel_id=1, replica_groups=mesh['pa'=8,'pb'=4] {'pb'}, dimensions={0} | all-to-all | bytes 8192 | tf_op jit(solution)/shard_map/all_to_all | solution.py:88
  69.8 0.2 copy.34
  70.0 4.5 %fusion.20 = f32[4,128,1,1024]{3,2,1,0:T(1,128)S(1)} fusion(bf16[4,128,4,1]{2,3,1,0:T(2,128)(2,1)S(1)} %copy.34, bf16[4,128,4,1024]{3,2,1,0:T(4,128)(2,1)} %reshape_reshape.3), kind=kOutput, calls=%fused_computation.45 | convolution fusion | flops 4194304 | bytes 6295552 | tf_op jit(solution)/shard_map/sij,sijd->sid/dot_general | solution.py:96
  74.5 1.8 %copy.41 = f32[4,128,1,1024]{3,1,0,2:T(8,128)} copy(f32[4,128,1,1024]{3,2,1,0:T(1,128)S(1)} %fusion.20) | data formatting | bytes 4194304 | tf_op jit(solution)/shard_map/sij,sijd->sid/dot_general | solution.py:96
  76.3 4.4 %all-to-all-start.3 = ((f32[4,128,1024]{2,1,0:T(8,128)}), f32[4,128,1024]{2,1,0:T(8,128)}, u32[]{:S(2)}, u32[]{:S(2)}) async-start(f32[4,128,1024]{2,1,0:T(8,128)} %bitcast.36), calls=%async_computation.3 | async-start | bytes 4194304 | tf_op jit(solution)/shard_map/all_to_all | solution.py:97
  80.8 5.5 %mul.62 = f32[4,128,4,1024]{3,2,1,0:T(4,128)} broadcast(bf16[4,128,1024]{2,1,0:T(8,128)(2,1)S(1)} %bitcast.38), dimensions={0,1,3} | broadcast | bytes 9437184 | tf_op jit(solution)/shard_map/mul | solution.py:90
  86.3 10.0 %mul.63 = f32[2048,1024]{1,0:T(8,128)} reshape(f32[4,128,4,1024]{3,2,1,0:T(4,128)} %mul.62) | data formatting | bytes 16777216 | tf_op jit(solution)/shard_map/mul | solution.py:90
  96.3 1.8 %fusion.2 = f32[128,1,128]{2,1,0:T(1,128)S(1)} fusion(s32[128,64]{1,0:T(8,128)S(1)} %copy.21, bf16[128,64,1]{1,0,2:T(8,128)(2,1)S(1)} %slice_bitcast_fusion), kind=kOutput, calls=%fused_computation.7 | convolution fusion | flops 3145728 | bytes 114688 | tf_op jit(solution)/shard_map/ic,icr->ir/dot_general | solution.py:77
  98.1 1.1 convolution_multiply_fusion
  99.4 0.2 mul.60
  99.6 7.9 %convolution_convert_fusion = bf16[512,1024]{1,0:T(8,128)(2,1)} fusion(bf16[1024,1024]{1,0:T(8,128)(2,1)S(1)} %copy-done, f32[2048,1024]{1,0:T(8,128)} %mul.63, f32[2048]{0:T(1024)S(1)} %mul.60, s32[2048]{0:T(1024)S(1)} %bitcast.48), kind=kOutput, calls=%fused_computation.19 | convolution fusion | flops 3227516928 | bytes 11550720 | tf_op jit(solution)/shard_map/dot_general | solution.py:103
  107.5 26.5 %reduce-scatter.2.cloned.1.call-done = f32[16,1024]{1,0:T(8,128)} async-done(((f32[128,1024]{1,0:T(8,128)}), f32[16,1024]{1,0:T(8,128)}) %reduce-scatter.2.cloned.1.call-update) | async-done | bytes 65552 | tf_op jit(solution)/shard_map/reduce_scatter | solution.py:87
  133.9 2.1 %convolution_convert_fusion.2 = bf16[16,1024]{1,0:T(8,128)(2,1)} fusion(bf16[1024,1024]{1,0:T(8,128)(2,1)S(1)} %copy-done, f32[16,1024]{1,0:T(8,128)} %reduce-scatter.2.cloned.1.call-done), kind=kOutput, calls=%fused_computation.27 | convolution fusion | flops 33587200 | bytes 2195456 | tf_op jit(solution)/shard_map/dot_general | solution.py:100
  136.1 1.8 %reduce_sum.39 = f32[128,1024]{1,0:T(8,128)S(1)} reduce(f32[4,128,1024]{2,1,0:T(8,128)} %all-to-all-done.3, f32[]{:T(128)} %constant.11.clone.1), dimensions={0}, to_apply=%region_5.6 | reduce | flops 393216 | bytes 2621444 | tf_op jit(solution)/shard_map/reduce_sum | solution.py:98
  137.9 0.9 fusion.12
  (31 shorter events, 1.1 us)
Async XLA Ops:
  7.2 8.8 %copy-start = (bf16[1024,1024]{1,0:T(8,128)(2,1)S(1)}, bf16[1024,1024]{1,0:T(8,128)(2,1)}, u32[]{:S(2)}) copy-start(bf16[1024,1024]{1,0:T(8,128)(2,1)} %param.11) | copy-start | bytes 6291460
  7.2 35.9 %all-gather.2.cloned.1.call-start = ((), (), s32[]{:S(2)}) async-start(), calls=%async_computation.5 | async-start | bytes 1310720 | tf_op jit(solution)/shard_map/all_gather | solution.py:62
  9.7 19.6 %all-to-all-start = ((s32[4,1,512]{2,1,0:T(1,128)}), s32[4,1,512]{2,1,0:T(1,128)S(1)}, u32[]{:S(2)}, u32[]{:S(2)}) async-start(s32[4,1,512]{2,1,0:T(1,128)} %all_to_all.20), calls=%async_computation | async-start | bytes 16384 | tf_op jit(solution)/shard_map/all_to_all | solution.py:61
  43.0 18.5 %copy-start.3 = (s32[128]{0:T(128)S(1)}, s32[128]{0:T(128)}, u32[]{:S(2)}) copy-start(s32[128]{0:T(128)} %param.14) | copy-start | bytes 1540
  50.6 10.7 %all-to-all-start.1 = ((f32[4,128,4]{1,2,0:T(4,128)}), f32[4,128,4]{1,2,0:T(4,128)S(1)}, u32[]{:S(2)}, u32[]{:S(2)}) async-start(f32[4,128,4]{1,2,0:T(4,128)} %bitcast_multiply_fusion), calls=%async_computation.1 | async-start | bytes 16384 | tf_op jit(solution)/shard_map/all_to_all | solution.py:68
  74.5 6.3 %copy-start.2 = (bf16[512,1024]{1,0:T(8,128)(2,1)S(1)}, bf16[512,1024]{1,0:T(8,128)(2,1)}, u32[]{:S(2)}) copy-start(bf16[512,1024]{1,0:T(8,128)(2,1)} %all-gather.2.cloned.1.call-done) | copy-start | bytes 3145732
  76.3 59.8 %all-to-all-start.3 = ((f32[4,128,1024]{2,1,0:T(8,128)}), f32[4,128,1024]{2,1,0:T(8,128)}, u32[]{:S(2)}, u32[]{:S(2)}) async-start(f32[4,128,1024]{2,1,0:T(8,128)} %bitcast.36), calls=%async_computation.3 | async-start | bytes 4194304 | tf_op jit(solution)/shard_map/all_to_all | solution.py:97
  80.7 53.2 %reduce-scatter.2.cloned.1.call-start = ((), (), s32[]{:S(2)}) async-start(), calls=%async_computation.6 | async-start | bytes 589824 | tf_op jit(solution)/shard_map/reduce_scatter | solution.py:87
  86.3 11.8 %copy-start.1 = (bf16[128,1024]{1,0:T(8,128)(2,1)S(1)}, bf16[128,1024]{1,0:T(8,128)(2,1)}, u32[]{:S(2)}) copy-start(bf16[128,1024]{1,0:T(8,128)(2,1)} %param.8) | copy-start | bytes 786436
Sparse Core Ops, SparseCore 0:
  9.6 30.6 all-gather.1
  99.4 34.5 reduce-scatter.1
where the time goes:
time: 147 us; the launch traced here: 146 us
  matrix products  34 us (23%)
  waiting for transfers between devices  30.1 us (20%)
  local copies, waits for them, and re-layouts  26.5 us (18%)
  blocking collectives  17.2 us (12%)
  starting transfers between devices  16 us (11%)
  between operations  14.2 us (10%)
  other arithmetic  7.67 us (5%)
    reduce_scatter x1, waiting for transfers between devices, shards(): lax.psum_scatter(batch_part, 'pa', scatter_dimension=0, tiled=True)  26.5 us
    mul x4, local copies, waits for them, and re-layouts, shards(): score_scale * sent_back.astype(jnp.float32)[..., None]  15.8 us
    all_gather x1, blocking collectives, shards(): column = lax.all_gather(batch_proj, 'pa', axis=0, tiled=True)  9.29 us
    all_to_all x1, blocking collectives, shards(): lax.all_to_all(grad_hard, 'pb', split_axis=0, concat_axis=0, tiled=True)  7.94 us
    dot_general x1, matrix products, shards(): lax.dot_general(pool_grad.astype(jnp.bfloat16), projection, dims, preferr...  7.86 us
    another operation x1, local copies, waits for them, and re-layouts, shards(): pick_rows(pool_proj, received).reshape(owners, query_rows, per_owner, D)  7.2 us
    dot_general x1, matrix products, shards(): jnp.einsum('sid,sijd->sij', copies, picked, preferred_element_type=jnp.fl...  6.77 us
    dot_general x1, matrix products, pick_rows(): jnp.dot(selector, table, preferred_element_type=jnp.float32)  6.57 us
  transfers between devices with their start and end apart: 5, of which 2 were waited for; matrix products, arithmetic and copies ran while one was open for 34% of the time, Pallas kernels for 0%

commit v1 on v0

v1 whole, which is shorter than its diff:
```python
import functools
import math

import jax
import jax.numpy as jnp
from jax import lax
from jax.experimental import pallas as pl
from jax.experimental.pallas import tpu as pltpu
from jax.sharding import PartitionSpec as P

F32 = jnp.float32
BF16 = jnp.bfloat16
LANE_BASE = 16


def nt(a, b):
    return lax.dot_general(a, b, (((1,), (1,)), ((), ())), preferred_element_type=F32)


def tn(a, b):
    return lax.dot_general(a, b, (((0,), (0,)), ((), ())), preferred_element_type=F32)


def local_ids(packed_ref, me, rows, owners, per):
    width = rows
    found = None
    for owner in range(owners):
        parts = []
        for j in range(per):
            k = owner * per + j
            block, sub = divmod(k, 8)
            high = packed_ref[rows : rows + 8, 2 * block * width : (2 * block + 1) * width]
            low = packed_ref[rows : rows + 8, (2 * block + 1) * width : (2 * block + 2) * width]
            ids = high.astype(F32) * LANE_BASE + low.astype(F32)
            parts.append(ids[sub : sub + 1, :])
        if found is None:
            found = parts
        else:
            found = [jnp.where(me == owner, new, old) for new, old in zip(parts, found)]
    return found


def owner_kernel(rows, owners, per, scale, me_ref, packed_ref, table_ref, score_ref, term_ref):
    me = me_ref[0]
    count = table_ref.shape[0]
    ids = local_ids(packed_ref, me, rows, owners, per)
    query = packed_ref[:rows, :]
    dense = nt(table_ref[...], query)
    row_iota = lax.broadcasted_iota(jnp.int32, (count, rows), 0).astype(F32)
    hits = [row_iota == one for one in ids]
    scores = [jnp.sum(jnp.where(hit, dense, 0.0), axis=0, keepdims=True) * scale for hit in hits]
    top = functools.reduce(jnp.maximum, scores)
    weight = jnp.zeros((count, rows), F32)
    for hit, one in zip(hits, scores):
        weight = weight + jnp.where(hit, jnp.exp(one - top), 0.0)
    for j, one in enumerate(scores):
        score_ref[j : j + 1, :] = one
    term_ref[...] = tn(weight.astype(BF16), table_ref[...]).astype(BF16)


def group_kernel(scale, query_ref, column_ref, group_ref, lists_ref, score_ref, place_ref):
    rows = query_ref.shape[0]
    groups, size = lists_ref.shape
    count = column_ref.shape[0]
    score_ref[...] = nt(column_ref[...], query_ref[...]) * scale
    column_iota = lax.broadcasted_iota(jnp.int32, (groups, count), 1)
    places = jnp.zeros((groups, count), F32)
    lists = lists_ref[...]
    for c in range(size):
        places = places + jnp.where(lists[:, c : c + 1] == column_iota, float(c + 1), 0.0)
    group_iota = lax.broadcasted_iota(jnp.int32, (groups, rows), 0)
    mine = (group_iota == group_ref[...]).astype(BF16)
    place_ref[...] = tn(places.astype(BF16), mine)


def soft_kernel(owners, per, scale, *refs):
    score_ref, place_ref, label_ref, query_ref, column_ref, own_term_ref = refs[:6]
    hard_refs = refs[6 : 6 + owners]
    grad_refs = refs[6 + owners : 6 + 2 * owners]
    part_ref, sum_ref, factor_ref = refs[6 + 2 * owners :]
    rows = query_ref.shape[0]
    place = place_ref[...]
    member = place > 0.5
    dense = score_ref[...]
    tops = [jnp.max(ref[...], axis=0, keepdims=True) for ref in hard_refs]
    top = jnp.max(jnp.where(member, dense, -jnp.inf), axis=0, keepdims=True)
    top = functools.reduce(jnp.maximum, tops, top)
    power = jnp.where(member, jnp.exp(jnp.where(member, dense - top, 0.0)), 0.0)
    hard = [jnp.exp(ref[...] - top) for ref in hard_refs]
    total = jnp.sum(power, axis=0, keepdims=True)
    for one in hard:
        total = total + jnp.sum(one, axis=0, keepdims=True)
    target = (place == (label_ref[...] + 1).astype(F32)).astype(F32)
    grad = jnp.where(member, power / total - target, 0.0).astype(BF16)
    for ref, one in zip(grad_refs, hard):
        ref[...] = (one / total).astype(BF16)
    part_ref[...] = (
        lax.dot_general(grad, query_ref[...], (((1,), (0,)), ((), ())), preferred_element_type=F32)
        * scale
    ).astype(BF16)
    factor = [jnp.exp(one - top) / total for one in tops]
    factor = jnp.concatenate(factor + [jnp.zeros((rows - owners, rows), F32)], axis=0)
    factor = factor.T
    factor_ref[...] = factor
    sum_ref[...] = tn(grad, column_ref[...]) + factor[:, :1] * own_term_ref[...].astype(F32)


def pool_kernel(rows, owners, per, scale, me_ref, *refs):
    packed_refs = refs[:owners]
    grad_refs = refs[owners : 2 * owners]
    out_ref = refs[2 * owners]
    me = me_ref[0]
    count = out_ref.shape[0]
    row_iota = lax.broadcasted_iota(jnp.int32, (count, rows), 0).astype(F32)
    total = None
    for packed_ref, grad_ref in zip(packed_refs, grad_refs):
        ids = local_ids(packed_ref, me, rows, owners, per)
        grad = grad_ref[...].astype(F32)
        weight = jnp.zeros((count, rows), F32)
        for j, one in enumerate(ids):
            weight = weight + jnp.where(row_iota == one, grad[j : j + 1, :], 0.0)
        part = jnp.dot(
            weight.astype(BF16), packed_ref[:rows, :], preferred_element_type=F32
        )
        total = part if total is None else total + part
    out_ref[...] = (total * scale).astype(BF16)


def whole(count):
    return [pl.BlockSpec(memory_space=pltpu.VMEM)] * count


def call(kernel, outs, arrays, scalars=(), flops=0):
    outs = [jax.ShapeDtypeStruct(*one) for one in outs]
    moved = sum(a.size * a.dtype.itemsize for a in list(arrays) + outs)
    return pl.pallas_call(
        kernel,
        out_shape=outs,
        in_specs=[pl.BlockSpec(memory_space=pltpu.SMEM)] * len(scalars) + whole(len(arrays)),
        out_specs=whole(len(outs)),
        cost_estimate=pl.CostEstimate(flops=flops, bytes_accessed=moved, transcendentals=0),
    )(*scalars, *arrays)


def shards(
    queries, batch_hidden, pool_hidden, projection, hard_ids, query_group, labels, group_lists
):
    rows, depth = queries.shape
    scale = 1.0 / math.sqrt(depth)
    owners = lax.axis_size("pb")
    pool_count = pool_hidden.shape[0]
    hard_count = hard_ids.shape[1]
    per = hard_count // owners
    me = lax.axis_index("pb").astype(jnp.int32).reshape(1)

    ids = hard_ids.T.reshape(per, owners, rows).transpose(1, 0, 2)
    ids = ids - (jnp.arange(owners, dtype=jnp.int32) * pool_count)[:, None, None]
    ids = ids.reshape(hard_count // 8, 8, rows)
    pieces = []
    for block in range(hard_count // 8):
        pieces.append((ids[block] // LANE_BASE).astype(BF16))
        pieces.append((ids[block] % LANE_BASE).astype(BF16))
    tail = jnp.concatenate(pieces, axis=1)
    tail = jnp.pad(tail, ((0, 0), (0, depth - tail.shape[1])))
    packed = jnp.concatenate([queries, tail], axis=0)

    def shift(x, k):
        return lax.ppermute(x, "pb", [(i, (i + k) % owners) for i in range(owners)])

    blocks = [packed] + [shift(packed, k) for k in range(1, owners)]
    hidden = lax.all_gather(batch_hidden, "pa", axis=0, tiled=True)
    table = jnp.dot(pool_hidden, projection, preferred_element_type=F32).astype(BF16)
    column = jnp.dot(hidden, projection, preferred_element_type=F32).astype(BF16)
    column_count = column.shape[0]

    scores, place = call(
        functools.partial(group_kernel, scale),
        [((column_count, rows), F32), ((column_count, rows), F32)],
        [queries, column, query_group[None, :], group_lists],
        flops=2 * rows * column_count * depth,
    )
    hards, terms = [], []
    for block in blocks:
        hard, term = call(
            functools.partial(owner_kernel, rows, owners, per, scale),
            [((per, rows), F32), ((rows, depth), BF16)],
            [block, table],
            [me],
            flops=4 * rows * pool_count * depth,
        )
        hards.append(hard)
        terms.append(term)
    hards = [hards[0]] + [shift(hards[k], owners - k) for k in range(1, owners)]
    terms = [terms[0]] + [shift(terms[k], owners - k) for k in range(1, owners)]
    outs = call(
        functools.partial(soft_kernel, owners, per, scale),
        [((per, rows), BF16)] * owners
        + [((column_count, depth), BF16), ((rows, depth), F32), ((rows, rows), F32)],
        [scores, place, labels[None, :], queries, column, terms[0]] + hards,
        flops=4 * rows * column_count * depth,
    )
    grads, (part, total, factor) = outs[:owners], outs[owners:]
    grads = [grads[0]] + [shift(grads[k], k) for k in range(1, owners)]
    part = part.reshape(-1, batch_hidden.shape[0], depth)
    part = lax.all_to_all(part, "pa", split_axis=0, concat_axis=0, tiled=True)
    batch_grad = jnp.sum(part.astype(F32), axis=0).astype(BF16)
    batch_hidden_grad = nt(batch_grad, projection).astype(BF16)
    (pool_grad,) = call(
        functools.partial(pool_kernel, rows, owners, per, scale),
        [((pool_count, depth), BF16)],
        blocks + grads,
        [me],
        flops=2 * rows * owners * pool_count * depth,
    )
    pool_hidden_grad = nt(pool_grad, projection).astype(BF16)
    for k in range(1, owners):
        total = total + factor[:, k : k + 1] * terms[k].astype(F32)
    query_grad = (scale * total).astype(BF16)
    return (query_grad, batch_hidden_grad, pool_hidden_grad)


def solution(mesh):
    return jax.shard_map(
        shards,
        mesh=mesh,
        in_specs=(
            P(("pa", "pb"), None),
            P(("pa", "pb"), None),
            P(("pa", "pb"), None),
            P(),
            P(("pa", "pb"), None),
            P(("pa", "pb")),
            P(("pa", "pb")),
            P(),
        ),
        out_specs=(P(("pa", "pb"), None), P(("pa", "pb"), None), P(("pa", "pb"), None)),
        check_vma=False,
    )
```

time: 147 us -> 76 us (0.52)
  waiting for transfers between devices: 30.1 us -> 0.03 us
  matrix products: 34 us -> 9.35 us
  local copies, waits for them, and re-layouts: 26.5 us -> 4.48 us
  Pallas kernels: 0 us -> 20.9 us
  between operations: 14.2 us -> 0.78 us
  starting transfers between devices: 16 us -> 26.4 us
  blocking collectives: 17.2 us -> 9.51 us
  other arithmetic: 7.67 us -> 3.9 us
    reduce_scatter x1 -> x0, waiting for transfers between devices: 26.5 us -> none  [shards(): lax.psum_scatter(batch_part, 'pa', scatter_dimension=0, tiled=True)]
    dot_general x10 -> x4, matrix products: 34 us -> 9.35 us  [the longest x2 4.76 us: nt(): lax.dot_general(a, b, (((1,), (1,)), ((), ())), preferred_element_type=F32)]
    ppermute x0 -> x12, starting transfers between devices: none -> 22.9 us  [shift(): return lax.ppermute(x, 'pb', [(i, (i + k) % owners) for i in range(owners)])]
    pallas_call x0 -> x7, Pallas kernels: none -> 20.9 us  [call(): pl.pallas_call(kernel, out_shape=outs, in_specs=[pl.BlockSpec(memory_spac...]
    mul x5 -> x0, local copies, waits for them, and re-layouts: 15.9 us -> none  [the longest x4 15.8 us: shards(): score_scale * sent_back.astype(jnp.float32)[..., None]]
    all_to_all x3 -> x1, starting transfers between devices: 15.9 us -> 3.42 us  [shards(): part = lax.all_to_all(part, 'pa', split_axis=0, concat_axis=0, tiled=True)]
    all_to_all x1 -> x0, blocking collectives: 7.94 us -> none  [shards(): lax.all_to_all(grad_hard, 'pb', split_axis=0, concat_axis=0, tiled=True)]
    another operation x1 -> x0, local copies, waits for them, and re-layouts: 7.2 us -> none  [shards(): pick_rows(pool_proj, received).reshape(owners, query_rows, per_owner, D)]
  transfers between devices with their start and end apart: 5 -> 13, of which waited for: 2 -> 0; matrix products, arithmetic and copies ran while one was open for 34% -> 14% of each run, Pallas kernels for 0% -> 28%
where the time goes in v1:
time: 76 us; the launch traced here: 75.3 us
  starting transfers between devices  26.4 us (35%)
  Pallas kernels  20.9 us (28%)
  blocking collectives  9.51 us (13%)
  matrix products  9.35 us (12%)
  local copies, waits for them, and re-layouts  4.48 us (6%)
  other arithmetic  3.9 us (5%)
  between operations  0.78 us (1%)
    ppermute x12, starting transfers between devices, shift(): return lax.ppermute(x, 'pb', [(i, (i + k) % owners) for i in range(owners)])  22.9 us
    pallas_call x7, Pallas kernels, call(): pl.pallas_call(kernel, out_shape=outs, in_specs=[pl.BlockSpec(memory_spac...  20.9 us
    all_gather x1, blocking collectives, shards(): hidden = lax.all_gather(batch_hidden, 'pa', axis=0, tiled=True)  9.51 us
    dot_general x2, matrix products, nt(): lax.dot_general(a, b, (((1,), (1,)), ((), ())), preferred_element_type=F32)  4.76 us
    dot_general x1, matrix products, shards(): jnp.dot(pool_hidden, projection, preferred_element_type=F32).astype(BF16)  3.45 us
    all_to_all x1, starting transfers between devices, shards(): part = lax.all_to_all(part, 'pa', split_axis=0, concat_axis=0, tiled=True)  3.42 us
    unnamed x24, local copies, waits for them, and re-layouts  3.3 us
    convert_element_type x1, other arithmetic, shards(): query_grad = (scale * total).astype(BF16)  1.94 us
  transfers between devices with their start and end apart: 13, of which 0 were waited for; matrix products, arithmetic and copies ran while one was open for 14% of the time, Pallas kernels for 28%

profile of v1, /device:TPU:0, one launch (start us, length us, event | category | flops | bytes accessed | tf_op | source)
XLA Modules:
  0.0 75.3 jit_solution(8342220857671909944)
XLA Ops:
  0.7 0.9 %fusion.7 = s32[4,4,128]{2,1,0:T(4,128)S(1)} fusion(s32[4,4,128]{2,1,0:T(4,128)} %bitcast.22, s32[4]{0:T(128)S(1)} %iota_multiply_fusion), kind=kLoop, calls=%fused_computation.18 | loop fusion | flops 2048 | bytes 16400 | tf_op jit(solution)/shard_map/sub | solution.py:157
  1.6 1.0 %pad_maximum_fusion.packed_ref.refs_0_ = bf16[136,1024]{1,0:T(8,128)(2,1)S(1)} fusion(bf16[8,1024]{1,0:T(8,128)(2,1)S(1)} %fusion.6, bf16[128,1024]{1,0:T(8,128)(2,1)} %refs_3_.1), kind=kLoop, calls=%fused_computation.5 | loop fusion | flops 557056 | bytes 557056 | tf_op jit(solution)/shard_map/concatenate | solution.py:165
  2.6 5.1 %collective-permute-start.4 = (bf16[136,1024]{1,0:T(8,128)(2,1)S(1)}, bf16[136,1024]{1,0:T(8,128)(2,1)S(1)}, u32[]{:S(2)}, u32[]{:S(2)}) collective-permute-start(bf16[136,1024]{1,0:T(8,128)(2,1)S(1)} %pad_maximum_fusion.packed_ref.refs_0_), channel_id=1, source_target_pairs={{0,3},{1,0},{2,1},{3,2},{4,7},{5,4},{6,5},{7,6},{8,11},{9,8},{10,9... | collective-permute-start | bytes 835592 | tf_op jit(solution)/shard_map/ppermute | solution.py:168
  7.7 1.0 %collective-permute-start = (bf16[136,1024]{1,0:T(8,128)(2,1)S(1)}, bf16[136,1024]{1,0:T(8,128)(2,1)S(1)}, u32[]{:S(2)}, u32[]{:S(2)}) collective-permute-start(bf16[136,1024]{1,0:T(8,128)(2,1)S(1)} %pad_maximum_fusion.packed_ref.refs_0_), channel_id=1, source_target_pairs={{0,1},{1,2},{2,3},{3,0},{4,5},{5,6},{6,7},{7,4},{8,9},{9,10},{10,1... | collective-permute-start | bytes 835592 | tf_op jit(solution)/shard_map/ppermute | solution.py:168
  8.7 9.5 %all_gather.3 = bf16[128,1024]{1,0:T(8,128)(2,1)S(1)} all-gather(bf16[16,1024]{1,0:T(8,128)(2,1)} %param.9), channel_id=1, replica_groups=mesh['pa'=8,'pb'=4] {'pa'}, dimensions={0}, use_global_device_ids=true | all-gather | bytes 294912 | tf_op jit(solution)/shard_map/all_gather | solution.py:171
  18.3 3.4 %convolution_convert_fusion.1.table_ref = bf16[512,1024]{1,0:T(8,128)(2,1)} fusion(bf16[512,1024]{1,0:T(8,128)(2,1)} %param.10, bf16[1024,1024]{1,0:T(8,128)(2,1)S(1)} %copy-done), kind=kOutput, calls=%fused_computation.1 | convolution fusion | flops 1074266112 | bytes 4194304 | tf_op jit(solution)/shard_map/dot_general | solution.py:172
  21.7 3.1 %shard_map.104 = (f32[4,128]{1,0:T(4,128)}, bf16[128,1024]{1,0:T(8,128)(2,1)}) custom-call(s32[1]{0:T(128)} %bitcast.2.me_ref, bf16[136,1024]{1,0:T(8,128)(2,1)} %copy-done.1, bf16[512,1024]{1,0:T(8,128)(2,1)} %convolution_convert_fusion.1.table_ref), custom_call_target="tpu_custom_call" | custom-call | flops 268435456 | bytes 1591296 | tf_op jit(solution)/shard_map/pallas_call | solution.py:136
  24.8 1.1 %convolution_convert_fusion.2.column_ref.refs_4_ = bf16[128,1024]{1,0:T(8,128)(2,1)} fusion(bf16[128,1024]{1,0:T(8,128)(2,1)S(1)} %all_gather.3, bf16[1024,1024]{1,0:T(8,128)(2,1)S(1)} %copy-done), kind=kOutput, calls=%fused_computation.2 | convolution fusion | flops 268566528 | bytes 2621440 | tf_op jit(solution)/shard_map/dot_general | solution.py:173
  25.9 0.7 copy-done.2
  26.6 3.1 %shard_map.107 = (f32[4,128]{1,0:T(4,128)}, bf16[128,1024]{1,0:T(8,128)(2,1)}) custom-call(s32[1]{0:T(128)} %bitcast.2.me_ref, bf16[136,1024]{1,0:T(8,128)(2,1)} %copy-done.2, bf16[512,1024]{1,0:T(8,128)(2,1)} %convolution_convert_fusion.1.table_ref), custom_call_target="tpu_custom_call" | custom-call | flops 268435456 | bytes 1591296 | tf_op jit(solution)/shard_map/pallas_call | solution.py:136
  29.7 2.5 %collective-permute-start.5 = (f32[4,128]{1,0:T(4,128)}, f32[4,128]{1,0:T(4,128)S(1)}, u32[]{:S(2)}, u32[]{:S(2)}) collective-permute-start(f32[4,128]{1,0:T(4,128)} %get-tuple-element.26), channel_id=1, source_target_pairs={{0,1},{1,2},{2,3},{3,0},{4,5},{5,6},{6,7},{7,4},{8,9},{9,10},{10,1... | collective-permute-start | bytes 6152 | tf_op jit(solution)/shard_map/ppermute | solution.py:168
  32.2 0.7 copy-done.3
  32.9 3.1 %shard_map.106 = (f32[4,128]{1,0:T(4,128)}, bf16[128,1024]{1,0:T(8,128)(2,1)}) custom-call(s32[1]{0:T(128)} %bitcast.2.me_ref, bf16[136,1024]{1,0:T(8,128)(2,1)} %copy-done.3, bf16[512,1024]{1,0:T(8,128)(2,1)} %convolution_convert_fusion.1.table_ref), custom_call_target="tpu_custom_call" | custom-call | flops 268435456 | bytes 1591296 | tf_op jit(solution)/shard_map/pallas_call | solution.py:136
  36.0 0.9 %collective-permute-start.3 = (f32[4,128]{1,0:T(4,128)}, f32[4,128]{1,0:T(4,128)S(1)}, u32[]{:S(2)}, u32[]{:S(2)}) collective-permute-start(f32[4,128]{1,0:T(4,128)} %get-tuple-element.25), channel_id=1, source_target_pairs={{0,2},{1,3},{2,0},{3,1},{4,6},{5,7},{6,4},{7,5},{8,10},{9,11},{10,... | collective-permute-start | bytes 6152 | tf_op jit(solution)/shard_map/ppermute | solution.py:168
  36.9 0.7 copy-done.4
  37.7 3.1 %shard_map.105 = (f32[4,128]{1,0:T(4,128)}, bf16[128,1024]{1,0:T(8,128)(2,1)}) custom-call(s32[1]{0:T(128)} %bitcast.2.me_ref, bf16[136,1024]{1,0:T(8,128)(2,1)} %copy-done.4, bf16[512,1024]{1,0:T(8,128)(2,1)} %convolution_convert_fusion.1.table_ref), custom_call_target="tpu_custom_call" | custom-call | flops 268435456 | bytes 1591296 | tf_op jit(solution)/shard_map/pallas_call | solution.py:136
  40.8 1.5 %collective-permute-start.1 = (f32[4,128]{1,0:T(4,128)}, f32[4,128]{1,0:T(4,128)S(1)}, u32[]{:S(2)}, u32[]{:S(2)}) collective-permute-start(f32[4,128]{1,0:T(4,128)} %get-tuple-element.24), channel_id=1, source_target_pairs={{0,3},{1,0},{2,1},{3,2},{4,7},{5,4},{6,5},{7,6},{8,11},{9,8},{10,9... | collective-permute-start | bytes 6152 | tf_op jit(solution)/shard_map/ppermute | solution.py:168
  42.2 2.6 %shard_map.103 = (f32[128,128]{1,0:T(8,128)}, f32[128,128]{1,0:T(8,128)}) custom-call(bf16[128,1024]{1,0:T(8,128)(2,1)} %refs_3_.1, bf16[128,1024]{1,0:T(8,128)(2,1)} %convolution_convert_fusion.2.column_ref.refs_4_, s32[1,128]{1,0:T(1,128)} %bitcast.23, s32[64,64]{1,0:T(8,128)} %lists_ref.1), custom_call_target="tpu_custom_call" | custom-call | flops 33554432 | bytes 672256 | tf_op jit(solution)/shard_map/pallas_call | solution.py:136
  44.8 2.0 %collective-permute-start.6 = (bf16[128,1024]{1,0:T(8,128)(2,1)}, bf16[128,1024]{1,0:T(8,128)(2,1)S(1)}, u32[]{:S(2)}, u32[]{:S(2)}) collective-permute-start(bf16[128,1024]{1,0:T(8,128)(2,1)} %get-tuple-element.29), channel_id=1, source_target_pairs={{0,3},{1,0},{2,1},{3,2},{4,7},{5,4},{6,5},{7,6},{8,11},{9,8},{10,9... | collective-permute-start | bytes 786440 | tf_op jit(solution)/shard_map/ppermute | solution.py:168
  46.9 0.5 copy-done.6
  47.5 2.4 %shard_map.108 = (bf16[4,128]{1,0:T(4,128)(2,1)}, bf16[4,128]{1,0:T(4,128)(2,1)}, bf16[4,128]{1,0:T(4,128)(2,1)}, bf16[4,128]{1,0:T(4,128)(2,1)}, bf16[128,1024]...) custom-call(f32[128,128]{1,0:T(8,128)} %get-tuple-element.20.refs_0_, f32[128,128]{1,0:T(8,128)} %get-tuple-element.21.refs_1_, ...), custom_call_target="tpu_custom_call" | custom-call | flops 67108864 | bytes 1782272 | tf_op jit(solution)/shard_map/pallas_call | solution.py:136
  49.9 1.0 %collective-permute-start.9 = (bf16[4,128]{1,0:T(4,128)(2,1)}, bf16[4,128]{1,0:T(4,128)(2,1)S(1)}, u32[]{:S(2)}, u32[]{:S(2)}) collective-permute-start(bf16[4,128]{1,0:T(4,128)(2,1)} %get-tuple-element.34), channel_id=1, source_target_pairs={{0,1},{1,2},{2,3},{3,0},{4,5},{5,6},{6,7},{7,4},{8,9},{9,10},{10,1... | collective-permute-start | bytes 3080 | tf_op jit(solution)/shard_map/ppermute | solution.py:168
  50.9 2.0 %collective-permute-start.10 = (bf16[4,128]{1,0:T(4,128)(2,1)}, bf16[4,128]{1,0:T(4,128)(2,1)S(1)}, u32[]{:S(2)}, u32[]{:S(2)}) collective-permute-start(bf16[4,128]{1,0:T(4,128)(2,1)} %get-tuple-element.35), channel_id=1, source_target_pairs={{0,2},{1,3},{2,0},{3,1},{4,6},{5,7},{6,4},{7,5},{8,10},{9,11},{10,... | collective-permute-start | bytes 3080 | tf_op jit(solution)/shard_map/ppermute | solution.py:168
  52.8 2.9 %collective-permute-start.11 = (bf16[4,128]{1,0:T(4,128)(2,1)}, bf16[4,128]{1,0:T(4,128)(2,1)S(1)}, u32[]{:S(2)}, u32[]{:S(2)}) collective-permute-start(bf16[4,128]{1,0:T(4,128)(2,1)} %get-tuple-element.36), channel_id=1, source_target_pairs={{0,3},{1,0},{2,1},{3,2},{4,7},{5,4},{6,5},{7,6},{8,11},{9,8},{10,9... | collective-permute-start | bytes 3080 | tf_op jit(solution)/shard_map/ppermute | solution.py:168
  55.7 1.2 %slice_reduce_fusion.2 = (f32[128]{0:T(128)S(1)}, f32[128]{0:T(128)S(1)}, f32[128]{0:T(128)S(1)}) fusion(f32[128,128]{1,0:T(8,128)} %get-tuple-element.28), kind=kLoop, calls=%fused_computation.8 | loop fusion | bytes 3072 | tf_op jit(solution)/shard_map/slice | solution.py:217
  56.9 3.4 %all-to-all-start = ((bf16[8,16,1024]{2,1,0:T(8,128)(2,1)}), bf16[8,16,1024]{2,1,0:T(8,128)(2,1)S(1)}, u32[]{:S(2)}, u32[]{:S(2)}) async-start(bf16[8,16,1024]{2,1,0:T(8,128)(2,1)} %bitcast.19), calls=%async_computation | async-start | bytes 524288 | tf_op jit(solution)/shard_map/all_to_all | solution.py:205
  60.3 4.1 %collective-permute-start.8 = (bf16[128,1024]{1,0:T(8,128)(2,1)}, bf16[128,1024]{1,0:T(8,128)(2,1)}, u32[]{:S(2)}, u32[]{:S(2)}) collective-permute-start(bf16[128,1024]{1,0:T(8,128)(2,1)} %get-tuple-element.31), channel_id=1, source_target_pairs={{0,1},{1,2},{2,3},{3,0},{4,5},{5,6},{6,7},{7,4},{8,9},{9,10},{10,1... | collective-permute-start | bytes 786440 | tf_op jit(solution)/shard_map/ppermute | solution.py:168
  64.5 0.5 copy-done.10
  65.0 3.5 %shard_map.109 = bf16[512,1024]{1,0:T(8,128)(2,1)} custom-call(s32[1]{0:T(128)} %bitcast.2.me_ref, bf16[136,1024]{1,0:T(8,128)(2,1)} %copy-done.1, bf16[136,1024]{1,0:T(8,128)(2,1)} %copy-done.4, bf16[136,1024]{1,0:T(8,128)(2,1)} %copy-done.3, bf16[136,1024]{1,0:T(8,128)(2,1)} %copy-done.2, bf16[4,128]{1,0:T(4,128)(2,1)} %get-tuple-element.33.refs_4_, ...), custom_call_target="tpu_custom_call" | custom-call | flops 536870912 | bytes 2166784 | tf_op jit(solution)/shard_map/pallas_call | solution.py:136
  68.5 3.5 %convolution_convert_fusion = bf16[512,1024]{1,0:T(8,128)(2,1)} fusion(bf16[512,1024]{1,0:T(8,128)(2,1)} %shard_map.109, bf16[1024,1024]{1,0:T(8,128)(2,1)S(1)} %copy-done), kind=kOutput, calls=%fused_computation | convolution fusion | flops 1074266112 | bytes 4194304 | tf_op jit(solution)/shard_map/dot_general | solution.py:17
  72.0 1.3 %convolution_convert_fusion.3 = bf16[16,1024]{1,0:T(8,128)(2,1)} fusion(bf16[16,1024]{1,0:T(8,128)(2,1)S(1)} %reduce_sum.12, bf16[1024,1024]{1,0:T(8,128)(2,1)S(1)} %copy-done), kind=kOutput, calls=%fused_computation.3 | convolution fusion | flops 33570816 | bytes 2162688 | tf_op jit(solution)/shard_map/dot_general | solution.py:17
  73.3 1.9 %multiply_convert_fusion = bf16[128,1024]{1,0:T(8,128)(2,1)} fusion(bf16[128,1024]{1,0:T(8,128)(2,1)} %collective-permute-done.8, bf16[128,1024]{1,0:T(8,128)(2,1)S(1)} %collective-permute-done.7, f32[128,1024]{1,0:T(8,128)S(1)} %copy-done.5, bf16[128,1024]{1,0:T(8,128)(2,1)S(1)} %collective-permute-done.6, f32[128]{0:T(128)S(1)} %get-tuple-element.38, ...), kind=kLoop, calls=%fused_computation.4 | loop fusion | flops 1441792 | bytes 1574400 | tf_op jit(solution)/shard_map/convert_element_type | solution.py:218
  (39 shorter events, 0.2 us)
Async XLA Ops:
  0.6 17.6 %copy-start = (bf16[1024,1024]{1,0:T(8,128)(2,1)S(1)}, bf16[1024,1024]{1,0:T(8,128)(2,1)}, u32[]{:S(2)}) copy-start(bf16[1024,1024]{1,0:T(8,128)(2,1)} %param.11) | copy-start | bytes 6291460
  2.6 19.1 %copy-start.1 = (bf16[136,1024]{1,0:T(8,128)(2,1)}, bf16[136,1024]{1,0:T(8,128)(2,1)S(1)}, u32[]{:S(2)}) copy-start(bf16[136,1024]{1,0:T(8,128)(2,1)S(1)} %pad_maximum_fusion.packed_ref.refs_0_) | copy-start | bytes 835588
  2.6 23.3 %collective-permute-start.4 = (bf16[136,1024]{1,0:T(8,128)(2,1)S(1)}, bf16[136,1024]{1,0:T(8,128)(2,1)S(1)}, u32[]{:S(2)}, u32[]{:S(2)}) collective-permute-start(bf16[136,1024]{1,0:T(8,128)(2,1)S(1)} %pad_maximum_fusion.packed_ref.refs_0_), channel_id=1, source_target_pairs={{0,3},{1,0},{2,1},{3,2},{4,7},{5,4},{6,5},{7,6},{8,11},{9,8},{10,9... | collective-permute-start | bytes 835592 | tf_op jit(solution)/shard_map/ppermute | solution.py:168
  7.7 24.5 %collective-permute-start.2 = (bf16[136,1024]{1,0:T(8,128)(2,1)S(1)}, bf16[136,1024]{1,0:T(8,128)(2,1)S(1)}, u32[]{:S(2)}, u32[]{:S(2)}) collective-permute-start(bf16[136,1024]{1,0:T(8,128)(2,1)S(1)} %pad_maximum_fusion.packed_ref.refs_0_), channel_id=1, source_target_pairs={{0,2},{1,3},{2,0},{3,1},{4,6},{5,7},{6,4},{7,5},{8,10},{9,11},{10,... | collective-permute-start | bytes 835592 | tf_op jit(solution)/shard_map/ppermute | solution.py:168
  7.7 29.2 %collective-permute-start = (bf16[136,1024]{1,0:T(8,128)(2,1)S(1)}, bf16[136,1024]{1,0:T(8,128)(2,1)S(1)}, u32[]{:S(2)}, u32[]{:S(2)}) collective-permute-start(bf16[136,1024]{1,0:T(8,128)(2,1)S(1)} %pad_maximum_fusion.packed_ref.refs_0_), channel_id=1, source_target_pairs={{0,1},{1,2},{2,3},{3,0},{4,5},{5,6},{6,7},{7,4},{8,9},{9,10},{10,1... | collective-permute-start | bytes 835592 | tf_op jit(solution)/shard_map/ppermute | solution.py:168
  25.9 0.7 copy-start.2
  29.7 17.1 %collective-permute-start.5 = (f32[4,128]{1,0:T(4,128)}, f32[4,128]{1,0:T(4,128)S(1)}, u32[]{:S(2)}, u32[]{:S(2)}) collective-permute-start(f32[4,128]{1,0:T(4,128)} %get-tuple-element.26), channel_id=1, source_target_pairs={{0,1},{1,2},{2,3},{3,0},{4,5},{5,6},{6,7},{7,4},{8,9},{9,10},{10,1... | collective-permute-start | bytes 6152 | tf_op jit(solution)/shard_map/ppermute | solution.py:168
  32.2 0.7 copy-start.3
  36.0 10.8 %collective-permute-start.3 = (f32[4,128]{1,0:T(4,128)}, f32[4,128]{1,0:T(4,128)S(1)}, u32[]{:S(2)}, u32[]{:S(2)}) collective-permute-start(f32[4,128]{1,0:T(4,128)} %get-tuple-element.25), channel_id=1, source_target_pairs={{0,2},{1,3},{2,0},{3,1},{4,6},{5,7},{6,4},{7,5},{8,10},{9,11},{10,... | collective-permute-start | bytes 6152 | tf_op jit(solution)/shard_map/ppermute | solution.py:168
  36.9 0.7 copy-start.4
  40.8 6.1 %collective-permute-start.1 = (f32[4,128]{1,0:T(4,128)}, f32[4,128]{1,0:T(4,128)S(1)}, u32[]{:S(2)}, u32[]{:S(2)}) collective-permute-start(f32[4,128]{1,0:T(4,128)} %get-tuple-element.24), channel_id=1, source_target_pairs={{0,3},{1,0},{2,1},{3,2},{4,7},{5,4},{6,5},{7,6},{8,11},{9,8},{10,9... | collective-permute-start | bytes 6152 | tf_op jit(solution)/shard_map/ppermute | solution.py:168
  44.8 28.5 %collective-permute-start.6 = (bf16[128,1024]{1,0:T(8,128)(2,1)}, bf16[128,1024]{1,0:T(8,128)(2,1)S(1)}, u32[]{:S(2)}, u32[]{:S(2)}) collective-permute-start(bf16[128,1024]{1,0:T(8,128)(2,1)} %get-tuple-element.29), channel_id=1, source_target_pairs={{0,3},{1,0},{2,1},{3,2},{4,7},{5,4},{6,5},{7,6},{8,11},{9,8},{10,9... | collective-permute-start | bytes 786440 | tf_op jit(solution)/shard_map/ppermute | solution.py:168
  46.8 26.5 %collective-permute-start.7 = (bf16[128,1024]{1,0:T(8,128)(2,1)}, bf16[128,1024]{1,0:T(8,128)(2,1)S(1)}, u32[]{:S(2)}, u32[]{:S(2)}) collective-permute-start(bf16[128,1024]{1,0:T(8,128)(2,1)} %get-tuple-element.30), channel_id=1, source_target_pairs={{0,2},{1,3},{2,0},{3,1},{4,6},{5,7},{6,4},{7,5},{8,10},{9,11},{10,... | collective-permute-start | bytes 786440 | tf_op jit(solution)/shard_map/ppermute | solution.py:168
  46.8 0.6 copy-start.6
  46.8 0.6 copy-start.7
  46.9 0.6 copy-start.8
  49.9 10.4 %collective-permute-start.9 = (bf16[4,128]{1,0:T(4,128)(2,1)}, bf16[4,128]{1,0:T(4,128)(2,1)S(1)}, u32[]{:S(2)}, u32[]{:S(2)}) collective-permute-start(bf16[4,128]{1,0:T(4,128)(2,1)} %get-tuple-element.34), channel_id=1, source_target_pairs={{0,1},{1,2},{2,3},{3,0},{4,5},{5,6},{6,7},{7,4},{8,9},{9,10},{10,1... | collective-permute-start | bytes 3080 | tf_op jit(solution)/shard_map/ppermute | solution.py:168
  50.9 13.6 %collective-permute-start.10 = (bf16[4,128]{1,0:T(4,128)(2,1)}, bf16[4,128]{1,0:T(4,128)(2,1)S(1)}, u32[]{:S(2)}, u32[]{:S(2)}) collective-permute-start(bf16[4,128]{1,0:T(4,128)(2,1)} %get-tuple-element.35), channel_id=1, source_target_pairs={{0,2},{1,3},{2,0},{3,1},{4,6},{5,7},{6,4},{7,5},{8,10},{9,11},{10,... | collective-permute-start | bytes 3080 | tf_op jit(solution)/shard_map/ppermute | solution.py:168
  52.8 11.6 %collective-permute-start.11 = (bf16[4,128]{1,0:T(4,128)(2,1)}, bf16[4,128]{1,0:T(4,128)(2,1)S(1)}, u32[]{:S(2)}, u32[]{:S(2)}) collective-permute-start(bf16[4,128]{1,0:T(4,128)(2,1)} %get-tuple-element.36), channel_id=1, source_target_pairs={{0,3},{1,0},{2,1},{3,2},{4,7},{5,4},{6,5},{7,6},{8,11},{9,8},{10,9... | collective-permute-start | bytes 3080 | tf_op jit(solution)/shard_map/ppermute | solution.py:168
  56.9 15.1 %all-to-all-start = ((bf16[8,16,1024]{2,1,0:T(8,128)(2,1)}), bf16[8,16,1024]{2,1,0:T(8,128)(2,1)S(1)}, u32[]{:S(2)}, u32[]{:S(2)}) async-start(bf16[8,16,1024]{2,1,0:T(8,128)(2,1)} %bitcast.19), calls=%async_computation | async-start | bytes 524288 | tf_op jit(solution)/shard_map/all_to_all | solution.py:205
  60.3 4.1 %copy-start.9 = (bf16[4,128]{1,0:T(4,128)(2,1)}, bf16[4,128]{1,0:T(4,128)(2,1)S(1)}, u32[]{:S(2)}) copy-start(bf16[4,128]{1,0:T(4,128)(2,1)S(1)} %collective-permute-done.9.refs_5_) | copy-start | bytes 3076
  60.3 13.0 %collective-permute-start.8 = (bf16[128,1024]{1,0:T(8,128)(2,1)}, bf16[128,1024]{1,0:T(8,128)(2,1)}, u32[]{:S(2)}, u32[]{:S(2)}) collective-permute-start(bf16[128,1024]{1,0:T(8,128)(2,1)} %get-tuple-element.31), channel_id=1, source_target_pairs={{0,1},{1,2},{2,3},{3,0},{4,5},{5,6},{6,7},{7,4},{8,9},{9,10},{10,1... | collective-permute-start | bytes 786440 | tf_op jit(solution)/shard_map/ppermute | solution.py:168
  64.4 0.6 copy-start.10
  64.4 0.6 copy-start.11
  72.0 1.3 %copy-start.5 = (f32[128,1024]{1,0:T(8,128)S(1)}, f32[128,1024]{1,0:T(8,128)}, u32[]{:S(2)}) copy-start(f32[128,1024]{1,0:T(8,128)} %get-tuple-element.27) | copy-start | bytes 1572868

commit v2 on v0

v2 whole, which is shorter than its diff:
```python
import functools
import math

import jax
import jax.numpy as jnp
from jax import lax
from jax.experimental import pallas as pl
from jax.experimental.pallas import tpu as pltpu
from jax.sharding import PartitionSpec as P

F32 = jnp.float32
BF16 = jnp.bfloat16
LOW_BITS = 4
SUB = 8
VMEM_LIMIT = 8 << 20


def nn(a, b):
    return lax.dot_general(a, b, (((1,), (0,)), ((), ())), preferred_element_type=F32)


def nt(a, b):
    return lax.dot_general(a, b, (((1,), (1,)), ((), ())), preferred_element_type=F32)


def tn(a, b):
    return lax.dot_general(a, b, (((0,), (0,)), ((), ())), preferred_element_type=F32)


def pack_kernel(owners, pool_count, ids_ref, query_ref, packed_ref, sem):
    rows, depth = query_ref.shape
    hard_count = ids_ref.shape[0]
    per = hard_count // owners
    copy = pltpu.make_async_copy(query_ref, packed_ref.at[:rows, :], sem)
    copy.start()
    packed_ref[rows:, :] = jnp.zeros((SUB, depth), BF16)
    for block in range(hard_count // SUB):
        lines = []
        for place in range(block * SUB, (block + 1) * SUB):
            owner, j = divmod(place, per)
            k = j * owners + owner
            lines.append(ids_ref[k : k + 1, :] - owner * pool_count)
        ids = jnp.concatenate(lines, axis=0)
        high = jnp.right_shift(ids, LOW_BITS)
        low = ids - jnp.left_shift(high, LOW_BITS)
        start = 2 * block * rows
        packed_ref[rows:, start : start + rows] = high.astype(F32).astype(BF16)
        packed_ref[rows:, start + rows : start + 2 * rows] = low.astype(F32).astype(BF16)
    copy.wait()


def local_ids(packed_ref, me, rows, owners, per):
    found = None
    for owner in range(owners):
        parts = []
        for j in range(per):
            block, sub = divmod(owner * per + j, SUB)
            start = 2 * block * rows
            high = packed_ref[rows:, start : start + rows].astype(F32)
            low = packed_ref[rows:, start + rows : start + 2 * rows].astype(F32)
            ids = high * float(1 << LOW_BITS) + low
            parts.append(ids[sub : sub + 1, :])
        if found is None:
            found = parts
        else:
            found = [jnp.where(me == owner, new, old) for new, old in zip(parts, found)]
    return found


def score_block(me, packed_ref, table_ref, rows, owners, per, scale):
    count = table_ref.shape[0]
    ids = local_ids(packed_ref, me, rows, owners, per)
    dense = nt(table_ref[...], packed_ref[:rows, :])
    row_iota = lax.broadcasted_iota(jnp.int32, (count, rows), 0).astype(F32)
    hits = [row_iota == one for one in ids]
    scores = [jnp.sum(jnp.where(hit, dense, 0.0), axis=0, keepdims=True) * scale for hit in hits]
    top = functools.reduce(jnp.maximum, scores)
    powers = [jnp.exp(one - top) for one in scores]
    weight = jnp.zeros((count, rows), F32)
    for hit, one in zip(hits, powers):
        weight = weight + jnp.where(hit, one, 0.0)
    return weight, top, functools.reduce(jnp.add, powers)


def own_kernel(owners, per, scale, packed_ref, hidden_ref, projection_ref, *outs):
    table_ref, turned_ref, stat_ref, weight_ref, term_ref = outs
    me = lax.axis_index("pb")
    rows = packed_ref.shape[0] - SUB
    table_ref[...] = nn(hidden_ref[...], projection_ref[...]).astype(BF16)
    turned_ref[...] = nt(packed_ref[:rows, :], projection_ref[...]).astype(BF16)
    weight, top, total = score_block(me, packed_ref, table_ref, rows, owners, per, scale)
    stat_ref[0:1, :] = top
    stat_ref[1:2, :] = total
    weight_ref[...] = weight
    term_ref[...] = tn(weight.astype(BF16), table_ref[...]).astype(BF16)


def far_kernel(owners, per, scale, table_ref, own_stat_ref, group_stat_ref, *refs):
    far = owners - 1
    me = lax.axis_index("pb")
    packed_refs, stat_ref = refs[:far], refs[far]
    weight_refs, term_refs = refs[owners : owners + far], refs[owners + far :]
    rows = packed_refs[0].shape[0] - SUB
    stat_ref[0:2, :] = own_stat_ref[...]
    stat_ref[2 * owners :, :] = group_stat_ref[...]
    for slot in range(1, owners):
        packed_ref = packed_refs[slot - 1]
        weight, top, total = score_block(me, packed_ref, table_ref, rows, owners, per, scale)
        stat_ref[2 * slot : 2 * slot + 1, :] = top
        stat_ref[2 * slot + 1 : 2 * slot + 2, :] = total
        weight_refs[slot - 1][...] = weight
        term_refs[slot - 1][...] = tn(weight.astype(BF16), table_ref[...]).astype(BF16)


def turn_kernel(count, projection_ref, *refs):
    for packed_ref, out_ref in zip(refs[:count], refs[-count:]):
        rows = out_ref.shape[0]
        out_ref[...] = nt(packed_ref[:rows, :], projection_ref[...]).astype(BF16)


def group_kernel(scale, query_ref, hidden_ref, projection_ref, group_ref, lists_ref, *outs):
    column_ref, power_ref, place_ref, stat_ref = outs
    rows = query_ref.shape[0]
    groups, size = lists_ref.shape
    count = column_ref.shape[0]
    column_ref[...] = nn(hidden_ref[...], projection_ref[...]).astype(BF16)
    dense = nt(column_ref[...], query_ref[...]) * scale
    column_iota = lax.broadcasted_iota(jnp.int32, (groups, count), 1)
    places = jnp.zeros((groups, count), F32)
    lists = lists_ref[...]
    for c in range(size):
        places = places + jnp.where(lists[:, c : c + 1] == column_iota, float(c + 1), 0.0)
    group_iota = lax.broadcasted_iota(jnp.int32, (groups, rows), 0)
    mine = (group_iota == group_ref[...]).astype(F32).astype(BF16)
    place = tn(places.astype(BF16), mine)
    member = place > 0.5
    top = jnp.max(jnp.where(member, dense, -jnp.inf), axis=0, keepdims=True)
    power = jnp.where(member, jnp.exp(jnp.where(member, dense - top, 0.0)), 0.0)
    power_ref[...] = power
    place_ref[...] = place
    stat_ref[0:1, :] = top
    stat_ref[1:2, :] = jnp.sum(power, axis=0, keepdims=True)


def totals(stat_refs, owners, source):
    group_ref = stat_refs[source]
    tops = [group_ref[2 * owners : 2 * owners + 1, :]]
    sums = [group_ref[2 * owners + 1 : 2 * owners + 2, :]]
    for step, ref in enumerate(stat_refs):
        slot = (source - step) % owners
        tops.append(ref[2 * slot : 2 * slot + 1, :])
        sums.append(ref[2 * slot + 1 : 2 * slot + 2, :])
    top = functools.reduce(jnp.maximum, tops)
    total = functools.reduce(jnp.add, [s * jnp.exp(t - top) for s, t in zip(sums, tops)])
    return top, total


def soft_kernel(owners, scale, *refs):
    power_ref, place_ref, label_ref, query_ref, column_ref, own_term_ref = refs[:6]
    stat_refs = refs[6 : 6 + owners]
    keep_ref, give_ref, sum_ref, factor_ref = refs[6 + owners :]
    rows = query_ref.shape[0]
    top, total = totals(stat_refs, owners, 0)
    place = place_ref[...]
    target = (place == (label_ref[...] + 1).astype(F32)).astype(F32)
    group_top = stat_refs[0][2 * owners : 2 * owners + 1, :]
    likely = power_ref[...] * jnp.exp(group_top - top) / total
    grad = jnp.where(place > 0.5, likely - target, 0.0)
    kept, _, size, _ = halves = (keep_ref.shape[0], 2, keep_ref.shape[1], rows)
    even, odd = grad.reshape(halves)[:, 0], grad.reshape(halves)[:, 1]
    first = lax.rem(lax.axis_index("pa"), 2) == 0
    mine = jnp.where(first, even, odd).reshape(kept * size, rows).astype(BF16)
    other = jnp.where(first, odd, even).reshape(kept * size, rows).astype(BF16)
    give_ref[...] = (nn(other, query_ref[...]) * scale).astype(BF16)
    keep_ref[...] = (nn(mine, query_ref[...]) * scale).reshape(keep_ref.shape)
    factor = []
    for slot in range(owners):
        ref = stat_refs[(owners - slot) % owners]
        factor.append(jnp.exp(ref[2 * slot : 2 * slot + 1, :] - top) / total)
    factor = jnp.concatenate(factor + [jnp.zeros((rows - owners, rows), F32)], axis=0).T
    factor_ref[...] = factor
    own = factor[:, :1] * own_term_ref[...].astype(F32)
    sum_ref[...] = tn(grad.astype(BF16), column_ref[...]) + own


def merge_kernel(keep_ref, got_ref, own_ref, *outs):
    pairs = keep_ref.shape[0]
    pair = lax.div(lax.axis_index("pa"), 2)
    own_ref[...] = keep_ref[pair] + got_ref[pair].astype(F32)
    for step in range(1, pairs):
        to = lax.rem(pair + step, pairs)
        outs[step - 1][...] = (keep_ref[to] + got_ref[to].astype(F32)).astype(BF16)


def pool_kernel(owners, scale, *refs):
    stat_refs = refs[:owners]
    weight_refs = refs[owners : 2 * owners]
    turned_refs = refs[2 * owners : 3 * owners]
    out_ref = refs[3 * owners]
    acc = None
    for source in range(owners):
        top, total = totals(stat_refs, owners, source)
        factor = jnp.exp(stat_refs[0][2 * source : 2 * source + 1, :] - top) / total
        part = nn((weight_refs[source][...] * factor).astype(BF16), turned_refs[source][...])
        acc = part if acc is None else acc + part
    out_ref[...] = (acc * scale).astype(BF16)


def batch_kernel(projection_ref, own_ref, *refs):
    total = own_ref[...]
    for ref in refs[:-1]:
        total = total + ref[...].astype(F32)
    refs[-1][...] = nt(total.astype(BF16), projection_ref[...]).astype(BF16)


def query_kernel(owners, scale, sum_ref, factor_ref, *refs):
    out_ref = refs[-1]
    total = sum_ref[...]
    for slot in range(1, owners):
        total = total + factor_ref[:, slot : slot + 1] * refs[slot - 1][...].astype(F32)
    out_ref[...] = (total * scale).astype(BF16)


def call(kernel, outs, arrays, after=(), flops=0, in_place=(), scratch=()):
    outs = [jax.ShapeDtypeStruct(*one) for one in outs]
    arrays = list(arrays) + list(in_place)
    moved = sum(a.size * a.dtype.itemsize for a in arrays + outs)
    count, waits = len(arrays), len(after)
    vmem = pl.BlockSpec(memory_space=pltpu.VMEM)

    def body(*refs):
        kernel(*refs[:count], *refs[count + waits :])

    results = pl.pallas_call(
        body,
        out_shape=outs,
        in_specs=[vmem] * (len(arrays) - len(in_place))
        + [pl.BlockSpec(memory_space=pltpu.HBM)] * len(in_place)
        + [pl.BlockSpec(memory_space=pl.ANY)] * waits,
        out_specs=[vmem] * len(outs),
        scratch_shapes=list(scratch),
        compiler_params=pltpu.CompilerParams(vmem_limit_bytes=VMEM_LIMIT),
        cost_estimate=pl.CostEstimate(flops=flops, bytes_accessed=moved, transcendentals=0),
    )(*arrays, *after)
    return list(results)


def shards(
    queries, batch_hidden, pool_hidden, projection, hard_ids, query_group, labels, group_lists
):
    rows, depth = queries.shape
    scale = 1.0 / math.sqrt(depth)
    owners = lax.axis_size("pb")
    pool_count = pool_hidden.shape[0]
    per = hard_ids.shape[1] // owners
    column_count = batch_hidden.shape[0] * lax.axis_size("pa")
    term, weight = ((rows, depth), BF16), ((pool_count, rows), F32)

    def shift(x, k):
        return lax.ppermute(x, "pb", [(i, (i + k) % owners) for i in range(owners)])

    (packed,) = call(
        functools.partial(pack_kernel, owners, pool_count),
        [((rows + SUB, depth), BF16)],
        [hard_ids.T],
        in_place=[queries],
        scratch=[pltpu.SemaphoreType.DMA],
    )
    far = [shift(packed, k) for k in range(1, owners)]
    hidden = lax.all_gather(batch_hidden, "pa", axis=0, tiled=True)
    table, turned, own_stat, own_weight, own_term = call(
        functools.partial(own_kernel, owners, per, scale),
        [((pool_count, depth), BF16), term, ((2, rows), F32), weight, term],
        [packed, pool_hidden, projection],
        flops=2 * depth * (pool_count * depth + rows * depth + 2 * rows * pool_count),
    )
    column, power, place, group_stat = call(
        functools.partial(group_kernel, scale),
        [
            ((column_count, depth), BF16),
            ((column_count, rows), F32),
            ((column_count, rows), F32),
            ((2, rows), F32),
        ],
        [queries, hidden, projection, query_group[None, :], group_lists],
        flops=2 * depth * column_count * (rows + depth),
    )
    outs = call(
        functools.partial(far_kernel, owners, per, scale),
        [((2 * owners + 2, rows), F32)] + [weight] * (owners - 1) + [term] * (owners - 1),
        [table, own_stat, group_stat] + far,
        flops=4 * (owners - 1) * rows * pool_count * depth,
    )
    stat, weights, terms = outs[0], [own_weight] + outs[1:owners], outs[owners:]
    stats = [stat] + [shift(stat, k) for k in range(1, owners)]
    terms = [shift(terms[k - 1], owners - k) for k in range(1, owners)]
    turned = [turned] + call(
        functools.partial(turn_kernel, owners - 1),
        [term] * (owners - 1),
        [projection] + far,
        after=[stat],
        flops=2 * (owners - 1) * rows * depth * depth,
    )
    members, size = lax.axis_size("pa"), batch_hidden.shape[0]
    pairs = members // 2
    keep, give, total, factor = call(
        functools.partial(soft_kernel, owners, scale),
        [
            ((pairs, size, depth), F32),
            ((pairs * size, depth), BF16),
            ((rows, depth), F32),
            ((rows, rows), F32),
        ],
        [power, place, labels[None, :], queries, column, own_term] + stats,
        after=turned[1:2],
        flops=4 * rows * column_count * depth,
    )
    got = lax.ppermute(give, "pa", [(i, i ^ 1) for i in range(members)])
    parts = call(
        merge_kernel,
        [((size, depth), F32)] + [((size, depth), BF16)] * (pairs - 1),
        [keep, got.reshape(pairs, size, depth)],
        flops=column_count * depth,
    )
    for step in range(1, pairs):
        to = [(i, (i + 2 * step) % members) for i in range(members)]
        parts[step] = lax.ppermute(parts[step], "pa", to)
    (pool_hidden_grad,) = call(
        functools.partial(pool_kernel, owners, scale),
        [((pool_count, depth), BF16)],
        stats + weights + turned,
        flops=2 * rows * owners * pool_count * depth,
    )
    (batch_hidden_grad,) = call(
        batch_kernel,
        [(batch_hidden.shape, BF16)],
        [projection] + parts,
        flops=2 * batch_hidden.shape[0] * depth * depth,
    )
    (query_grad,) = call(
        functools.partial(query_kernel, owners, scale),
        [((rows, depth), BF16)],
        [total, factor] + terms,
        flops=4 * rows * depth * owners,
    )
    return (query_grad, batch_hidden_grad, pool_hidden_grad)


def solution(mesh):
    return jax.shard_map(
        shards,
        mesh=mesh,
        in_specs=(
            P(("pa", "pb"), None),
            P(("pa", "pb"), None),
            P(("pa", "pb"), None),
            P(),
            P(("pa", "pb"), None),
            P(("pa", "pb")),
            P(("pa", "pb")),
            P(),
        ),
        out_specs=(P(("pa", "pb"), None), P(("pa", "pb"), None), P(("pa", "pb"), None)),
        check_vma=False,
    )
```

time: 147 us -> 64.2 us (0.44)
  matrix products: 34 us -> 0 us
  local copies, waits for them, and re-layouts: 26.5 us -> 6.48 us
  waiting for transfers between devices: 30.1 us -> 14.8 us
  Pallas kernels: 0 us -> 14.1 us
  between operations: 14.2 us -> 0.77 us
  blocking collectives: 17.2 us -> 9.51 us
  other arithmetic: 7.67 us -> 0 us
  starting transfers between devices: 16 us -> 18.1 us
    dot_general x10 -> x0, matrix products: 34 us -> none  [the longest x1 7.86 us: shards(): lax.dot_general(pool_grad.astype(jnp.bfloat16), projection, dims, preferr...]
    reduce_scatter x1 -> x0, waiting for transfers between devices: 26.5 us -> none  [shards(): lax.psum_scatter(batch_part, 'pa', scatter_dimension=0, tiled=True)]
    ppermute x0 -> x13, starting transfers between devices: none -> 18.1 us  [the longest x9 13.5 us: shift(): return lax.ppermute(x, 'pb', [(i, (i + k) % owners) for i in range(owners)])]
    mul x5 -> x0, local copies, waits for them, and re-layouts: 15.9 us -> none  [the longest x4 15.8 us: shards(): score_scale * sent_back.astype(jnp.float32)[..., None]]
    all_to_all x3 -> x0, starting transfers between devices: 15.9 us -> none  [the longest x1 6.35 us: shards(): lax.all_to_all(requests, 'pb', split_axis=0, concat_axis=0, tiled=True)]
    ppermute x0 -> x13, waiting for transfers between devices: none -> 14.8 us  [the longest x9 11.5 us: shift(): return lax.ppermute(x, 'pb', [(i, (i + k) % owners) for i in range(owners)])]
    pallas_call x0 -> x10, Pallas kernels: none -> 14.1 us  [call(): pl.pallas_call(body, out_shape=outs, in_specs=[vmem] * (len(arrays) - len...]
    all_to_all x1 -> x0, blocking collectives: 7.94 us -> none  [shards(): lax.all_to_all(grad_hard, 'pb', split_axis=0, concat_axis=0, tiled=True)]
  transfers between devices with their start and end apart: 5 -> 13, of which waited for: 2 -> 5; matrix products, arithmetic and copies ran while one was open for 34% -> 0% of each run, Pallas kernels for 0% -> 15%
where the time goes in v2:
time: 64.2 us; the launch traced here: 63.8 us
  starting transfers between devices  18.1 us (28%)
  waiting for transfers between devices  14.8 us (23%)
  Pallas kernels  14.1 us (22%)
  blocking collectives  9.51 us (15%)
  local copies, waits for them, and re-layouts  6.48 us (10%)
  between operations  0.77 us (1%)
    pallas_call x10, Pallas kernels, call(): pl.pallas_call(body, out_shape=outs, in_specs=[vmem] * (len(arrays) - len...  14.1 us
    ppermute x9, starting transfers between devices, shift(): return lax.ppermute(x, 'pb', [(i, (i + k) % owners) for i in range(owners)])  13.5 us
    ppermute x9, waiting for transfers between devices, shift(): return lax.ppermute(x, 'pb', [(i, (i + k) % owners) for i in range(owners)])  11.5 us
    all_gather x1, blocking collectives, shards(): hidden = lax.all_gather(batch_hidden, 'pa', axis=0, tiled=True)  9.51 us
    unnamed x18, local copies, waits for them, and re-layouts  6.48 us
    ppermute x3, starting transfers between devices, shards(): parts[step] = lax.ppermute(parts[step], 'pa', to)  4.6 us
    ppermute x3, waiting for transfers between devices, shards(): parts[step] = lax.ppermute(parts[step], 'pa', to)  1.95 us
    ppermute x1, waiting for transfers between devices, shards(): got = lax.ppermute(give, 'pa', [(i, i ^ 1) for i in range(members)])  1.33 us
  transfers between devices with their start and end apart: 13, of which 5 were waited for; matrix products, arithmetic and copies ran while one was open for 0% of the time, Pallas kernels for 15%

profile of v2, /device:TPU:0, one launch (start us, length us, event | category | flops | bytes accessed | tf_op | source)
XLA Modules:
  0.0 63.8 jit_solution(1640016731245453716)
XLA Ops:
  0.6 0.9 %copy-done.2 = bf16[128,1024]{1,0:T(8,128)(2,1)S(1)} copy-done((bf16[128,1024]{1,0:T(8,128)(2,1)S(1)}, bf16[128,1024]{1,0:T(8,128)(2,1)}, u32[]{:S(2)}) %copy-start.2) | copy-done | bytes 262168
  1.6 0.7 %copy-done.5 = s32[128,16]{0,1:T(8,128)S(1)} copy-done((s32[128,16]{0,1:T(8,128)S(1)}, s32[128,16]{0,1:T(8,128)}, u32[]{:S(2)}) %copy-start.5) | copy-done | bytes 8216
  2.3 5.1 %collective-permute-start.2 = (bf16[136,1024]{1,0:T(8,128)(2,1)S(1)}, bf16[136,1024]{1,0:T(8,128)(2,1)S(1)}, u32[]{:S(2)}, u32[]{:S(2)}) collective-permute-start(bf16[136,1024]{1,0:T(8,128)(2,1)S(1)} %shard_map.104.refs_0_), channel_id=1, source_target_pairs={{0,3},{1,0},{2,1},{3,2},{4,7},{5,4},{6,5},{7,6},{8,11},{9,8},{10,9... | collective-permute-start | bytes 835592 | tf_op jit(solution)/shard_map/ppermute | solution.py:260
  7.5 1.0 %collective-permute-start = (bf16[136,1024]{1,0:T(8,128)(2,1)S(1)}, bf16[136,1024]{1,0:T(8,128)(2,1)S(1)}, u32[]{:S(2)}, u32[]{:S(2)}) collective-permute-start(bf16[136,1024]{1,0:T(8,128)(2,1)S(1)} %shard_map.104.refs_0_), channel_id=1, source_target_pairs={{0,1},{1,2},{2,3},{3,0},{4,5},{5,6},{6,7},{7,4},{8,9},{9,10},{10,1... | collective-permute-start | bytes 835592 | tf_op jit(solution)/shard_map/ppermute | solution.py:260
  8.5 9.5 %all_gather.3.refs_1_ = bf16[128,1024]{1,0:T(8,128)(2,1)S(1)} all-gather(bf16[16,1024]{1,0:T(8,128)(2,1)} %param.9), channel_id=1, replica_groups=mesh['pa'=8,'pb'=4] {'pa'}, dimensions={0}, use_global_device_ids=true | all-gather | bytes 294912 | tf_op jit(solution)/shard_map/all_gather | solution.py:270
  18.0 1.6 %copy-done = bf16[1024,1024]{1,0:T(8,128)(2,1)S(1)} copy-done((bf16[1024,1024]{1,0:T(8,128)(2,1)S(1)}, bf16[1024,1024]{1,0:T(8,128)(2,1)}, u32[]{:S(2)}) %copy-start) | copy-done | bytes 2097176
  19.6 0.8 %copy-done.4 = s32[64,64]{1,0:T(8,128)S(1)} copy-done((s32[64,64]{1,0:T(8,128)S(1)}, s32[64,64]{1,0:T(8,128)}, u32[]{:S(2)}) %copy-start.4) | copy-done | bytes 16408
  20.3 0.7 %copy-done.6 = s32[128]{0:T(128)S(1)} copy-done((s32[128]{0:T(128)S(1)}, s32[128]{0:T(128)}, u32[]{:S(2)}) %copy-start.6) | copy-done | bytes 536
  21.0 1.0 %shard_map.103 = (bf16[128,1024]{1,0:T(8,128)(2,1)S(1)}, f32[128,128]{1,0:T(8,128)S(1)}, f32[128,128]{1,0:T(8,128)S(1)}, f32[2,128]{1,0:T(2,128)S(1)}) custom-call(bf16[128,1024]{1,0:T(8,128)(2,1)S(1)} %copy-done.2, bf16[128,1024]{1,0:T(8,128)(2,1)S(1)} %all_gather.3.refs_1_, bf16[1024,1024]{1,0:T(8,128)(2,1)S(1)} %copy-done, s32[1,128]{1,0:T(1,128)S(1)} %bitcast.6, ...), custom_call_target="tpu_custom_call" | custom-call | flops 301989888 | bytes 3032576 | tf_op jit(solution)/shard_map/pallas_call | solution.py:234
  22.0 0.6 copy-done.1
  22.6 1.2 %copy-done.8 = bf16[512,1024]{1,0:T(8,128)(2,1)S(1)} copy-done((bf16[512,1024]{1,0:T(8,128)(2,1)S(1)}, bf16[512,1024]{1,0:T(8,128)(2,1)}, u32[]{:S(2)}) %copy-start.8) | copy-done | bytes 1048600
  23.8 2.8 %shard_map.105 = (bf16[512,1024]{1,0:T(8,128)(2,1)S(1)}, bf16[128,1024]{1,0:T(8,128)(2,1)S(1)}, f32[2,128]{1,0:T(2,128)S(1)}, f32[512,128]{1,0:T(8,128)S(1)}, bf16[128,1024]{1,0:T(8,128)(2,1)S(1)}) custom-call(bf16[136,1024]{1,0:T(8,128)(2,1)S(1)} %shard_map.104.refs_0_, bf16[512,1024]{1,0:T(8,128)(2,1)S(1)} %copy-done.8, bf16[1024,1024]{1,0:T(8,128)(2,1)S(1)} %copy-done.1), custom_call_target="tpu_custom_call" | custom-call | flops 1610612736 | bytes 5260288 | tf_op jit(solution)/shard_map/pallas_call | solution.py:234
  26.6 4.5 %collective-permute-done.1.refs_4_.refs_2_ = bf16[136,1024]{1,0:T(8,128)(2,1)S(1)} collective-permute-done((bf16[136,1024]{1,0:T(8,128)(2,1)S(1)}, bf16[136,1024]{1,0:T(8,128)(2,1)S(1)}, u32[]{:S(2)}, u32[]{:S(2)}) %collective-permute-start.1) | collective-permute-done | bytes 278560 | tf_op jit(solution)/shard_map/ppermute | solution.py:260
  31.2 3.2 %shard_map.106 = (f32[10,128]{1,0:T(8,128)S(1)}, f32[512,128]{1,0:T(8,128)S(1)}, f32[512,128]{1,0:T(8,128)S(1)}, f32[512,128]{1,0:T(8,128)S(1)}, bf16[128,1024]{...) custom-call(bf16[512,1024]{1,0:T(8,128)(2,1)S(1)} %get-tuple-element.34.refs_0_, ...), custom_call_target="tpu_custom_call" | custom-call | flops 805306368 | bytes 3464192 | tf_op jit(solution)/shard_map/pallas_call | solution.py:234
  34.4 0.1 collective-permute-start.5
  34.5 2.9 %collective-permute-start.4 = (f32[10,128]{1,0:T(8,128)S(1)}, f32[10,128]{1,0:T(8,128)S(1)}, u32[]{:S(2)}, u32[]{:S(2)}) collective-permute-start(f32[10,128]{1,0:T(8,128)S(1)} %get-tuple-element.37.refs_4_.refs_6_.refs_0_), channel_id=1, source_target_pairs={{0,2},{1,3},{2,0},{3,1},{4,6},{5,7},{6,4},{7,5},{8,10},{9,11},{10,... | collective-permute-start | bytes 15368 | tf_op jit(solution)/shard_map/ppermute | solution.py:260
  37.4 1.9 %collective-permute-start.3 = (f32[10,128]{1,0:T(8,128)S(1)}, f32[10,128]{1,0:T(8,128)S(1)}, u32[]{:S(2)}, u32[]{:S(2)}) collective-permute-start(f32[10,128]{1,0:T(8,128)S(1)} %get-tuple-element.37.refs_4_.refs_6_.refs_0_), channel_id=1, source_target_pairs={{0,1},{1,2},{2,3},{3,0},{4,5},{5,6},{6,7},{7,4},{8,9},{9,10},{10,1... | collective-permute-start | bytes 15368 | tf_op jit(solution)/shard_map/ppermute | solution.py:260
  39.3 1.9 %collective-permute-start.6 = (bf16[128,1024]{1,0:T(8,128)(2,1)S(1)}, bf16[128,1024]{1,0:T(8,128)(2,1)S(1)}, u32[]{:S(2)}, u32[]{:S(2)}) collective-permute-start(bf16[128,1024]{1,0:T(8,128)(2,1)S(1)} %get-tuple-element.41), channel_id=1, source_target_pairs={{0,3},{1,0},{2,1},{3,2},{4,7},{5,4},{6,5},{7,6},{8,11},{9,8},{10,9... | collective-permute-start | bytes 786440 | tf_op jit(solution)/shard_map/ppermute | solution.py:260
  41.2 0.6 collective-permute-start.8
  41.8 2.2 %shard_map.107 = (bf16[128,1024]{1,0:T(8,128)(2,1)S(1)}, bf16[128,1024]{1,0:T(8,128)(2,1)S(1)}, bf16[128,1024]{1,0:T(8,128)(2,1)S(1)}) custom-call(bf16[1024,1024]{1,0:T(8,128)(2,1)S(1)} %copy-done.1, bf16[136,1024]{1,0:T(8,128)(2,1)S(1)} %collective-permute-done.refs_3_.refs_1_, bf16[136,1024]{1,0:T(8,128)(2,1)S(1)} %collective-permute-done.1.refs_4_.refs_2_, ...), custom_call_target="tpu_custom_call" | custom-call | flops 805306368 | bytes 3719168 | tf_op jit(solution)/shard_map/pallas_call | solution.py:234
  44.0 0.4 shard_map.108
  44.4 0.1 collective-permute-start.9
  44.4 1.3 %collective-permute-done.9 = bf16[64,1024]{1,0:T(8,128)(2,1)S(1)} collective-permute-done((bf16[64,1024]{1,0:T(8,128)(2,1)S(1)}, bf16[64,1024]{1,0:T(8,128)(2,1)S(1)}, u32[]{:S(2)}, u32[]{:S(2)}) %collective-permute-start.9) | collective-permute-done | bytes 131104 | tf_op jit(solution)/shard_map/ppermute | solution.py:318
  45.8 1.5 %collective-permute-start.10 = (bf16[16,1024]{1,0:T(8,128)(2,1)S(1)}, bf16[16,1024]{1,0:T(8,128)(2,1)S(1)}, u32[]{:S(2)}, u32[]{:S(2)}) collective-permute-start(bf16[16,1024]{1,0:T(8,128)(2,1)S(1)} %get-tuple-element.47), channel_id=1, source_target_pairs={{0,8},{4,12},{8,16},{12,20},{16,24},{20,28},{24,0},{28,4},{1,9},{5... | collective-permute-start | bytes 98312 | tf_op jit(solution)/shard_map/ppermute | solution.py:327
  47.3 1.5 %collective-permute-start.11 = (bf16[16,1024]{1,0:T(8,128)(2,1)S(1)}, bf16[16,1024]{1,0:T(8,128)(2,1)S(1)}, u32[]{:S(2)}, u32[]{:S(2)}) collective-permute-start(bf16[16,1024]{1,0:T(8,128)(2,1)S(1)} %get-tuple-element.48), channel_id=1, source_target_pairs={{0,16},{4,20},{8,24},{12,28},{16,0},{20,4},{24,8},{28,12},{1,17},{... | collective-permute-start | bytes 98312 | tf_op jit(solution)/shard_map/ppermute | solution.py:327
  48.9 1.8 %collective-permute-done.10.refs_2_ = bf16[16,1024]{1,0:T(8,128)(2,1)S(1)} collective-permute-done((bf16[16,1024]{1,0:T(8,128)(2,1)S(1)}, bf16[16,1024]{1,0:T(8,128)(2,1)S(1)}, u32[]{:S(2)}, u32[]{:S(2)}) %collective-permute-start.10) | collective-permute-done | bytes 32800 | tf_op jit(solution)/shard_map/ppermute | solution.py:327
  50.7 1.5 %collective-permute-start.12 = (bf16[16,1024]{1,0:T(8,128)(2,1)S(1)}, bf16[16,1024]{1,0:T(8,128)(2,1)S(1)}, u32[]{:S(2)}, u32[]{:S(2)}) collective-permute-start(bf16[16,1024]{1,0:T(8,128)(2,1)S(1)} %get-tuple-element.49), channel_id=1, source_target_pairs={{0,24},{4,28},{8,0},{12,4},{16,8},{20,12},{24,16},{28,20},{1,25},{... | collective-permute-start | bytes 98312 | tf_op jit(solution)/shard_map/ppermute | solution.py:327
  52.2 2.2 %shard_map.112 = bf16[512,1024]{1,0:T(8,128)(2,1)} custom-call(f32[10,128]{1,0:T(8,128)S(1)} %get-tuple-element.37.refs_4_.refs_6_.refs_0_, f32[10,128]{1,0:T(8,128)S(1)} %collective-permute-done.3.refs_7_.refs_1_, f32[10,128]{1,0:T(8,128)S(1)} %collective-permute-done.4.refs_8_.refs_2_, f32[10,128]{1,0:T(8,128)S(1)} %collective-permute-done.5.refs_9_.refs_3_, ...), custom_call_target="tpu_custom_call" | custom-call | flops 536870912 | bytes 3166208 | tf_op jit(solution)/shard_map/pallas_call | solution.py:234
  54.4 0.1 collective-permute-done.12.refs_4_
  54.6 1.3 %shard_map.111 = bf16[16,1024]{1,0:T(8,128)(2,1)} custom-call(bf16[1024,1024]{1,0:T(8,128)(2,1)S(1)} %copy-done.1, f32[16,1024]{1,0:T(8,128)S(1)} %get-tuple-element.46.refs_1_, bf16[16,1024]{1,0:T(8,128)(2,1)S(1)} %collective-permute-done.10.refs_2_, bf16[16,1024]{1,0:T(8,128)(2,1)S(1)} %collective-permute-done.11.refs_3_, ...), custom_call_target="tpu_custom_call" | custom-call | flops 33554432 | bytes 2293760 | tf_op jit(solution)/shard_map/pallas_call | solution.py:234
  55.9 6.9 %collective-permute-done.7.refs_3_ = bf16[128,1024]{1,0:T(8,128)(2,1)S(1)} collective-permute-done((bf16[128,1024]{1,0:T(8,128)(2,1)S(1)}, bf16[128,1024]{1,0:T(8,128)(2,1)S(1)}, u32[]{:S(2)}, u32[]{:S(2)}) %collective-permute-start.7) | collective-permute-done | bytes 262176 | tf_op jit(solution)/shard_map/ppermute | solution.py:260
  62.8 1.0 %shard_map.109 = bf16[128,1024]{1,0:T(8,128)(2,1)} custom-call(f32[128,1024]{1,0:T(8,128)S(1)} %get-tuple-element.39.refs_0_, f32[128,128]{1,0:T(8,128)S(1)} %get-tuple-element.40.refs_1_, bf16[128,1024]{1,0:T(8,128)(2,1)S(1)} %collective-permute-done.6.refs_2_, bf16[128,1024]{1,0:T(8,128)(2,1)S(1)} %collective-permute-done.7.refs_3_, ...), custom_call_target="tpu_custom_call" | custom-call | flops 2097152 | bytes 1638400 | tf_op jit(solution)/shard_map/pallas_call | solution.py:234
  (23 shorter events, 0.1 us)
Async XLA Ops:
  0.6 1.0 %copy-start.2 = (bf16[128,1024]{1,0:T(8,128)(2,1)S(1)}, bf16[128,1024]{1,0:T(8,128)(2,1)}, u32[]{:S(2)}) copy-start(bf16[128,1024]{1,0:T(8,128)(2,1)} %refs_3_.1) | copy-start | bytes 786436
  1.6 0.7 %copy-start.5 = (s32[128,16]{0,1:T(8,128)S(1)}, s32[128,16]{0,1:T(8,128)}, u32[]{:S(2)}) copy-start(s32[128,16]{0,1:T(8,128)} %param.12) | copy-start | bytes 24580
  2.3 24.3 %collective-permute-start.2 = (bf16[136,1024]{1,0:T(8,128)(2,1)S(1)}, bf16[136,1024]{1,0:T(8,128)(2,1)S(1)}, u32[]{:S(2)}, u32[]{:S(2)}) collective-permute-start(bf16[136,1024]{1,0:T(8,128)(2,1)S(1)} %shard_map.104.refs_0_), channel_id=1, source_target_pairs={{0,3},{1,0},{2,1},{3,2},{4,7},{5,4},{6,5},{7,6},{8,11},{9,8},{10,9... | collective-permute-start | bytes 835592 | tf_op jit(solution)/shard_map/ppermute | solution.py:260
  7.5 23.7 %collective-permute-start.1 = (bf16[136,1024]{1,0:T(8,128)(2,1)S(1)}, bf16[136,1024]{1,0:T(8,128)(2,1)S(1)}, u32[]{:S(2)}, u32[]{:S(2)}) collective-permute-start(bf16[136,1024]{1,0:T(8,128)(2,1)S(1)} %shard_map.104.refs_0_), channel_id=1, source_target_pairs={{0,2},{1,3},{2,0},{3,1},{4,6},{5,7},{6,4},{7,5},{8,10},{9,11},{10,... | collective-permute-start | bytes 835592 | tf_op jit(solution)/shard_map/ppermute | solution.py:260
  7.5 23.7 %collective-permute-start = (bf16[136,1024]{1,0:T(8,128)(2,1)S(1)}, bf16[136,1024]{1,0:T(8,128)(2,1)S(1)}, u32[]{:S(2)}, u32[]{:S(2)}) collective-permute-start(bf16[136,1024]{1,0:T(8,128)(2,1)S(1)} %shard_map.104.refs_0_), channel_id=1, source_target_pairs={{0,1},{1,2},{2,3},{3,0},{4,5},{5,6},{6,7},{7,4},{8,9},{9,10},{10,1... | collective-permute-start | bytes 835592 | tf_op jit(solution)/shard_map/ppermute | solution.py:260
  18.0 1.6 %copy-start = (bf16[1024,1024]{1,0:T(8,128)(2,1)S(1)}, bf16[1024,1024]{1,0:T(8,128)(2,1)}, u32[]{:S(2)}) copy-start(bf16[1024,1024]{1,0:T(8,128)(2,1)} %refs_0_.5) | copy-start | bytes 6291460
  19.6 0.8 %copy-start.4 = (s32[64,64]{1,0:T(8,128)S(1)}, s32[64,64]{1,0:T(8,128)}, u32[]{:S(2)}) copy-start(s32[64,64]{1,0:T(8,128)} %refs_4_.1) | copy-start | bytes 49156
  20.3 0.7 %copy-start.6 = (s32[128]{0:T(128)S(1)}, s32[128]{0:T(128)}, u32[]{:S(2)}) copy-start(s32[128]{0:T(128)} %param.13) | copy-start | bytes 1540
  21.0 1.6 %copy-start.1 = (bf16[1024,1024]{1,0:T(8,128)(2,1)S(1)}, bf16[1024,1024]{1,0:T(8,128)(2,1)}, u32[]{:S(2)}) copy-start(bf16[1024,1024]{1,0:T(8,128)(2,1)} %refs_0_.5) | copy-start | bytes 6291460
  22.6 1.2 %copy-start.8 = (bf16[512,1024]{1,0:T(8,128)(2,1)S(1)}, bf16[512,1024]{1,0:T(8,128)(2,1)}, u32[]{:S(2)}) copy-start(bf16[512,1024]{1,0:T(8,128)(2,1)} %refs_1_.3) | copy-start | bytes 3145732
  34.4 9.6 %copy-start.3 = (bf16[128,1024]{1,0:T(8,128)(2,1)S(1)}, bf16[128,1024]{1,0:T(8,128)(2,1)}, u32[]{:S(2)}) copy-start(bf16[128,1024]{1,0:T(8,128)(2,1)} %refs_3_.1) | copy-start | bytes 786436
  34.4 9.6 %copy-start.7 = (s32[128]{0:T(128)S(1)}, s32[128]{0:T(128)}, u32[]{:S(2)}) copy-start(s32[128]{0:T(128)} %param.14) | copy-start | bytes 1540
  34.4 6.8 %collective-permute-start.5 = (f32[10,128]{1,0:T(8,128)S(1)}, f32[10,128]{1,0:T(8,128)S(1)}, u32[]{:S(2)}, u32[]{:S(2)}) collective-permute-start(f32[10,128]{1,0:T(8,128)S(1)} %get-tuple-element.37.refs_4_.refs_6_.refs_0_), channel_id=1, source_target_pairs={{0,3},{1,0},{2,1},{3,2},{4,7},{5,4},{6,5},{7,6},{8,11},{9,8},{10,9... | collective-permute-start | bytes 15368 | tf_op jit(solution)/shard_map/ppermute | solution.py:260
  34.5 9.4 %collective-permute-start.4 = (f32[10,128]{1,0:T(8,128)S(1)}, f32[10,128]{1,0:T(8,128)S(1)}, u32[]{:S(2)}, u32[]{:S(2)}) collective-permute-start(f32[10,128]{1,0:T(8,128)S(1)} %get-tuple-element.37.refs_4_.refs_6_.refs_0_), channel_id=1, source_target_pairs={{0,2},{1,3},{2,0},{3,1},{4,6},{5,7},{6,4},{7,5},{8,10},{9,11},{10,... | collective-permute-start | bytes 15368 | tf_op jit(solution)/shard_map/ppermute | solution.py:260
  37.4 6.6 %collective-permute-start.3 = (f32[10,128]{1,0:T(8,128)S(1)}, f32[10,128]{1,0:T(8,128)S(1)}, u32[]{:S(2)}, u32[]{:S(2)}) collective-permute-start(f32[10,128]{1,0:T(8,128)S(1)} %get-tuple-element.37.refs_4_.refs_6_.refs_0_), channel_id=1, source_target_pairs={{0,1},{1,2},{2,3},{3,0},{4,5},{5,6},{6,7},{7,4},{8,9},{9,10},{10,1... | collective-permute-start | bytes 15368 | tf_op jit(solution)/shard_map/ppermute | solution.py:260
  39.3 16.5 %collective-permute-start.6 = (bf16[128,1024]{1,0:T(8,128)(2,1)S(1)}, bf16[128,1024]{1,0:T(8,128)(2,1)S(1)}, u32[]{:S(2)}, u32[]{:S(2)}) collective-permute-start(bf16[128,1024]{1,0:T(8,128)(2,1)S(1)} %get-tuple-element.41), channel_id=1, source_target_pairs={{0,3},{1,0},{2,1},{3,2},{4,7},{5,4},{6,5},{7,6},{8,11},{9,8},{10,9... | collective-permute-start | bytes 786440 | tf_op jit(solution)/shard_map/ppermute | solution.py:260
  41.2 21.6 %collective-permute-start.7 = (bf16[128,1024]{1,0:T(8,128)(2,1)S(1)}, bf16[128,1024]{1,0:T(8,128)(2,1)S(1)}, u32[]{:S(2)}, u32[]{:S(2)}) collective-permute-start(bf16[128,1024]{1,0:T(8,128)(2,1)S(1)} %get-tuple-element.42), channel_id=1, source_target_pairs={{0,2},{1,3},{2,0},{3,1},{4,6},{5,7},{6,4},{7,5},{8,10},{9,11},{10,... | collective-permute-start | bytes 786440 | tf_op jit(solution)/shard_map/ppermute | solution.py:260
  41.2 21.6 %collective-permute-start.8 = (bf16[128,1024]{1,0:T(8,128)(2,1)S(1)}, bf16[128,1024]{1,0:T(8,128)(2,1)S(1)}, u32[]{:S(2)}, u32[]{:S(2)}) collective-permute-start(bf16[128,1024]{1,0:T(8,128)(2,1)S(1)} %get-tuple-element.43), channel_id=1, source_target_pairs={{0,1},{1,2},{2,3},{3,0},{4,5},{5,6},{6,7},{7,4},{8,9},{9,10},{10,1... | collective-permute-start | bytes 786440 | tf_op jit(solution)/shard_map/ppermute | solution.py:260
  44.4 1.4 %collective-permute-start.9 = (bf16[64,1024]{1,0:T(8,128)(2,1)S(1)}, bf16[64,1024]{1,0:T(8,128)(2,1)S(1)}, u32[]{:S(2)}, u32[]{:S(2)}) collective-permute-start(bf16[64,1024]{1,0:T(8,128)(2,1)S(1)} %get-tuple-element.45), channel_id=1, source_target_pairs={{0,4},{4,0},{8,12},{12,8},{16,20},{20,16},{24,28},{28,24},{1,5},{5... | collective-permute-start | bytes 393224 | tf_op jit(solution)/shard_map/ppermute | solution.py:318
  45.8 4.9 %collective-permute-start.10 = (bf16[16,1024]{1,0:T(8,128)(2,1)S(1)}, bf16[16,1024]{1,0:T(8,128)(2,1)S(1)}, u32[]{:S(2)}, u32[]{:S(2)}) collective-permute-start(bf16[16,1024]{1,0:T(8,128)(2,1)S(1)} %get-tuple-element.47), channel_id=1, source_target_pairs={{0,8},{4,12},{8,16},{12,20},{16,24},{20,28},{24,0},{28,4},{1,9},{5... | collective-permute-start | bytes 98312 | tf_op jit(solution)/shard_map/ppermute | solution.py:327
  47.3 7.1 %collective-permute-start.11 = (bf16[16,1024]{1,0:T(8,128)(2,1)S(1)}, bf16[16,1024]{1,0:T(8,128)(2,1)S(1)}, u32[]{:S(2)}, u32[]{:S(2)}) collective-permute-start(bf16[16,1024]{1,0:T(8,128)(2,1)S(1)} %get-tuple-element.48), channel_id=1, source_target_pairs={{0,16},{4,20},{8,24},{12,28},{16,0},{20,4},{24,8},{28,12},{1,17},{... | collective-permute-start | bytes 98312 | tf_op jit(solution)/shard_map/ppermute | solution.py:327
  50.7 3.9 %collective-permute-start.12 = (bf16[16,1024]{1,0:T(8,128)(2,1)S(1)}, bf16[16,1024]{1,0:T(8,128)(2,1)S(1)}, u32[]{:S(2)}, u32[]{:S(2)}) collective-permute-start(bf16[16,1024]{1,0:T(8,128)(2,1)S(1)} %get-tuple-element.49), channel_id=1, source_target_pairs={{0,24},{4,28},{8,0},{12,4},{16,8},{20,12},{24,16},{28,20},{1,25},{... | collective-permute-start | bytes 98312 | tf_op jit(solution)/shard_map/ppermute | solution.py:327

commit v3 on v2

--- a/solution.py
+++ b/solution.py
@@ -7,6 +7,7 @@
 from jax.experimental import pallas as pl
 from jax.experimental.pallas import tpu as pltpu
 from jax.sharding import PartitionSpec as P
+
 
 F32 = jnp.float32
 BF16 = jnp.bfloat16
@@ -95,21 +96,49 @@
     term_ref[...] = tn(weight.astype(BF16), table_ref[...]).astype(BF16)
 
 
-def far_kernel(owners, per, scale, table_ref, own_stat_ref, group_stat_ref, *refs):
-    far = owners - 1
+def score_kernel(owners, per, scale, table_ref, packed_ref, stat_ref, weight_ref):
+    rows = packed_ref.shape[0] - SUB
     me = lax.axis_index("pb")
-    packed_refs, stat_ref = refs[:far], refs[far]
-    weight_refs, term_refs = refs[owners : owners + far], refs[owners + far :]
-    rows = packed_refs[0].shape[0] - SUB
-    stat_ref[0:2, :] = own_stat_ref[...]
-    stat_ref[2 * owners :, :] = group_stat_ref[...]
-    for slot in range(1, owners):
-        packed_ref = packed_refs[slot - 1]
-        weight, top, total = score_block(me, packed_ref, table_ref, rows, owners, per, scale)
-        stat_ref[2 * slot : 2 * slot + 1, :] = top
-        stat_ref[2 * slot + 1 : 2 * slot + 2, :] = total
-        weight_refs[slot - 1][...] = weight
-        term_refs[slot - 1][...] = tn(weight.astype(BF16), table_ref[...]).astype(BF16)
+    weight, top, total = score_block(me, packed_ref, table_ref, rows, owners, per, scale)
+    stat_ref[0:1, :] = top
+    stat_ref[1:2, :] = total
+    weight_ref[...] = weight
+
+
+def term_kernel(table_ref, stat_ref, weight_ref, *refs):
+    old_ref, out_ref = refs if len(refs) == 2 else (None, refs[0])
+    weight, top = weight_ref[...], stat_ref[0:1, :]
+    rows = weight.shape[1]
+    if old_ref is not None:
+        parts = [old_ref[rows:, k * rows : (k + 1) * rows].astype(F32)[0:1, :] for k in range(3)]
+        before = parts[0] + parts[1] + parts[2]
+        both = jnp.maximum(before, top)
+        weight = weight * jnp.exp(top - both)
+        column = jnp.broadcast_to(jnp.exp(before - both), (rows, rows)).T[:, :1]
+        top = both
+    term = tn(weight.astype(BF16), table_ref[...])
+    if old_ref is not None:
+        term = term + column * old_ref[:rows, :].astype(F32)
+    out_ref[:rows, :] = term.astype(BF16)
+    if out_ref.shape[0] > rows:
+        out_ref[rows:, :] = jnp.zeros((SUB, out_ref.shape[1]), BF16)
+        left = jnp.broadcast_to(top, (SUB, rows))
+        for k in range(3):
+            part = left.astype(BF16)
+            out_ref[rows:, k * rows : (k + 1) * rows] = part
+            left = left - part.astype(F32)
+
+
+def join_kernel(*refs):
+    for k, ref in enumerate(refs[:-1]):
+        refs[-1][2 * k : 2 * k + 2, :] = ref[...]
+
+
+def pair_kernel(mine_ref, other_ref, out_ref):
+    first = lax.rem(lax.axis_index("pa"), 2) == 0
+    mine, other = mine_ref[...], other_ref[...]
+    out_ref[0] = jnp.where(first, mine, other)
+    out_ref[1] = jnp.where(first, other, mine)
 
 
 def turn_kernel(count, projection_ref, *refs):
@@ -118,12 +147,16 @@
         out_ref[...] = nt(packed_ref[:rows, :], projection_ref[...]).astype(BF16)
 
 
-def group_kernel(scale, query_ref, hidden_ref, projection_ref, group_ref, lists_ref, *outs):
-    column_ref, power_ref, place_ref, stat_ref = outs
+def group_kernel(scale, pairs, query_ref, projection_ref, group_ref, lists_ref, *refs):
+    column_ref, power_ref, place_ref, stat_ref, hidden_ref = refs[pairs:]
     rows = query_ref.shape[0]
     groups, size = lists_ref.shape
     count = column_ref.shape[0]
-    column_ref[...] = nn(hidden_ref[...], projection_ref[...]).astype(BF16)
+    pair = lax.div(lax.axis_index("pa"), 2)
+    for step, ref in enumerate(refs[:pairs]):
+        hidden_ref[lax.rem(pair - step + pairs, pairs)] = ref[...]
+    hidden = hidden_ref[...].reshape(count, query_ref.shape[1])
+    column_ref[...] = nn(hidden, projection_ref[...]).astype(BF16)
     dense = nt(column_ref[...], query_ref[...]) * scale
     column_iota = lax.broadcasted_iota(jnp.int32, (groups, count), 1)
     places = jnp.zeros((groups, count), F32)
@@ -155,7 +188,7 @@
     return top, total
 
 
-def soft_kernel(owners, scale, *refs):
+def soft_kernel(owners, direct, scale, *refs):
     power_ref, place_ref, label_ref, query_ref, column_ref, own_term_ref = refs[:6]
     stat_refs = refs[6 : 6 + owners]
     keep_ref, give_ref, sum_ref, factor_ref = refs[6 + owners :]
@@ -173,11 +206,10 @@
     other = jnp.where(first, odd, even).reshape(kept * size, rows).astype(BF16)
     give_ref[...] = (nn(other, query_ref[...]) * scale).astype(BF16)
     keep_ref[...] = (nn(mine, query_ref[...]) * scale).reshape(keep_ref.shape)
-    factor = []
-    for slot in range(owners):
-        ref = stat_refs[(owners - slot) % owners]
-        factor.append(jnp.exp(ref[2 * slot : 2 * slot + 1, :] - top) / total)
-    factor = jnp.concatenate(factor + [jnp.zeros((rows - owners, rows), F32)], axis=0).T
+    tops = [stat_refs[(owners - k) % owners][2 * k : 2 * k + 1, :] for k in range(owners)]
+    tops = tops[: direct + 1] + [functools.reduce(jnp.maximum, tops[direct + 1 :])]
+    factor = [jnp.exp(one - top) / total for one in tops]
+    factor = jnp.concatenate(factor + [jnp.zeros((rows - direct - 2, rows), F32)], axis=0).T
     factor_ref[...] = factor
     own = factor[:, :1] * own_term_ref[...].astype(F32)
     sum_ref[...] = tn(grad.astype(BF16), column_ref[...]) + own
@@ -213,11 +245,11 @@
     refs[-1][...] = nt(total.astype(BF16), projection_ref[...]).astype(BF16)
 
 
-def query_kernel(owners, scale, sum_ref, factor_ref, *refs):
+def query_kernel(scale, sum_ref, factor_ref, *refs):
     out_ref = refs[-1]
     total = sum_ref[...]
-    for slot in range(1, owners):
-        total = total + factor_ref[:, slot : slot + 1] * refs[slot - 1][...].astype(F32)
+    for k, ref in enumerate(refs[:-1]):
+        total = total + factor_ref[:, k + 1 : k + 2] * ref[...].astype(F32)
     out_ref[...] = (total * scale).astype(BF16)
 
 
@@ -254,10 +286,24 @@
     pool_count = pool_hidden.shape[0]
     per = hard_ids.shape[1] // owners
     column_count = batch_hidden.shape[0] * lax.axis_size("pa")
+    members, size = lax.axis_size("pa"), batch_hidden.shape[0]
+    pairs = members // 2
     term, weight = ((rows, depth), BF16), ((pool_count, rows), F32)
 
+    ring = [0] + list(range(1, owners, 2)) + list(range(2, owners, 2))[::-1]
+
     def shift(x, k):
-        return lax.ppermute(x, "pb", [(i, (i + k) % owners) for i in range(owners)])
+        to = [(ring[p], ring[(p + k) % owners]) for p in range(owners)]
+        return lax.ppermute(x, "pb", to)
+
+    def hold(x, others):
+        return lax.optimization_barrier([x] + list(others))[0]
+
+    def swap(x):
+        return lax.ppermute(x, "pa", [(i, i ^ 1) for i in range(members)])
+
+    def pass_on(x, step):
+        return lax.ppermute(x, "pa", [(i, (i + 2 * step) % members) for i in range(members)])
 
     (packed,) = call(
         functools.partial(pack_kernel, owners, pool_count),
@@ -266,45 +312,77 @@
         in_place=[queries],
         scratch=[pltpu.SemaphoreType.DMA],
     )
-    far = [shift(packed, k) for k in range(1, owners)]
-    hidden = lax.all_gather(batch_hidden, "pa", axis=0, tiled=True)
+    block = shift(packed, 1)
+    other = swap(batch_hidden)
     table, turned, own_stat, own_weight, own_term = call(
         functools.partial(own_kernel, owners, per, scale),
         [((pool_count, depth), BF16), term, ((2, rows), F32), weight, term],
         [packed, pool_hidden, projection],
         flops=2 * depth * (pool_count * depth + rows * depth + 2 * rows * pool_count),
     )
+    (chip,) = call(pair_kernel, [((2, size, depth), BF16)], [batch_hidden, other], flops=size * depth)
     column, power, place, group_stat = call(
-        functools.partial(group_kernel, scale),
+        functools.partial(group_kernel, scale, pairs),
         [
             ((column_count, depth), BF16),
             ((column_count, rows), F32),
             ((column_count, rows), F32),
             ((2, rows), F32),
         ],
-        [queries, hidden, projection, query_group[None, :], group_lists],
+        [queries, projection, query_group[None, :], group_lists]
+        + [chip]
+        + [pass_on(chip, step) for step in range(1, pairs)],
+        scratch=[pltpu.VMEM((pairs, 2, size, depth), BF16)],
         flops=2 * depth * column_count * (rows + depth),
     )
-    outs = call(
-        functools.partial(far_kernel, owners, per, scale),
-        [((2 * owners + 2, rows), F32)] + [weight] * (owners - 1) + [term] * (owners - 1),
-        [table, own_stat, group_stat] + far,
-        flops=4 * (owners - 1) * rows * pool_count * depth,
-    )
-    stat, weights, terms = outs[0], [own_weight] + outs[1:owners], outs[owners:]
-    stats = [stat] + [shift(stat, k) for k in range(1, owners)]
-    terms = [shift(terms[k - 1], owners - k) for k in range(1, owners)]
-    turned = [turned] + call(
-        functools.partial(turn_kernel, owners - 1),
-        [term] * (owners - 1),
-        [projection] + far,
-        after=[stat],
-        flops=2 * (owners - 1) * rows * depth * depth,
-    )
-    members, size = lax.axis_size("pa"), batch_hidden.shape[0]
-    pairs = members // 2
+    stats, weights, terms, turned = [own_stat], [own_weight], [], [turned]
+    direct = owners // 2 - 1
+    waits, chain = [own_stat, chip], None
+    for slot in range(1, owners):
+        last = slot + 1 == owners
+        later = None if last else shift(hold(block, waits), 1)
+        one_stat, one_weight = call(
+            functools.partial(score_kernel, owners, per, scale),
+            [((2, rows), F32), weight],
+            [table, block],
+            after=turned[1:] if last else (),
+            flops=2 * rows * pool_count * depth,
+        )
+        stats.append(one_stat)
+        weights.append(one_weight)
+        if last:
+            (stat,) = call(
+                join_kernel, [((2 * owners + 2, rows), F32)], stats + [group_stat], flops=rows
+            )
+        straight = slot <= direct or last
+        shape = ((rows, depth), BF16) if straight else ((rows + SUB, depth), BF16)
+        (one_term,) = call(
+            term_kernel,
+            [shape],
+            [table, one_stat, one_weight] + ([] if chain is None else [chain]),
+            flops=2 * rows * pool_count * depth,
+        )
+        if slot <= direct:
+            terms.append((slot, one_term))
+        else:
+            chain = (slot, one_term)
+            if not last:
+                chain = shift(one_term, 1)
+        turned += call(
+            functools.partial(turn_kernel, 1),
+            [term],
+            [projection, block],
+            after=[stat if last else one_stat],
+            flops=2 * rows * depth * depth,
+        )
+        waits = [one_stat, group_stat]
+        block = later
+    stats = [stat]
+    for k in range(1, owners):
+        stats.append(shift(stat, k))
+    terms = [shift(hold(one, [stat]), owners - k) for k, one in terms + [chain]]
     keep, give, total, factor = call(
-        functools.partial(soft_kernel, owners, scale),
+        functools.partial(soft_kernel, owners, direct, scale),
         [
             ((pairs, size, depth), F32),
             ((pairs * size, depth), BF16),
@@ -312,10 +390,10 @@
             ((rows, rows), F32),
         ],
         [power, place, labels[None, :], queries, column, own_term] + stats,
-        after=turned[1:2],
+        after=turned[-1:],
         flops=4 * rows * column_count * depth,
     )
-    got = lax.ppermute(give, "pa", [(i, i ^ 1) for i in range(members)])
+    got = swap(give)
     parts = call(
         merge_kernel,
         [((size, depth), F32)] + [((size, depth), BF16)] * (pairs - 1),
@@ -323,8 +401,7 @@
         flops=column_count * depth,
     )
     for step in range(1, pairs):
-        to = [(i, (i + 2 * step) % members) for i in range(members)]
-        parts[step] = lax.ppermute(parts[step], "pa", to)
+        parts[step] = pass_on(parts[step], step)
     (pool_hidden_grad,) = call(
         functools.partial(pool_kernel, owners, scale),
         [((pool_count, depth), BF16)],
@@ -338,7 +415,7 @@
         flops=2 * batch_hidden.shape[0] * depth * depth,
     )
     (query_grad,) = call(
-        functools.partial(query_kernel, owners, scale),
+        functools.partial(query_kernel, scale),
         [((rows, depth), BF16)],
         [total, factor] + terms,
         flops=4 * rows * depth * owners,
@@ -347,19 +424,11 @@
 
 
 def solution(mesh):
+    spread = P(("pa", "pb"))
     return jax.shard_map(
         shards,
         mesh=mesh,
-        in_specs=(
-            P(("pa", "pb"), None),
-            P(("pa", "pb"), None),
-            P(("pa", "pb"), None),
-            P(),
-            P(("pa", "pb"), None),
-            P(("pa", "pb")),
-            P(("pa", "pb")),
-            P(),
-        ),
-        out_specs=(P(("pa", "pb"), None), P(("pa", "pb"), None), P(("pa", "pb"), None)),
+        in_specs=(spread, spread, spread, P(), spread, spread, spread, P()),
+        out_specs=(spread, spread, spread),
         check_vma=False,
     )

time: 64.2 us -> 61.3 us (0.955)
  blocking collectives: 9.51 us -> 0 us
  waiting for transfers between devices: 14.8 us -> 20.2 us
  starting transfers between devices: 18.1 us -> 21.8 us
  local copies, waits for them, and re-layouts: 6.48 us -> 4.48 us
    all_gather x1 -> x0, blocking collectives: 9.51 us -> none  [shards(): hidden = lax.all_gather(batch_hidden, 'pa', axis=0, tiled=True)]
    ppermute x13 -> x17, waiting for transfers between devices: 14.8 us -> 20.2 us  [the longest x9 14.2 us: shift(): return lax.ppermute(x, 'pb', to)]
    ppermute x13 -> x17, starting transfers between devices: 18.1 us -> 21.8 us  [the longest x9 14.7 us: shift(): return lax.ppermute(x, 'pb', to)]
    unnamed x18 -> x20, local copies, waits for them, and re-layouts: 6.48 us -> 4.48 us
    pallas_call x10 -> x19, Pallas kernels: 14.1 us -> 13.8 us  [call(): pl.pallas_call(body, out_shape=outs, in_specs=[vmem] * (len(arrays) - len...]
  transfers between devices with their start and end apart: 13 -> 17, of which waited for: 5 -> 10; matrix products, arithmetic and copies ran while one was open for 0% -> 0% of each run, Pallas kernels for 15% -> 21%
where the time goes in v3:
time: 61.3 us; the launch traced here: 61.1 us
  starting transfers between devices  21.8 us (36%)
  waiting for transfers between devices  20.2 us (33%)
  Pallas kernels  13.8 us (23%)
  local copies, waits for them, and re-layouts  4.48 us (7%)
  between operations  0.83 us (1%)
    ppermute x9, starting transfers between devices, shift(): return lax.ppermute(x, 'pb', to)  14.7 us
    ppermute x9, waiting for transfers between devices, shift(): return lax.ppermute(x, 'pb', to)  14.2 us
    pallas_call x19, Pallas kernels, call(): pl.pallas_call(body, out_shape=outs, in_specs=[vmem] * (len(arrays) - len...  13.8 us
    ppermute x6, starting transfers between devices, pass_on(): lax.ppermute(x, 'pa', [(i, (i + 2 * step) % members) for i in range(membe...  7 us
    ppermute x6, waiting for transfers between devices, pass_on(): lax.ppermute(x, 'pa', [(i, (i + 2 * step) % members) for i in range(membe...  4.58 us
    unnamed x20, local copies, waits for them, and re-layouts  4.48 us
    ppermute x2, waiting for transfers between devices, swap(): return lax.ppermute(x, 'pa', [(i, i ^ 1) for i in range(members)])  1.34 us
  transfers between devices with their start and end apart: 17, of which 10 were waited for; matrix products, arithmetic and copies ran while one was open for 0% of the time, Pallas kernels for 21%

profile of v3, /device:TPU:0, one launch (start us, length us, event | category | flops | bytes accessed | tf_op | source)
XLA Modules:
  0.0 61.1 jit_solution(8468097079453099271)
XLA Ops:
  0.6 0.9 %copy-done.2 = bf16[128,1024]{1,0:T(8,128)(2,1)S(1)} copy-done((bf16[128,1024]{1,0:T(8,128)(2,1)S(1)}, bf16[128,1024]{1,0:T(8,128)(2,1)}, u32[]{:S(2)}) %copy-start.2) | copy-done | bytes 262168
  1.6 0.7 %copy-done.6 = s32[128,16]{0,1:T(8,128)S(1)} copy-done((s32[128,16]{0,1:T(8,128)S(1)}, s32[128,16]{0,1:T(8,128)}, u32[]{:S(2)}) %copy-start.6) | copy-done | bytes 8216
  2.3 3.1 %collective-permute-start.4 = (bf16[136,1024]{1,0:T(8,128)(2,1)S(1)}, bf16[136,1024]{1,0:T(8,128)(2,1)S(1)}, u32[]{:S(2)}, u32[]{:S(2)}) collective-permute-start(bf16[136,1024]{1,0:T(8,128)(2,1)S(1)} %shard_map.105.refs_0_), channel_id=1, source_target_pairs={{0,1},{1,3},{3,2},{2,0},{4,5},{5,7},{7,6},{6,4},{8,9},{9,11},{11,1... | collective-permute-start | bytes 835592 | tf_op jit(solution)/shard_map/ppermute | solution.py:297
  5.5 1.6 %copy-done = bf16[1024,1024]{1,0:T(8,128)(2,1)S(1)} copy-done((bf16[1024,1024]{1,0:T(8,128)(2,1)S(1)}, bf16[1024,1024]{1,0:T(8,128)(2,1)}, u32[]{:S(2)}) %copy-start) | copy-done | bytes 2097176
  7.0 1.2 %copy-done.9 = bf16[512,1024]{1,0:T(8,128)(2,1)S(1)} copy-done((bf16[512,1024]{1,0:T(8,128)(2,1)S(1)}, bf16[512,1024]{1,0:T(8,128)(2,1)}, u32[]{:S(2)}) %copy-start.9) | copy-done | bytes 1048600
  8.3 2.8 %shard_map.106 = (bf16[512,1024]{1,0:T(8,128)(2,1)S(1)}, bf16[128,1024]{1,0:T(8,128)(2,1)S(1)}, f32[2,128]{1,0:T(2,128)S(1)}, f32[512,128]{1,0:T(8,128)S(1)}, bf16[128,1024]{1,0:T(8,128)(2,1)S(1)}) custom-call(bf16[136,1024]{1,0:T(8,128)(2,1)S(1)} %shard_map.105.refs_0_, bf16[512,1024]{1,0:T(8,128)(2,1)S(1)} %copy-done.9, bf16[1024,1024]{1,0:T(8,128)(2,1)S(1)} %copy-done), custom_call_target="tpu_custom_call" | custom-call | flops 1610612736 | bytes 5260288 | tf_op jit(solution)/shard_map/pallas_call | solution.py:266
  11.1 2.0 %collective-permute-done.4.refs_1_ = bf16[136,1024]{1,0:T(8,128)(2,1)S(1)} collective-permute-done((bf16[136,1024]{1,0:T(8,128)(2,1)S(1)}, bf16[136,1024]{1,0:T(8,128)(2,1)S(1)}, u32[]{:S(2)}, u32[]{:S(2)}) %collective-permute-start.4) | collective-permute-done | bytes 278560 | tf_op jit(solution)/shard_map/ppermute | solution.py:297
  13.1 0.8 %collective-permute-start.5 = (bf16[136,1024]{1,0:T(8,128)(2,1)S(1)}, bf16[136,1024]{1,0:T(8,128)(2,1)S(1)}, u32[]{:S(2)}, u32[]{:S(2)}) collective-permute-start(bf16[136,1024]{1,0:T(8,128)(2,1)S(1)} %collective-permute-done.4.refs_1_), channel_id=1, source_target_pairs={{0,1},{1,3},{3,2},{2,0},{4,5},{5,7},{7,6},{6,4},{8,9},{9,11},{11,1... | collective-permute-start | bytes 835592 | tf_op jit(solution)/shard_map/ppermute | solution.py:297
  14.0 2.4 %collective-permute-start.3 = (bf16[2,16,1024]{2,1,0:T(8,128)(2,1)S(1)}, bf16[2,16,1024]{2,1,0:T(8,128)(2,1)S(1)}, u32[]{:S(2)}, u32[]{:S(2)}) collective-permute-start(bf16[2,16,1024]{2,1,0:T(8,128)(2,1)S(1)} %shard_map.103.refs_4_), channel_id=1, source_target_pairs={{0,24},{4,28},{8,0},{12,4},{16,8},{20,12},{24,16},{28,20},{1,25},{... | collective-permute-start | bytes 196616 | tf_op jit(solution)/shard_map/ppermute | solution.py:306
  16.9 0.6 collective-permute-start.1
  17.5 1.2 %collective-permute-done.3.refs_7_ = bf16[2,16,1024]{2,1,0:T(8,128)(2,1)S(1)} collective-permute-done((bf16[2,16,1024]{2,1,0:T(8,128)(2,1)S(1)}, bf16[2,16,1024]{2,1,0:T(8,128)(2,1)S(1)}, u32[]{:S(2)}, u32[]{:S(2)}) %collective-permute-start.3) | collective-permute-done | bytes 65568 | tf_op jit(solution)/shard_map/ppermute | solution.py:306
  18.7 2.6 %collective-permute-done.2.refs_6_ = bf16[2,16,1024]{2,1,0:T(8,128)(2,1)S(1)} collective-permute-done((bf16[2,16,1024]{2,1,0:T(8,128)(2,1)S(1)}, bf16[2,16,1024]{2,1,0:T(8,128)(2,1)S(1)}, u32[]{:S(2)}, u32[]{:S(2)}) %collective-permute-start.2) | collective-permute-done | bytes 65568 | tf_op jit(solution)/shard_map/ppermute | solution.py:306
  21.3 0.8 %collective-permute-done.1.refs_5_ = bf16[2,16,1024]{2,1,0:T(8,128)(2,1)S(1)} collective-permute-done((bf16[2,16,1024]{2,1,0:T(8,128)(2,1)S(1)}, bf16[2,16,1024]{2,1,0:T(8,128)(2,1)S(1)}, u32[]{:S(2)}, u32[]{:S(2)}) %collective-permute-start.1) | collective-permute-done | bytes 65568 | tf_op jit(solution)/shard_map/ppermute | solution.py:306
  22.1 1.0 %shard_map.104 = (bf16[128,1024]{1,0:T(8,128)(2,1)S(1)}, f32[128,128]{1,0:T(8,128)S(1)}, f32[128,128]{1,0:T(8,128)S(1)}, f32[2,128]{1,0:T(2,128)S(1)}) custom-call(bf16[128,1024]{1,0:T(8,128)(2,1)S(1)} %copy-done.3, bf16[1024,1024]{1,0:T(8,128)(2,1)S(1)} %copy-done.1, s32[1,128]{1,0:T(1,128)S(1)} %bitcast.6, s32[64,64]{1,0:T(8,128)S(1)} %copy-done.4, ...), custom_call_target="tpu_custom_call" | custom-call | flops 301989888 | bytes 3032576 | tf_op jit(solution)/shard_map/pallas_call | solution.py:266
  23.1 0.6 shard_map.107
  23.7 3.4 %collective-permute-start.6 = (bf16[136,1024]{1,0:T(8,128)(2,1)S(1)}, bf16[136,1024]{1,0:T(8,128)(2,1)S(1)}, u32[]{:S(2)}, u32[]{:S(2)}) collective-permute-start(bf16[136,1024]{1,0:T(8,128)(2,1)S(1)} %collective-permute-done.5.refs_1_), channel_id=1, source_target_pairs={{0,1},{1,3},{3,2},{2,0},{4,5},{5,7},{7,6},{6,4},{8,9},{9,11},{11,1... | collective-permute-start | bytes 835592 | tf_op jit(solution)/shard_map/ppermute | solution.py:297
  28.5 0.8 %shard_map.109.refs_2_.refs_9_ = bf16[128,1024]{1,0:T(8,128)(2,1)S(1)} custom-call(bf16[1024,1024]{1,0:T(8,128)(2,1)S(1)} %copy-done.1, bf16[136,1024]{1,0:T(8,128)(2,1)S(1)} %collective-permute-done.4.refs_1_, f32[2,128]{1,0:T(2,128)S(1)} %get-tuple-element.36.refs_2_.refs_1_), custom_call_target="tpu_custom_call" | custom-call | flops 268435456 | bytes 2637824 | tf_op jit(solution)/shard_map/pallas_call | solution.py:266
  29.3 0.8 %shard_map.110.refs_3_.refs_10_ = bf16[128,1024]{1,0:T(8,128)(2,1)S(1)} custom-call(bf16[1024,1024]{1,0:T(8,128)(2,1)S(1)} %copy-done.1, bf16[136,1024]{1,0:T(8,128)(2,1)S(1)} %collective-permute-done.5.refs_1_, f32[2,128]{1,0:T(2,128)S(1)} %get-tuple-element.38.refs_2_.refs_1_), custom_call_target="tpu_custom_call" | custom-call | flops 268435456 | bytes 2637824 | tf_op jit(solution)/shard_map/pallas_call | solution.py:266
  30.1 4.1 %collective-permute-done.6.refs_1_ = bf16[136,1024]{1,0:T(8,128)(2,1)S(1)} collective-permute-done((bf16[136,1024]{1,0:T(8,128)(2,1)S(1)}, bf16[136,1024]{1,0:T(8,128)(2,1)S(1)}, u32[]{:S(2)}, u32[]{:S(2)}) %collective-permute-start.6) | collective-permute-done | bytes 278560 | tf_op jit(solution)/shard_map/ppermute | solution.py:297
  34.8 3.0 %collective-permute-done.11.refs_3_ = bf16[136,1024]{1,0:T(8,128)(2,1)S(1)} collective-permute-done((bf16[136,1024]{1,0:T(8,128)(2,1)S(1)}, bf16[136,1024]{1,0:T(8,128)(2,1)S(1)}, u32[]{:S(2)}, u32[]{:S(2)}) %collective-permute-start.11) | collective-permute-done | bytes 278560 | tf_op jit(solution)/shard_map/ppermute | solution.py:297
  38.5 1.8 %collective-permute-start.12 = (bf16[128,1024]{1,0:T(8,128)(2,1)S(1)}, bf16[128,1024]{1,0:T(8,128)(2,1)S(1)}, u32[]{:S(2)}, u32[]{:S(2)}) collective-permute-start(bf16[128,1024]{1,0:T(8,128)(2,1)S(1)} %shard_map.117), channel_id=1, source_target_pairs={{0,1},{1,3},{3,2},{2,0},{4,5},{5,7},{7,6},{6,4},{8,9},{9,11},{11,1... | collective-permute-start | bytes 786440 | tf_op jit(solution)/shard_map/ppermute | solution.py:297
  40.2 1.1 %collective-permute-start.9 = (f32[10,128]{1,0:T(8,128)S(1)}, f32[10,128]{1,0:T(8,128)S(1)}, u32[]{:S(2)}, u32[]{:S(2)}) collective-permute-start(f32[10,128]{1,0:T(8,128)S(1)} %shard_map.112.refs_2_.refs_6_.refs_0_), channel_id=1, source_target_pairs={{0,2},{1,0},{3,1},{2,3},{4,6},{5,4},{7,5},{6,7},{8,10},{9,8},{11,9... | collective-permute-start | bytes 15368 | tf_op jit(solution)/shard_map/ppermute | solution.py:297
  41.4 4.0 %collective-permute-start.8 = (f32[10,128]{1,0:T(8,128)S(1)}, f32[10,128]{1,0:T(8,128)S(1)}, u32[]{:S(2)}, u32[]{:S(2)}) collective-permute-start(f32[10,128]{1,0:T(8,128)S(1)} %shard_map.112.refs_2_.refs_6_.refs_0_), channel_id=1, source_target_pairs={{0,3},{1,2},{3,0},{2,1},{4,7},{5,6},{7,4},{6,5},{8,11},{9,10},{11,... | collective-permute-start | bytes 15368 | tf_op jit(solution)/shard_map/ppermute | solution.py:297
  45.4 0.8 %shard_map.113.refs_10_.refs_11_ = bf16[128,1024]{1,0:T(8,128)(2,1)S(1)} custom-call(bf16[1024,1024]{1,0:T(8,128)(2,1)S(1)} %copy-done.1, bf16[136,1024]{1,0:T(8,128)(2,1)S(1)} %collective-permute-done.6.refs_1_, f32[10,128]{1,0:T(8,128)S(1)} %shard_map.112.refs_2_.refs_6_.refs_0_), custom_call_target="tpu_custom_call" | custom-call | flops 268435456 | bytes 2637824 | tf_op jit(solution)/shard_map/pallas_call | solution.py:266
  46.2 2.2 %collective-permute-done.9.refs_9_.refs_3_ = f32[10,128]{1,0:T(8,128)S(1)} collective-permute-done((f32[10,128]{1,0:T(8,128)S(1)}, f32[10,128]{1,0:T(8,128)S(1)}, u32[]{:S(2)}, u32[]{:S(2)}) %collective-permute-start.9) | collective-permute-done | bytes 5152 | tf_op jit(solution)/shard_map/ppermute | solution.py:297
  48.5 2.8 %collective-permute-done.8.refs_8_.refs_2_ = f32[10,128]{1,0:T(8,128)S(1)} collective-permute-done((f32[10,128]{1,0:T(8,128)S(1)}, f32[10,128]{1,0:T(8,128)S(1)}, u32[]{:S(2)}, u32[]{:S(2)}) %collective-permute-start.8) | collective-permute-done | bytes 5152 | tf_op jit(solution)/shard_map/ppermute | solution.py:297
  51.8 1.3 %collective-permute-done.13 = bf16[64,1024]{1,0:T(8,128)(2,1)S(1)} collective-permute-done((bf16[64,1024]{1,0:T(8,128)(2,1)S(1)}, bf16[64,1024]{1,0:T(8,128)(2,1)S(1)}, u32[]{:S(2)}, u32[]{:S(2)}) %collective-permute-start.13) | collective-permute-done | bytes 131104 | tf_op jit(solution)/shard_map/ppermute | solution.py:303
  53.2 0.9 %collective-permute-start.15 = (bf16[16,1024]{1,0:T(8,128)(2,1)S(1)}, bf16[16,1024]{1,0:T(8,128)(2,1)S(1)}, u32[]{:S(2)}, u32[]{:S(2)}) collective-permute-start(bf16[16,1024]{1,0:T(8,128)(2,1)S(1)} %get-tuple-element.53), channel_id=1, source_target_pairs={{0,16},{4,20},{8,24},{12,28},{16,0},{20,4},{24,8},{28,12},{1,17},{... | collective-permute-start | bytes 98312 | tf_op jit(solution)/shard_map/ppermute | solution.py:306
  54.1 2.5 %collective-permute-start.16 = (bf16[16,1024]{1,0:T(8,128)(2,1)S(1)}, bf16[16,1024]{1,0:T(8,128)(2,1)S(1)}, u32[]{:S(2)}, u32[]{:S(2)}) collective-permute-start(bf16[16,1024]{1,0:T(8,128)(2,1)S(1)} %get-tuple-element.54), channel_id=1, source_target_pairs={{0,24},{4,28},{8,0},{12,4},{16,8},{20,12},{24,16},{28,20},{1,25},{... | collective-permute-start | bytes 98312 | tf_op jit(solution)/shard_map/ppermute | solution.py:306
  56.7 2.2 %shard_map.121 = bf16[512,1024]{1,0:T(8,128)(2,1)} custom-call(f32[10,128]{1,0:T(8,128)S(1)} %shard_map.112.refs_2_.refs_6_.refs_0_, f32[10,128]{1,0:T(8,128)S(1)} %collective-permute-done.7.refs_7_.refs_1_, f32[10,128]{1,0:T(8,128)S(1)} %collective-permute-done.8.refs_8_.refs_2_, f32[10,128]{1,0:T(8,128)S(1)} %collective-permute-done.9.refs_9_.refs_3_, ...), custom_call_target="tpu_custom_call" | custom-call | flops 536870912 | bytes 3166208 | tf_op jit(solution)/shard_map/pallas_call | solution.py:266
  58.9 1.3 %shard_map.120 = bf16[16,1024]{1,0:T(8,128)(2,1)} custom-call(bf16[1024,1024]{1,0:T(8,128)(2,1)S(1)} %copy-done.1, f32[16,1024]{1,0:T(8,128)S(1)} %get-tuple-element.51.refs_1_, bf16[16,1024]{1,0:T(8,128)(2,1)S(1)} %collective-permute-done.14.refs_2_, bf16[16,1024]{1,0:T(8,128)(2,1)S(1)} %collective-permute-done.15.refs_3_, ...), custom_call_target="tpu_custom_call" | custom-call | flops 33554432 | bytes 2293760 | tf_op jit(solution)/shard_map/pallas_call | solution.py:266
  60.2 0.9 %shard_map.118 = bf16[128,1024]{1,0:T(8,128)(2,1)} custom-call(f32[128,1024]{1,0:T(8,128)S(1)} %get-tuple-element.42.refs_0_, f32[128,128]{1,0:T(8,128)S(1)} %get-tuple-element.43.refs_1_, bf16[128,1024]{1,0:T(8,128)(2,1)S(1)} %collective-permute-done.10.refs_2_, bf16[128,1024]{1,0:T(8,128)(2,1)S(1)} %collective-permute-done.12.refs_3_), custom_call_target="tpu_custom_call" | custom-call | flops 2097152 | bytes 1376256 | tf_op jit(solution)/shard_map/pallas_call | solution.py:266
  (41 shorter events, 3.8 us)
Async XLA Ops:
  0.6 1.0 %copy-start.2 = (bf16[128,1024]{1,0:T(8,128)(2,1)S(1)}, bf16[128,1024]{1,0:T(8,128)(2,1)}, u32[]{:S(2)}) copy-start(bf16[128,1024]{1,0:T(8,128)(2,1)} %refs_3_.3) | copy-start | bytes 786436
  1.6 0.7 %copy-start.6 = (s32[128,16]{0,1:T(8,128)S(1)}, s32[128,16]{0,1:T(8,128)}, u32[]{:S(2)}) copy-start(s32[128,16]{0,1:T(8,128)} %param.12) | copy-start | bytes 24580
  2.3 8.8 %copy-start.5 = (bf16[16,1024]{1,0:T(8,128)(2,1)S(1)}, bf16[16,1024]{1,0:T(8,128)(2,1)}, u32[]{:S(2)}) copy-start(bf16[16,1024]{1,0:T(8,128)(2,1)} %refs_0_.6) | copy-start | bytes 98308
  2.3 19.8 %copy-start.3 = (bf16[128,1024]{1,0:T(8,128)(2,1)S(1)}, bf16[128,1024]{1,0:T(8,128)(2,1)}, u32[]{:S(2)}) copy-start(bf16[128,1024]{1,0:T(8,128)(2,1)} %refs_3_.3) | copy-start | bytes 786436
  2.3 19.8 %copy-start.4 = (s32[64,64]{1,0:T(8,128)S(1)}, s32[64,64]{1,0:T(8,128)}, u32[]{:S(2)}) copy-start(s32[64,64]{1,0:T(8,128)} %refs_3_.2) | copy-start | bytes 49156
  2.3 19.8 %copy-start.7 = (s32[128]{0:T(128)S(1)}, s32[128]{0:T(128)}, u32[]{:S(2)}) copy-start(s32[128]{0:T(128)} %param.13) | copy-start | bytes 1540
  2.3 10.8 %collective-permute-start.4 = (bf16[136,1024]{1,0:T(8,128)(2,1)S(1)}, bf16[136,1024]{1,0:T(8,128)(2,1)S(1)}, u32[]{:S(2)}, u32[]{:S(2)}) collective-permute-start(bf16[136,1024]{1,0:T(8,128)(2,1)S(1)} %shard_map.105.refs_0_), channel_id=1, source_target_pairs={{0,1},{1,3},{3,2},{2,0},{4,5},{5,7},{7,6},{6,4},{8,9},{9,11},{11,1... | collective-permute-start | bytes 835592 | tf_op jit(solution)/shard_map/ppermute | solution.py:297
  5.5 5.6 %collective-permute-start = (bf16[16,1024]{1,0:T(8,128)(2,1)}, bf16[16,1024]{1,0:T(8,128)(2,1)S(1)}, u32[]{:S(2)}, u32[]{:S(2)}) collective-permute-start(bf16[16,1024]{1,0:T(8,128)(2,1)} %refs_0_.6), channel_id=1, source_target_pairs={{0,4},{4,0},{8,12},{12,8},{16,20},{20,16},{24,28},{28,24},{1,5},{5... | collective-permute-start | bytes 98312 | tf_op jit(solution)/shard_map/ppermute | solution.py:303
  5.5 1.6 %copy-start = (bf16[1024,1024]{1,0:T(8,128)(2,1)S(1)}, bf16[1024,1024]{1,0:T(8,128)(2,1)}, u32[]{:S(2)}) copy-start(bf16[1024,1024]{1,0:T(8,128)(2,1)} %refs_0_.11) | copy-start | bytes 6291460
  7.0 1.2 %copy-start.9 = (bf16[512,1024]{1,0:T(8,128)(2,1)S(1)}, bf16[512,1024]{1,0:T(8,128)(2,1)}, u32[]{:S(2)}) copy-start(bf16[512,1024]{1,0:T(8,128)(2,1)} %refs_1_.5) | copy-start | bytes 3145732
  8.3 13.8 %copy-start.1 = (bf16[1024,1024]{1,0:T(8,128)(2,1)S(1)}, bf16[1024,1024]{1,0:T(8,128)(2,1)}, u32[]{:S(2)}) copy-start(bf16[1024,1024]{1,0:T(8,128)(2,1)} %refs_0_.11) | copy-start | bytes 6291460
  13.1 10.6 %collective-permute-start.5 = (bf16[136,1024]{1,0:T(8,128)(2,1)S(1)}, bf16[136,1024]{1,0:T(8,128)(2,1)S(1)}, u32[]{:S(2)}, u32[]{:S(2)}) collective-permute-start(bf16[136,1024]{1,0:T(8,128)(2,1)S(1)} %collective-permute-done.4.refs_1_), channel_id=1, source_target_pairs={{0,1},{1,3},{3,2},{2,0},{4,5},{5,7},{7,6},{6,4},{8,9},{9,11},{11,1... | collective-permute-start | bytes 835592 | tf_op jit(solution)/shard_map/ppermute | solution.py:297
  14.0 4.7 %collective-permute-start.3 = (bf16[2,16,1024]{2,1,0:T(8,128)(2,1)S(1)}, bf16[2,16,1024]{2,1,0:T(8,128)(2,1)S(1)}, u32[]{:S(2)}, u32[]{:S(2)}) collective-permute-start(bf16[2,16,1024]{2,1,0:T(8,128)(2,1)S(1)} %shard_map.103.refs_4_), channel_id=1, source_target_pairs={{0,24},{4,28},{8,0},{12,4},{16,8},{20,12},{24,16},{28,20},{1,25},{... | collective-permute-start | bytes 196616 | tf_op jit(solution)/shard_map/ppermute | solution.py:306
  16.4 4.9 %collective-permute-start.2 = (bf16[2,16,1024]{2,1,0:T(8,128)(2,1)S(1)}, bf16[2,16,1024]{2,1,0:T(8,128)(2,1)S(1)}, u32[]{:S(2)}, u32[]{:S(2)}) collective-permute-start(bf16[2,16,1024]{2,1,0:T(8,128)(2,1)S(1)} %shard_map.103.refs_4_), channel_id=1, source_target_pairs={{0,16},{4,20},{8,24},{12,28},{16,0},{20,4},{24,8},{28,12},{1,17},{... | collective-permute-start | bytes 196616 | tf_op jit(solution)/shard_map/ppermute | solution.py:306
  16.9 5.2 %collective-permute-start.1 = (bf16[2,16,1024]{2,1,0:T(8,128)(2,1)S(1)}, bf16[2,16,1024]{2,1,0:T(8,128)(2,1)S(1)}, u32[]{:S(2)}, u32[]{:S(2)}) collective-permute-start(bf16[2,16,1024]{2,1,0:T(8,128)(2,1)S(1)} %shard_map.103.refs_4_), channel_id=1, source_target_pairs={{0,8},{4,12},{8,16},{12,20},{16,24},{20,28},{24,0},{28,4},{1,9},{5... | collective-permute-start | bytes 196616 | tf_op jit(solution)/shard_map/ppermute | solution.py:306
  23.7 10.5 %collective-permute-start.6 = (bf16[136,1024]{1,0:T(8,128)(2,1)S(1)}, bf16[136,1024]{1,0:T(8,128)(2,1)S(1)}, u32[]{:S(2)}, u32[]{:S(2)}) collective-permute-start(bf16[136,1024]{1,0:T(8,128)(2,1)S(1)} %collective-permute-done.5.refs_1_), channel_id=1, source_target_pairs={{0,1},{1,3},{3,2},{2,0},{4,5},{5,7},{7,6},{6,4},{8,9},{9,11},{11,1... | collective-permute-start | bytes 835592 | tf_op jit(solution)/shard_map/ppermute | solution.py:297
  28.1 9.7 %collective-permute-start.11 = (bf16[136,1024]{1,0:T(8,128)(2,1)S(1)}, bf16[136,1024]{1,0:T(8,128)(2,1)S(1)}, u32[]{:S(2)}, u32[]{:S(2)}) collective-permute-start(bf16[136,1024]{1,0:T(8,128)(2,1)S(1)} %shard_map.116), channel_id=1, source_target_pairs={{0,1},{1,3},{3,2},{2,0},{4,5},{5,7},{7,6},{6,4},{8,9},{9,11},{11,1... | collective-permute-start | bytes 835592 | tf_op jit(solution)/shard_map/ppermute | solution.py:297
  37.8 13.6 %copy-start.8 = (s32[128]{0:T(128)S(1)}, s32[128]{0:T(128)}, u32[]{:S(2)}) copy-start(s32[128]{0:T(128)} %param.14) | copy-start | bytes 1540
  38.2 22.0 %collective-permute-start.10 = (bf16[128,1024]{1,0:T(8,128)(2,1)S(1)}, bf16[128,1024]{1,0:T(8,128)(2,1)S(1)}, u32[]{:S(2)}, u32[]{:S(2)}) collective-permute-start(bf16[128,1024]{1,0:T(8,128)(2,1)S(1)} %shard_map.115), channel_id=1, source_target_pairs={{0,2},{1,0},{3,1},{2,3},{4,6},{5,4},{7,5},{6,7},{8,10},{9,8},{11,9... | collective-permute-start | bytes 786440 | tf_op jit(solution)/shard_map/ppermute | solution.py:297
  38.5 21.7 %collective-permute-start.12 = (bf16[128,1024]{1,0:T(8,128)(2,1)S(1)}, bf16[128,1024]{1,0:T(8,128)(2,1)S(1)}, u32[]{:S(2)}, u32[]{:S(2)}) collective-permute-start(bf16[128,1024]{1,0:T(8,128)(2,1)S(1)} %shard_map.117), channel_id=1, source_target_pairs={{0,1},{1,3},{3,2},{2,0},{4,5},{5,7},{7,6},{6,4},{8,9},{9,11},{11,1... | collective-permute-start | bytes 786440 | tf_op jit(solution)/shard_map/ppermute | solution.py:297
  40.2 8.2 %collective-permute-start.9 = (f32[10,128]{1,0:T(8,128)S(1)}, f32[10,128]{1,0:T(8,128)S(1)}, u32[]{:S(2)}, u32[]{:S(2)}) collective-permute-start(f32[10,128]{1,0:T(8,128)S(1)} %shard_map.112.refs_2_.refs_6_.refs_0_), channel_id=1, source_target_pairs={{0,2},{1,0},{3,1},{2,3},{4,6},{5,4},{7,5},{6,7},{8,10},{9,8},{11,9... | collective-permute-start | bytes 15368 | tf_op jit(solution)/shard_map/ppermute | solution.py:297
  41.4 9.8 %collective-permute-start.8 = (f32[10,128]{1,0:T(8,128)S(1)}, f32[10,128]{1,0:T(8,128)S(1)}, u32[]{:S(2)}, u32[]{:S(2)}) collective-permute-start(f32[10,128]{1,0:T(8,128)S(1)} %shard_map.112.refs_2_.refs_6_.refs_0_), channel_id=1, source_target_pairs={{0,3},{1,2},{3,0},{2,1},{4,7},{5,6},{7,4},{6,5},{8,11},{9,10},{11,... | collective-permute-start | bytes 15368 | tf_op jit(solution)/shard_map/ppermute | solution.py:297
  45.4 6.0 %collective-permute-start.7 = (f32[10,128]{1,0:T(8,128)S(1)}, f32[10,128]{1,0:T(8,128)S(1)}, u32[]{:S(2)}, u32[]{:S(2)}) collective-permute-start(f32[10,128]{1,0:T(8,128)S(1)} %shard_map.112.refs_2_.refs_6_.refs_0_), channel_id=1, source_target_pairs={{0,1},{1,3},{3,2},{2,0},{4,5},{5,7},{7,6},{6,4},{8,9},{9,11},{11,1... | collective-permute-start | bytes 15368 | tf_op jit(solution)/shard_map/ppermute | solution.py:297
  51.7 1.4 %collective-permute-start.13 = (bf16[64,1024]{1,0:T(8,128)(2,1)S(1)}, bf16[64,1024]{1,0:T(8,128)(2,1)S(1)}, u32[]{:S(2)}, u32[]{:S(2)}) collective-permute-start(bf16[64,1024]{1,0:T(8,128)(2,1)S(1)} %get-tuple-element.50), channel_id=1, source_target_pairs={{0,4},{4,0},{8,12},{12,8},{16,20},{20,16},{24,28},{28,24},{1,5},{5... | collective-permute-start | bytes 393224 | tf_op jit(solution)/shard_map/ppermute | solution.py:303
  53.2 5.7 %collective-permute-start.14 = (bf16[16,1024]{1,0:T(8,128)(2,1)S(1)}, bf16[16,1024]{1,0:T(8,128)(2,1)S(1)}, u32[]{:S(2)}, u32[]{:S(2)}) collective-permute-start(bf16[16,1024]{1,0:T(8,128)(2,1)S(1)} %get-tuple-element.52), channel_id=1, source_target_pairs={{0,8},{4,12},{8,16},{12,20},{16,24},{20,28},{24,0},{28,4},{1,9},{5... | collective-permute-start | bytes 98312 | tf_op jit(solution)/shard_map/ppermute | solution.py:306
  53.2 5.6 %collective-permute-start.15 = (bf16[16,1024]{1,0:T(8,128)(2,1)S(1)}, bf16[16,1024]{1,0:T(8,128)(2,1)S(1)}, u32[]{:S(2)}, u32[]{:S(2)}) collective-permute-start(bf16[16,1024]{1,0:T(8,128)(2,1)S(1)} %get-tuple-element.53), channel_id=1, source_target_pairs={{0,16},{4,20},{8,24},{12,28},{16,0},{20,4},{24,8},{28,12},{1,17},{... | collective-permute-start | bytes 98312 | tf_op jit(solution)/shard_map/ppermute | solution.py:306
  54.1 4.7 %collective-permute-start.16 = (bf16[16,1024]{1,0:T(8,128)(2,1)S(1)}, bf16[16,1024]{1,0:T(8,128)(2,1)S(1)}, u32[]{:S(2)}, u32[]{:S(2)}) collective-permute-start(bf16[16,1024]{1,0:T(8,128)(2,1)S(1)} %get-tuple-element.54), channel_id=1, source_target_pairs={{0,24},{4,28},{8,0},{12,4},{16,8},{20,12},{24,16},{28,20},{1,25},{... | collective-permute-start | bytes 98312 | tf_op jit(solution)/shard_map/ppermute | solution.py:306

commit v4 on v3

--- a/solution.py
+++ b/solution.py
@@ -28,12 +28,15 @@
     return lax.dot_general(a, b, (((0,), (0,)), ((), ())), preferred_element_type=F32)
 
 
-def pack_kernel(owners, pool_count, ids_ref, query_ref, packed_ref, sem):
+def pack_kernel(owners, pool_count, ids_hbm, query_ref, packed_ref, sem, ids_ref, ids_sem):
     rows, depth = query_ref.shape
     hard_count = ids_ref.shape[0]
     per = hard_count // owners
     copy = pltpu.make_async_copy(query_ref, packed_ref.at[:rows, :], sem)
+    ids_copy = pltpu.make_async_copy(ids_hbm, ids_ref, ids_sem)
+    ids_copy.start()
     copy.start()
+    ids_copy.wait()
     packed_ref[rows:, :] = jnp.zeros((SUB, depth), BF16)
     for block in range(hard_count // SUB):
         lines = []
@@ -308,9 +311,16 @@
     (packed,) = call(
         functools.partial(pack_kernel, owners, pool_count),
         [((rows + SUB, depth), BF16)],
-        [hard_ids.T],
-        in_place=[queries],
-        scratch=[pltpu.SemaphoreType.DMA],
+        [],
+        in_place=[
+            pltpu.with_memory_space_constraint(hard_ids.T, pltpu.HBM),
+            pltpu.with_memory_space_constraint(queries, pltpu.HBM),
+        ],
+        scratch=[
+            pltpu.SemaphoreType.DMA,
+            pltpu.VMEM(hard_ids.shape[::-1], jnp.int32),
+            pltpu.SemaphoreType.DMA,
+        ],
     )
     block = shift(packed, 1)
     other = swap(batch_hidden)
@@ -321,6 +331,7 @@
         flops=2 * depth * (pool_count * depth + rows * depth + 2 * rows * pool_count),
     )
     (chip,) = call(pair_kernel, [((2, size, depth), BF16)], [batch_hidden, other], flops=size * depth)
+    chips = [chip] + [pass_on(chip, step) for step in range(1, pairs)]
     column, power, place, group_stat = call(
         functools.partial(group_kernel, scale, pairs),
         [
@@ -329,9 +340,7 @@
             ((column_count, rows), F32),
             ((2, rows), F32),
         ],
-        [queries, projection, query_group[None, :], group_lists]
-        + [chip]
-        + [pass_on(chip, step) for step in range(1, pairs)],
+        [queries, projection, query_group[None, :], group_lists] + chips,
         scratch=[pltpu.VMEM((pairs, 2, size, depth), BF16)],
         flops=2 * depth * column_count * (rows + depth),
     )
@@ -375,12 +384,15 @@
             after=[stat if last else one_stat],
             flops=2 * rows * depth * depth,
         )
-        waits = [one_stat, group_stat]
+        waits = [one_stat]
         block = later
     stats = [stat]
     for k in range(1, owners):
         stats.append(shift(stat, k))
-    terms = [shift(hold(one, [stat]), owners - k) for k, one in terms + [chain]]
+    back = []
+    for k, one in terms + [chain]:
+        back.append(shift(hold(one, [stat]) if k <= direct else one, owners - k))
+    terms = back
     keep, give, total, factor = call(
         functools.partial(soft_kernel, owners, direct, scale),
         [

time: 61.3 us -> 60.3 us (0.984)
  local copies, waits for them, and re-layouts: 4.48 us -> 2.84 us
  Pallas kernels: 13.8 us -> 14.8 us
    unnamed x20 -> x16, local copies, waits for them, and re-layouts: 4.48 us -> 2.84 us
    ppermute x6, starting transfers between devices: 7 us -> 8.51 us  [pass_on(): lax.ppermute(x, 'pa', [(i, (i + 2 * step) % members) for i in range(membe...]
    ppermute x9, starting transfers between devices: 14.7 us -> 13.4 us  [shift(): return lax.ppermute(x, 'pb', to)]
    pallas_call x19, Pallas kernels: 13.8 us -> 14.8 us  [call(): pl.pallas_call(body, out_shape=outs, in_specs=[vmem] * (len(arrays) - len...]
  transfers between devices with their start and end apart: 17 -> 17, of which waited for: 10 -> 9; matrix products, arithmetic and copies ran while one was open for 0% -> 0% of each run, Pallas kernels for 21% -> 21%
where the time goes in v4:
time: 60.3 us; the launch traced here: 60.1 us
  starting transfers between devices  21.9 us (36%)
  waiting for transfers between devices  19.7 us (33%)
  Pallas kernels  14.8 us (25%)
  local copies, waits for them, and re-layouts  2.84 us (5%)
  between operations  0.84 us (1%)
    pallas_call x19, Pallas kernels, call(): pl.pallas_call(body, out_shape=outs, in_specs=[vmem] * (len(arrays) - len...  14.8 us
    ppermute x9, waiting for transfers between devices, shift(): return lax.ppermute(x, 'pb', to)  13.8 us
    ppermute x9, starting transfers between devices, shift(): return lax.ppermute(x, 'pb', to)  13.4 us
    ppermute x6, starting transfers between devices, pass_on(): lax.ppermute(x, 'pa', [(i, (i + 2 * step) % members) for i in range(membe...  8.51 us
    ppermute x6, waiting for transfers between devices, pass_on(): lax.ppermute(x, 'pa', [(i, (i + 2 * step) % members) for i in range(membe...  4.58 us
    unnamed x16, local copies, waits for them, and re-layouts  2.84 us
    ppermute x2, waiting for transfers between devices, swap(): return lax.ppermute(x, 'pa', [(i, i ^ 1) for i in range(members)])  1.34 us
  transfers between devices with their start and end apart: 17, of which 9 were waited for; matrix products, arithmetic and copies ran while one was open for 0% of the time, Pallas kernels for 21%

profile of v4, /device:TPU:0, one launch (start us, length us, event | category | flops | bytes accessed | tf_op | source)
XLA Modules:
  0.0 60.1 jit_solution(14496892459545975390)
XLA Ops:
  0.6 1.0 %shard_map.105.refs_0_ = bf16[136,1024]{1,0:T(8,128)(2,1)S(1)} custom-call(s32[16,128]{1,0:T(8,128)} %bitcast.7, bf16[128,1024]{1,0:T(8,128)(2,1)} %refs_3_.3), custom_call_target="tpu_custom_call" | custom-call | bytes 548864 | tf_op jit(solution)/shard_map/pallas_call | solution.py:269
  1.6 3.1 %collective-permute-start.4 = (bf16[136,1024]{1,0:T(8,128)(2,1)S(1)}, bf16[136,1024]{1,0:T(8,128)(2,1)S(1)}, u32[]{:S(2)}, u32[]{:S(2)}) collective-permute-start(bf16[136,1024]{1,0:T(8,128)(2,1)S(1)} %shard_map.105.refs_0_), channel_id=1, source_target_pairs={{0,1},{1,3},{3,2},{2,0},{4,5},{5,7},{7,6},{6,4},{8,9},{9,11},{11,1... | collective-permute-start | bytes 835592 | tf_op jit(solution)/shard_map/ppermute | solution.py:300
  4.8 1.6 %copy-done = bf16[1024,1024]{1,0:T(8,128)(2,1)S(1)} copy-done((bf16[1024,1024]{1,0:T(8,128)(2,1)S(1)}, bf16[1024,1024]{1,0:T(8,128)(2,1)}, u32[]{:S(2)}) %copy-start) | copy-done | bytes 2097176
  6.3 1.2 %copy-done.7 = bf16[512,1024]{1,0:T(8,128)(2,1)S(1)} copy-done((bf16[512,1024]{1,0:T(8,128)(2,1)S(1)}, bf16[512,1024]{1,0:T(8,128)(2,1)}, u32[]{:S(2)}) %copy-start.7) | copy-done | bytes 1048600
  7.6 2.8 %shard_map.106 = (bf16[512,1024]{1,0:T(8,128)(2,1)S(1)}, bf16[128,1024]{1,0:T(8,128)(2,1)S(1)}, f32[2,128]{1,0:T(2,128)S(1)}, f32[512,128]{1,0:T(8,128)S(1)}, bf16[128,1024]{1,0:T(8,128)(2,1)S(1)}) custom-call(bf16[136,1024]{1,0:T(8,128)(2,1)S(1)} %shard_map.105.refs_0_, bf16[512,1024]{1,0:T(8,128)(2,1)S(1)} %copy-done.7, bf16[1024,1024]{1,0:T(8,128)(2,1)S(1)} %copy-done), custom_call_target="tpu_custom_call" | custom-call | flops 1610612736 | bytes 5260288 | tf_op jit(solution)/shard_map/pallas_call | solution.py:269
  10.4 2.0 %collective-permute-done.4.refs_1_ = bf16[136,1024]{1,0:T(8,128)(2,1)S(1)} collective-permute-done((bf16[136,1024]{1,0:T(8,128)(2,1)S(1)}, bf16[136,1024]{1,0:T(8,128)(2,1)S(1)}, u32[]{:S(2)}, u32[]{:S(2)}) %collective-permute-start.4) | collective-permute-done | bytes 278560 | tf_op jit(solution)/shard_map/ppermute | solution.py:300
  12.4 0.8 %collective-permute-start.5 = (bf16[136,1024]{1,0:T(8,128)(2,1)S(1)}, bf16[136,1024]{1,0:T(8,128)(2,1)S(1)}, u32[]{:S(2)}, u32[]{:S(2)}) collective-permute-start(bf16[136,1024]{1,0:T(8,128)(2,1)S(1)} %collective-permute-done.4.refs_1_), channel_id=1, source_target_pairs={{0,1},{1,3},{3,2},{2,0},{4,5},{5,7},{7,6},{6,4},{8,9},{9,11},{11,1... | collective-permute-start | bytes 835592 | tf_op jit(solution)/shard_map/ppermute | solution.py:300
  13.8 7.3 %collective-permute-done.5.refs_1_ = bf16[136,1024]{1,0:T(8,128)(2,1)S(1)} collective-permute-done((bf16[136,1024]{1,0:T(8,128)(2,1)S(1)}, bf16[136,1024]{1,0:T(8,128)(2,1)S(1)}, u32[]{:S(2)}, u32[]{:S(2)}) %collective-permute-start.5) | collective-permute-done | bytes 278560 | tf_op jit(solution)/shard_map/ppermute | solution.py:300
  21.1 1.0 %collective-permute-start.6 = (bf16[136,1024]{1,0:T(8,128)(2,1)S(1)}, bf16[136,1024]{1,0:T(8,128)(2,1)S(1)}, u32[]{:S(2)}, u32[]{:S(2)}) collective-permute-start(bf16[136,1024]{1,0:T(8,128)(2,1)S(1)} %collective-permute-done.5.refs_1_), channel_id=1, source_target_pairs={{0,1},{1,3},{3,2},{2,0},{4,5},{5,7},{7,6},{6,4},{8,9},{9,11},{11,1... | collective-permute-start | bytes 835592 | tf_op jit(solution)/shard_map/ppermute | solution.py:300
  22.1 0.6 shard_map.108
  23.0 3.0 %collective-permute-start.11 = (bf16[136,1024]{1,0:T(8,128)(2,1)S(1)}, bf16[136,1024]{1,0:T(8,128)(2,1)S(1)}, u32[]{:S(2)}, u32[]{:S(2)}) collective-permute-start(bf16[136,1024]{1,0:T(8,128)(2,1)S(1)} %shard_map.116), channel_id=1, source_target_pairs={{0,1},{1,3},{3,2},{2,0},{4,5},{5,7},{7,6},{6,4},{8,9},{9,11},{11,1... | collective-permute-start | bytes 835592 | tf_op jit(solution)/shard_map/ppermute | solution.py:300
  26.0 2.4 %collective-permute-start.3 = (bf16[2,16,1024]{2,1,0:T(8,128)(2,1)S(1)}, bf16[2,16,1024]{2,1,0:T(8,128)(2,1)S(1)}, u32[]{:S(2)}, u32[]{:S(2)}) collective-permute-start(bf16[2,16,1024]{2,1,0:T(8,128)(2,1)S(1)} %shard_map.103.refs_4_), channel_id=1, source_target_pairs={{0,24},{4,28},{8,0},{12,4},{16,8},{20,12},{24,16},{28,20},{1,25},{... | collective-permute-start | bytes 196616 | tf_op jit(solution)/shard_map/ppermute | solution.py:309
  29.0 0.6 collective-permute-start.1
  29.6 1.4 %collective-permute-done.3.refs_7_ = bf16[2,16,1024]{2,1,0:T(8,128)(2,1)S(1)} collective-permute-done((bf16[2,16,1024]{2,1,0:T(8,128)(2,1)S(1)}, bf16[2,16,1024]{2,1,0:T(8,128)(2,1)S(1)}, u32[]{:S(2)}, u32[]{:S(2)}) %collective-permute-start.3) | collective-permute-done | bytes 65568 | tf_op jit(solution)/shard_map/ppermute | solution.py:309
  31.0 1.8 %collective-permute-done.2.refs_6_ = bf16[2,16,1024]{2,1,0:T(8,128)(2,1)S(1)} collective-permute-done((bf16[2,16,1024]{2,1,0:T(8,128)(2,1)S(1)}, bf16[2,16,1024]{2,1,0:T(8,128)(2,1)S(1)}, u32[]{:S(2)}, u32[]{:S(2)}) %collective-permute-start.2) | collective-permute-done | bytes 65568 | tf_op jit(solution)/shard_map/ppermute | solution.py:309
  32.8 1.4 %collective-permute-done.1.refs_5_ = bf16[2,16,1024]{2,1,0:T(8,128)(2,1)S(1)} collective-permute-done((bf16[2,16,1024]{2,1,0:T(8,128)(2,1)S(1)}, bf16[2,16,1024]{2,1,0:T(8,128)(2,1)S(1)}, u32[]{:S(2)}, u32[]{:S(2)}) %collective-permute-start.1) | collective-permute-done | bytes 65568 | tf_op jit(solution)/shard_map/ppermute | solution.py:309
  34.2 1.0 %shard_map.104 = (bf16[128,1024]{1,0:T(8,128)(2,1)S(1)}, f32[128,128]{1,0:T(8,128)S(1)}, f32[128,128]{1,0:T(8,128)S(1)}, f32[2,128]{1,0:T(2,128)S(1)}) custom-call(bf16[128,1024]{1,0:T(8,128)(2,1)S(1)} %copy-done.2, bf16[1024,1024]{1,0:T(8,128)(2,1)S(1)} %copy-done.1, s32[1,128]{1,0:T(1,128)S(1)} %bitcast.5, s32[64,64]{1,0:T(8,128)S(1)} %copy-done.3, ...), custom_call_target="tpu_custom_call" | custom-call | flops 301989888 | bytes 3032576 | tf_op jit(solution)/shard_map/pallas_call | solution.py:269
  35.5 0.8 %shard_map.109.refs_2_.refs_9_ = bf16[128,1024]{1,0:T(8,128)(2,1)S(1)} custom-call(bf16[1024,1024]{1,0:T(8,128)(2,1)S(1)} %copy-done.1, bf16[136,1024]{1,0:T(8,128)(2,1)S(1)} %collective-permute-done.4.refs_1_, f32[2,128]{1,0:T(2,128)S(1)} %get-tuple-element.35.refs_2_.refs_1_), custom_call_target="tpu_custom_call" | custom-call | flops 268435456 | bytes 2637824 | tf_op jit(solution)/shard_map/pallas_call | solution.py:269
  36.4 0.8 %shard_map.110.refs_3_.refs_10_ = bf16[128,1024]{1,0:T(8,128)(2,1)S(1)} custom-call(bf16[1024,1024]{1,0:T(8,128)(2,1)S(1)} %copy-done.1, bf16[136,1024]{1,0:T(8,128)(2,1)S(1)} %collective-permute-done.5.refs_1_, f32[2,128]{1,0:T(2,128)S(1)} %get-tuple-element.37.refs_2_.refs_1_), custom_call_target="tpu_custom_call" | custom-call | flops 268435456 | bytes 2637824 | tf_op jit(solution)/shard_map/pallas_call | solution.py:269
  37.2 0.6 shard_map.111
  38.3 2.0 %collective-permute-start.12 = (bf16[128,1024]{1,0:T(8,128)(2,1)S(1)}, bf16[128,1024]{1,0:T(8,128)(2,1)S(1)}, u32[]{:S(2)}, u32[]{:S(2)}) collective-permute-start(bf16[128,1024]{1,0:T(8,128)(2,1)S(1)} %shard_map.117), channel_id=1, source_target_pairs={{0,1},{1,3},{3,2},{2,0},{4,5},{5,7},{7,6},{6,4},{8,9},{9,11},{11,1... | collective-permute-start | bytes 786440 | tf_op jit(solution)/shard_map/ppermute | solution.py:300
  40.3 0.9 %collective-permute-start.9 = (f32[10,128]{1,0:T(8,128)S(1)}, f32[10,128]{1,0:T(8,128)S(1)}, u32[]{:S(2)}, u32[]{:S(2)}) collective-permute-start(f32[10,128]{1,0:T(8,128)S(1)} %shard_map.112.refs_2_.refs_6_.refs_0_), channel_id=1, source_target_pairs={{0,2},{1,0},{3,1},{2,3},{4,6},{5,4},{7,5},{6,7},{8,10},{9,8},{11,9... | collective-permute-start | bytes 15368 | tf_op jit(solution)/shard_map/ppermute | solution.py:300
  41.2 2.4 %collective-permute-start.8 = (f32[10,128]{1,0:T(8,128)S(1)}, f32[10,128]{1,0:T(8,128)S(1)}, u32[]{:S(2)}, u32[]{:S(2)}) collective-permute-start(f32[10,128]{1,0:T(8,128)S(1)} %shard_map.112.refs_2_.refs_6_.refs_0_), channel_id=1, source_target_pairs={{0,3},{1,2},{3,0},{2,1},{4,7},{5,6},{7,4},{6,5},{8,11},{9,10},{11,... | collective-permute-start | bytes 15368 | tf_op jit(solution)/shard_map/ppermute | solution.py:300
  43.6 0.8 %shard_map.113.refs_10_.refs_11_ = bf16[128,1024]{1,0:T(8,128)(2,1)S(1)} custom-call(bf16[1024,1024]{1,0:T(8,128)(2,1)S(1)} %copy-done.1, bf16[136,1024]{1,0:T(8,128)(2,1)S(1)} %collective-permute-done.6.refs_1_, f32[10,128]{1,0:T(8,128)S(1)} %shard_map.112.refs_2_.refs_6_.refs_0_), custom_call_target="tpu_custom_call" | custom-call | flops 268435456 | bytes 2637824 | tf_op jit(solution)/shard_map/pallas_call | solution.py:269
  44.5 2.7 %collective-permute-done.9.refs_9_.refs_3_ = f32[10,128]{1,0:T(8,128)S(1)} collective-permute-done((f32[10,128]{1,0:T(8,128)S(1)}, f32[10,128]{1,0:T(8,128)S(1)}, u32[]{:S(2)}, u32[]{:S(2)}) %collective-permute-start.9) | collective-permute-done | bytes 5152 | tf_op jit(solution)/shard_map/ppermute | solution.py:300
  47.2 1.6 %collective-permute-done.8.refs_8_.refs_2_ = f32[10,128]{1,0:T(8,128)S(1)} collective-permute-done((f32[10,128]{1,0:T(8,128)S(1)}, f32[10,128]{1,0:T(8,128)S(1)}, u32[]{:S(2)}, u32[]{:S(2)}) %collective-permute-start.8) | collective-permute-done | bytes 5152 | tf_op jit(solution)/shard_map/ppermute | solution.py:300
  49.4 1.3 %collective-permute-done.13 = bf16[64,1024]{1,0:T(8,128)(2,1)S(1)} collective-permute-done((bf16[64,1024]{1,0:T(8,128)(2,1)S(1)}, bf16[64,1024]{1,0:T(8,128)(2,1)S(1)}, u32[]{:S(2)}, u32[]{:S(2)}) %collective-permute-start.13) | collective-permute-done | bytes 131104 | tf_op jit(solution)/shard_map/ppermute | solution.py:306
  51.2 2.8 %collective-permute-start.15 = (bf16[16,1024]{1,0:T(8,128)(2,1)S(1)}, bf16[16,1024]{1,0:T(8,128)(2,1)S(1)}, u32[]{:S(2)}, u32[]{:S(2)}) collective-permute-start(bf16[16,1024]{1,0:T(8,128)(2,1)S(1)} %get-tuple-element.51), channel_id=1, source_target_pairs={{0,16},{4,20},{8,24},{12,28},{16,0},{20,4},{24,8},{28,12},{1,17},{... | collective-permute-start | bytes 98312 | tf_op jit(solution)/shard_map/ppermute | solution.py:309
  53.9 1.8 %collective-permute-start.16 = (bf16[16,1024]{1,0:T(8,128)(2,1)S(1)}, bf16[16,1024]{1,0:T(8,128)(2,1)S(1)}, u32[]{:S(2)}, u32[]{:S(2)}) collective-permute-start(bf16[16,1024]{1,0:T(8,128)(2,1)S(1)} %get-tuple-element.52), channel_id=1, source_target_pairs={{0,24},{4,28},{8,0},{12,4},{16,8},{20,12},{24,16},{28,20},{1,25},{... | collective-permute-start | bytes 98312 | tf_op jit(solution)/shard_map/ppermute | solution.py:309
  55.7 2.2 %shard_map.121 = bf16[512,1024]{1,0:T(8,128)(2,1)} custom-call(f32[10,128]{1,0:T(8,128)S(1)} %shard_map.112.refs_2_.refs_6_.refs_0_, f32[10,128]{1,0:T(8,128)S(1)} %collective-permute-done.7.refs_7_.refs_1_, f32[10,128]{1,0:T(8,128)S(1)} %collective-permute-done.8.refs_8_.refs_2_, f32[10,128]{1,0:T(8,128)S(1)} %collective-permute-done.9.refs_9_.refs_3_, ...), custom_call_target="tpu_custom_call" | custom-call | flops 536870912 | bytes 3166208 | tf_op jit(solution)/shard_map/pallas_call | solution.py:269
  57.9 1.3 %shard_map.120 = bf16[16,1024]{1,0:T(8,128)(2,1)} custom-call(bf16[1024,1024]{1,0:T(8,128)(2,1)S(1)} %copy-done.1, f32[16,1024]{1,0:T(8,128)S(1)} %get-tuple-element.49.refs_1_, bf16[16,1024]{1,0:T(8,128)(2,1)S(1)} %collective-permute-done.14.refs_2_, bf16[16,1024]{1,0:T(8,128)(2,1)S(1)} %collective-permute-done.15.refs_3_, ...), custom_call_target="tpu_custom_call" | custom-call | flops 33554432 | bytes 2293760 | tf_op jit(solution)/shard_map/pallas_call | solution.py:269
  59.2 0.9 %shard_map.118 = bf16[128,1024]{1,0:T(8,128)(2,1)} custom-call(f32[128,1024]{1,0:T(8,128)S(1)} %get-tuple-element.41.refs_0_, f32[128,128]{1,0:T(8,128)S(1)} %get-tuple-element.42.refs_1_, bf16[128,1024]{1,0:T(8,128)(2,1)S(1)} %collective-permute-done.10.refs_2_, bf16[128,1024]{1,0:T(8,128)(2,1)S(1)} %collective-permute-done.12.refs_3_), custom_call_target="tpu_custom_call" | custom-call | flops 2097152 | bytes 1376256 | tf_op jit(solution)/shard_map/pallas_call | solution.py:269
  (37 shorter events, 3.3 us)
Async XLA Ops:
  0.6 9.7 %copy-start.4 = (bf16[16,1024]{1,0:T(8,128)(2,1)S(1)}, bf16[16,1024]{1,0:T(8,128)(2,1)}, u32[]{:S(2)}) copy-start(bf16[16,1024]{1,0:T(8,128)(2,1)} %refs_0_.6) | copy-start | bytes 98308
  1.6 10.8 %collective-permute-start.4 = (bf16[136,1024]{1,0:T(8,128)(2,1)S(1)}, bf16[136,1024]{1,0:T(8,128)(2,1)S(1)}, u32[]{:S(2)}, u32[]{:S(2)}) collective-permute-start(bf16[136,1024]{1,0:T(8,128)(2,1)S(1)} %shard_map.105.refs_0_), channel_id=1, source_target_pairs={{0,1},{1,3},{3,2},{2,0},{4,5},{5,7},{7,6},{6,4},{8,9},{9,11},{11,1... | collective-permute-start | bytes 835592 | tf_op jit(solution)/shard_map/ppermute | solution.py:300
  4.7 5.6 %collective-permute-start = (bf16[16,1024]{1,0:T(8,128)(2,1)}, bf16[16,1024]{1,0:T(8,128)(2,1)S(1)}, u32[]{:S(2)}, u32[]{:S(2)}) collective-permute-start(bf16[16,1024]{1,0:T(8,128)(2,1)} %refs_0_.6), channel_id=1, source_target_pairs={{0,4},{4,0},{8,12},{12,8},{16,20},{20,16},{24,28},{28,24},{1,5},{5... | collective-permute-start | bytes 98312 | tf_op jit(solution)/shard_map/ppermute | solution.py:306
  4.7 1.6 %copy-start = (bf16[1024,1024]{1,0:T(8,128)(2,1)S(1)}, bf16[1024,1024]{1,0:T(8,128)(2,1)}, u32[]{:S(2)}) copy-start(bf16[1024,1024]{1,0:T(8,128)(2,1)} %refs_0_.11) | copy-start | bytes 6291460
  6.3 1.2 %copy-start.7 = (bf16[512,1024]{1,0:T(8,128)(2,1)S(1)}, bf16[512,1024]{1,0:T(8,128)(2,1)}, u32[]{:S(2)}) copy-start(bf16[512,1024]{1,0:T(8,128)(2,1)} %refs_1_.5) | copy-start | bytes 3145732
  12.4 8.7 %collective-permute-start.5 = (bf16[136,1024]{1,0:T(8,128)(2,1)S(1)}, bf16[136,1024]{1,0:T(8,128)(2,1)S(1)}, u32[]{:S(2)}, u32[]{:S(2)}) collective-permute-start(bf16[136,1024]{1,0:T(8,128)(2,1)S(1)} %collective-permute-done.4.refs_1_), channel_id=1, source_target_pairs={{0,1},{1,3},{3,2},{2,0},{4,5},{5,7},{7,6},{6,4},{8,9},{9,11},{11,1... | collective-permute-start | bytes 835592 | tf_op jit(solution)/shard_map/ppermute | solution.py:300
  13.2 20.9 %copy-start.1 = (bf16[1024,1024]{1,0:T(8,128)(2,1)S(1)}, bf16[1024,1024]{1,0:T(8,128)(2,1)}, u32[]{:S(2)}) copy-start(bf16[1024,1024]{1,0:T(8,128)(2,1)} %refs_0_.11) | copy-start | bytes 6291460
  13.3 20.9 %copy-start.2 = (bf16[128,1024]{1,0:T(8,128)(2,1)S(1)}, bf16[128,1024]{1,0:T(8,128)(2,1)}, u32[]{:S(2)}) copy-start(bf16[128,1024]{1,0:T(8,128)(2,1)} %refs_3_.3) | copy-start | bytes 786436
  13.3 20.9 %copy-start.3 = (s32[64,64]{1,0:T(8,128)S(1)}, s32[64,64]{1,0:T(8,128)}, u32[]{:S(2)}) copy-start(s32[64,64]{1,0:T(8,128)} %refs_3_.2) | copy-start | bytes 49156
  13.3 20.9 %copy-start.5 = (s32[128]{0:T(128)S(1)}, s32[128]{0:T(128)}, u32[]{:S(2)}) copy-start(s32[128]{0:T(128)} %param.13) | copy-start | bytes 1540
  21.1 16.1 %collective-permute-start.6 = (bf16[136,1024]{1,0:T(8,128)(2,1)S(1)}, bf16[136,1024]{1,0:T(8,128)(2,1)S(1)}, u32[]{:S(2)}, u32[]{:S(2)}) collective-permute-start(bf16[136,1024]{1,0:T(8,128)(2,1)S(1)} %collective-permute-done.5.refs_1_), channel_id=1, source_target_pairs={{0,1},{1,3},{3,2},{2,0},{4,5},{5,7},{7,6},{6,4},{8,9},{9,11},{11,1... | collective-permute-start | bytes 835592 | tf_op jit(solution)/shard_map/ppermute | solution.py:300
  23.0 14.8 %collective-permute-start.11 = (bf16[136,1024]{1,0:T(8,128)(2,1)S(1)}, bf16[136,1024]{1,0:T(8,128)(2,1)S(1)}, u32[]{:S(2)}, u32[]{:S(2)}) collective-permute-start(bf16[136,1024]{1,0:T(8,128)(2,1)S(1)} %shard_map.116), channel_id=1, source_target_pairs={{0,1},{1,3},{3,2},{2,0},{4,5},{5,7},{7,6},{6,4},{8,9},{9,11},{11,1... | collective-permute-start | bytes 835592 | tf_op jit(solution)/shard_map/ppermute | solution.py:300
  26.0 4.9 %collective-permute-start.3 = (bf16[2,16,1024]{2,1,0:T(8,128)(2,1)S(1)}, bf16[2,16,1024]{2,1,0:T(8,128)(2,1)S(1)}, u32[]{:S(2)}, u32[]{:S(2)}) collective-permute-start(bf16[2,16,1024]{2,1,0:T(8,128)(2,1)S(1)} %shard_map.103.refs_4_), channel_id=1, source_target_pairs={{0,24},{4,28},{8,0},{12,4},{16,8},{20,12},{24,16},{28,20},{1,25},{... | collective-permute-start | bytes 196616 | tf_op jit(solution)/shard_map/ppermute | solution.py:309
  28.5 4.3 %collective-permute-start.2 = (bf16[2,16,1024]{2,1,0:T(8,128)(2,1)S(1)}, bf16[2,16,1024]{2,1,0:T(8,128)(2,1)S(1)}, u32[]{:S(2)}, u32[]{:S(2)}) collective-permute-start(bf16[2,16,1024]{2,1,0:T(8,128)(2,1)S(1)} %shard_map.103.refs_4_), channel_id=1, source_target_pairs={{0,16},{4,20},{8,24},{12,28},{16,0},{20,4},{24,8},{28,12},{1,17},{... | collective-permute-start | bytes 196616 | tf_op jit(solution)/shard_map/ppermute | solution.py:309
  29.0 5.2 %collective-permute-start.1 = (bf16[2,16,1024]{2,1,0:T(8,128)(2,1)S(1)}, bf16[2,16,1024]{2,1,0:T(8,128)(2,1)S(1)}, u32[]{:S(2)}, u32[]{:S(2)}) collective-permute-start(bf16[2,16,1024]{2,1,0:T(8,128)(2,1)S(1)} %shard_map.103.refs_4_), channel_id=1, source_target_pairs={{0,8},{4,12},{8,16},{12,20},{16,24},{20,28},{24,0},{28,4},{1,9},{5... | collective-permute-start | bytes 196616 | tf_op jit(solution)/shard_map/ppermute | solution.py:309
  37.8 21.4 %collective-permute-start.10 = (bf16[128,1024]{1,0:T(8,128)(2,1)S(1)}, bf16[128,1024]{1,0:T(8,128)(2,1)S(1)}, u32[]{:S(2)}, u32[]{:S(2)}) collective-permute-start(bf16[128,1024]{1,0:T(8,128)(2,1)S(1)} %shard_map.115), channel_id=1, source_target_pairs={{0,2},{1,0},{3,1},{2,3},{4,6},{5,4},{7,5},{6,7},{8,10},{9,8},{11,9... | collective-permute-start | bytes 786440 | tf_op jit(solution)/shard_map/ppermute | solution.py:300
  37.9 11.0 %copy-start.6 = (s32[128]{0:T(128)S(1)}, s32[128]{0:T(128)}, u32[]{:S(2)}) copy-start(s32[128]{0:T(128)} %param.14) | copy-start | bytes 1540
  38.3 21.0 %collective-permute-start.12 = (bf16[128,1024]{1,0:T(8,128)(2,1)S(1)}, bf16[128,1024]{1,0:T(8,128)(2,1)S(1)}, u32[]{:S(2)}, u32[]{:S(2)}) collective-permute-start(bf16[128,1024]{1,0:T(8,128)(2,1)S(1)} %shard_map.117), channel_id=1, source_target_pairs={{0,1},{1,3},{3,2},{2,0},{4,5},{5,7},{7,6},{6,4},{8,9},{9,11},{11,1... | collective-permute-start | bytes 786440 | tf_op jit(solution)/shard_map/ppermute | solution.py:300
  40.3 6.9 %collective-permute-start.9 = (f32[10,128]{1,0:T(8,128)S(1)}, f32[10,128]{1,0:T(8,128)S(1)}, u32[]{:S(2)}, u32[]{:S(2)}) collective-permute-start(f32[10,128]{1,0:T(8,128)S(1)} %shard_map.112.refs_2_.refs_6_.refs_0_), channel_id=1, source_target_pairs={{0,2},{1,0},{3,1},{2,3},{4,6},{5,4},{7,5},{6,7},{8,10},{9,8},{11,9... | collective-permute-start | bytes 15368 | tf_op jit(solution)/shard_map/ppermute | solution.py:300
  41.2 7.5 %collective-permute-start.8 = (f32[10,128]{1,0:T(8,128)S(1)}, f32[10,128]{1,0:T(8,128)S(1)}, u32[]{:S(2)}, u32[]{:S(2)}) collective-permute-start(f32[10,128]{1,0:T(8,128)S(1)} %shard_map.112.refs_2_.refs_6_.refs_0_), channel_id=1, source_target_pairs={{0,3},{1,2},{3,0},{2,1},{4,7},{5,6},{7,4},{6,5},{8,11},{9,10},{11,... | collective-permute-start | bytes 15368 | tf_op jit(solution)/shard_map/ppermute | solution.py:300
  43.6 5.3 %collective-permute-start.7 = (f32[10,128]{1,0:T(8,128)S(1)}, f32[10,128]{1,0:T(8,128)S(1)}, u32[]{:S(2)}, u32[]{:S(2)}) collective-permute-start(f32[10,128]{1,0:T(8,128)S(1)} %shard_map.112.refs_2_.refs_6_.refs_0_), channel_id=1, source_target_pairs={{0,1},{1,3},{3,2},{2,0},{4,5},{5,7},{7,6},{6,4},{8,9},{9,11},{11,1... | collective-permute-start | bytes 15368 | tf_op jit(solution)/shard_map/ppermute | solution.py:300
  49.3 1.4 %collective-permute-start.13 = (bf16[64,1024]{1,0:T(8,128)(2,1)S(1)}, bf16[64,1024]{1,0:T(8,128)(2,1)S(1)}, u32[]{:S(2)}, u32[]{:S(2)}) collective-permute-start(bf16[64,1024]{1,0:T(8,128)(2,1)S(1)} %get-tuple-element.48), channel_id=1, source_target_pairs={{0,4},{4,0},{8,12},{12,8},{16,20},{20,16},{24,28},{28,24},{1,5},{5... | collective-permute-start | bytes 393224 | tf_op jit(solution)/shard_map/ppermute | solution.py:306
  50.7 7.2 %collective-permute-start.14 = (bf16[16,1024]{1,0:T(8,128)(2,1)S(1)}, bf16[16,1024]{1,0:T(8,128)(2,1)S(1)}, u32[]{:S(2)}, u32[]{:S(2)}) collective-permute-start(bf16[16,1024]{1,0:T(8,128)(2,1)S(1)} %get-tuple-element.50), channel_id=1, source_target_pairs={{0,8},{4,12},{8,16},{12,20},{16,24},{20,28},{24,0},{28,4},{1,9},{5... | collective-permute-start | bytes 98312 | tf_op jit(solution)/shard_map/ppermute | solution.py:309
  51.2 6.8 %collective-permute-start.15 = (bf16[16,1024]{1,0:T(8,128)(2,1)S(1)}, bf16[16,1024]{1,0:T(8,128)(2,1)S(1)}, u32[]{:S(2)}, u32[]{:S(2)}) collective-permute-start(bf16[16,1024]{1,0:T(8,128)(2,1)S(1)} %get-tuple-element.51), channel_id=1, source_target_pairs={{0,16},{4,20},{8,24},{12,28},{16,0},{20,4},{24,8},{28,12},{1,17},{... | collective-permute-start | bytes 98312 | tf_op jit(solution)/shard_map/ppermute | solution.py:309
  53.9 4.0 %collective-permute-start.16 = (bf16[16,1024]{1,0:T(8,128)(2,1)S(1)}, bf16[16,1024]{1,0:T(8,128)(2,1)S(1)}, u32[]{:S(2)}, u32[]{:S(2)}) collective-permute-start(bf16[16,1024]{1,0:T(8,128)(2,1)S(1)} %get-tuple-element.52), channel_id=1, source_target_pairs={{0,24},{4,28},{8,0},{12,4},{16,8},{20,12},{24,16},{28,20},{1,25},{... | collective-permute-start | bytes 98312 | tf_op jit(solution)/shard_map/ppermute | solution.py:309

commit v5 on v4

--- a/solution.py
+++ b/solution.py
@@ -192,10 +192,10 @@
 
 
 def soft_kernel(owners, direct, scale, *refs):
-    power_ref, place_ref, label_ref, query_ref, column_ref, own_term_ref = refs[:6]
+    power_ref, place_ref, label_ref, turned_ref, column_ref, own_term_ref = refs[:6]
     stat_refs = refs[6 : 6 + owners]
     keep_ref, give_ref, sum_ref, factor_ref = refs[6 + owners :]
-    rows = query_ref.shape[0]
+    rows = turned_ref.shape[0]
     top, total = totals(stat_refs, owners, 0)
     place = place_ref[...]
     target = (place == (label_ref[...] + 1).astype(F32)).astype(F32)
@@ -207,8 +207,8 @@
     first = lax.rem(lax.axis_index("pa"), 2) == 0
     mine = jnp.where(first, even, odd).reshape(kept * size, rows).astype(BF16)
     other = jnp.where(first, odd, even).reshape(kept * size, rows).astype(BF16)
-    give_ref[...] = (nn(other, query_ref[...]) * scale).astype(BF16)
-    keep_ref[...] = (nn(mine, query_ref[...]) * scale).reshape(keep_ref.shape)
+    give_ref[...] = (nn(other, turned_ref[...]) * scale).astype(BF16)
+    keep_ref[...] = (nn(mine, turned_ref[...]) * scale).reshape(keep_ref.shape)
     tops = [stat_refs[(owners - k) % owners][2 * k : 2 * k + 1, :] for k in range(owners)]
     tops = tops[: direct + 1] + [functools.reduce(jnp.maximum, tops[direct + 1 :])]
     factor = [jnp.exp(one - top) / total for one in tops]
@@ -241,19 +241,15 @@
     out_ref[...] = (acc * scale).astype(BF16)
 
 
-def batch_kernel(projection_ref, own_ref, *refs):
-    total = own_ref[...]
-    for ref in refs[:-1]:
-        total = total + ref[...].astype(F32)
-    refs[-1][...] = nt(total.astype(BF16), projection_ref[...]).astype(BF16)
-
-
-def query_kernel(scale, sum_ref, factor_ref, *refs):
-    out_ref = refs[-1]
+def last_kernel(scale, parts, sum_ref, factor_ref, *refs):
+    query_ref, batch_ref = refs[-2:]
+    batch_ref[...] = functools.reduce(
+        jnp.add, [ref[...].astype(F32) for ref in refs[:parts]]
+    ).astype(BF16)
     total = sum_ref[...]
-    for k, ref in enumerate(refs[:-1]):
+    for k, ref in enumerate(refs[parts:-2]):
         total = total + factor_ref[:, k + 1 : k + 2] * ref[...].astype(F32)
-    out_ref[...] = (total * scale).astype(BF16)
+    query_ref[...] = (total * scale).astype(BF16)
 
 
 def call(kernel, outs, arrays, after=(), flops=0, in_place=(), scratch=()):
@@ -401,7 +397,7 @@
             ((rows, depth), F32),
             ((rows, rows), F32),
         ],
-        [power, place, labels[None, :], queries, column, own_term] + stats,
+        [power, place, labels[None, :], turned[0], column, own_term] + stats,
         after=turned[-1:],
         flops=4 * rows * column_count * depth,
     )
@@ -420,16 +416,10 @@
         stats + weights + turned,
         flops=2 * rows * owners * pool_count * depth,
     )
-    (batch_hidden_grad,) = call(
-        batch_kernel,
-        [(batch_hidden.shape, BF16)],
-        [projection] + parts,
-        flops=2 * batch_hidden.shape[0] * depth * depth,
-    )
-    (query_grad,) = call(
-        functools.partial(query_kernel, scale),
-        [((rows, depth), BF16)],
-        [total, factor] + terms,
+    query_grad, batch_hidden_grad = call(
+        functools.partial(last_kernel, scale, len(parts)),
+        [((rows, depth), BF16), (batch_hidden.shape, BF16)],
+        [total, factor] + parts + terms,
         flops=4 * rows * depth * owners,
     )
     return (query_grad, batch_hidden_grad, pool_hidden_grad)

time: 60.3 us -> 59.1 us (0.980)
  Pallas kernels: 14.8 us -> 13.5 us
    pallas_call x19 -> x18, Pallas kernels: 14.8 us -> 13.5 us  [call(): pl.pallas_call(body, out_shape=outs, in_specs=[vmem] * (len(arrays) - len...]
  transfers between devices with their start and end apart: 17 -> 17, of which waited for: 9 -> 9; matrix products, arithmetic and copies ran while one was open for 0% -> 0% of each run, Pallas kernels for 21% -> 20%
where the time goes in v5:
time: 59.1 us; the launch traced here: 58.9 us
  starting transfers between devices  22 us (37%)
  waiting for transfers between devices  19.7 us (33%)
  Pallas kernels  13.5 us (23%)
  local copies, waits for them, and re-layouts  2.84 us (5%)
  between operations  0.85 us (1%)
    ppermute x9, waiting for transfers between devices, shift(): return lax.ppermute(x, 'pb', to)  13.8 us
    pallas_call x18, Pallas kernels, call(): pl.pallas_call(body, out_shape=outs, in_specs=[vmem] * (len(arrays) - len...  13.5 us
    ppermute x9, starting transfers between devices, shift(): return lax.ppermute(x, 'pb', to)  13.4 us
    ppermute x6, starting transfers between devices, pass_on(): lax.ppermute(x, 'pa', [(i, (i + 2 * step) % members) for i in range(membe...  8.52 us
    ppermute x6, waiting for transfers between devices, pass_on(): lax.ppermute(x, 'pa', [(i, (i + 2 * step) % members) for i in range(membe...  4.58 us
    unnamed x16, local copies, waits for them, and re-layouts  2.84 us
    ppermute x2, waiting for transfers between devices, swap(): return lax.ppermute(x, 'pa', [(i, i ^ 1) for i in range(members)])  1.34 us
  transfers between devices with their start and end apart: 17, of which 9 were waited for; matrix products, arithmetic and copies ran while one was open for 0% of the time, Pallas kernels for 20%

profile of v5, /device:TPU:0, one launch (start us, length us, event | category | flops | bytes accessed | tf_op | source)
XLA Modules:
  0.0 58.9 jit_solution(1261013168957466365)
XLA Ops:
  0.6 1.0 %shard_map.105.refs_0_ = bf16[136,1024]{1,0:T(8,128)(2,1)S(1)} custom-call(s32[16,128]{1,0:T(8,128)} %bitcast.7, bf16[128,1024]{1,0:T(8,128)(2,1)} %refs_1_.4), custom_call_target="tpu_custom_call" | custom-call | bytes 548864 | tf_op jit(solution)/shard_map/pallas_call | solution.py:265
  1.6 3.1 %collective-permute-start.4 = (bf16[136,1024]{1,0:T(8,128)(2,1)S(1)}, bf16[136,1024]{1,0:T(8,128)(2,1)S(1)}, u32[]{:S(2)}, u32[]{:S(2)}) collective-permute-start(bf16[136,1024]{1,0:T(8,128)(2,1)S(1)} %shard_map.105.refs_0_), channel_id=1, source_target_pairs={{0,1},{1,3},{3,2},{2,0},{4,5},{5,7},{7,6},{6,4},{8,9},{9,11},{11,1... | collective-permute-start | bytes 835592 | tf_op jit(solution)/shard_map/ppermute | solution.py:296
  4.8 1.6 %copy-done = bf16[1024,1024]{1,0:T(8,128)(2,1)S(1)} copy-done((bf16[1024,1024]{1,0:T(8,128)(2,1)S(1)}, bf16[1024,1024]{1,0:T(8,128)(2,1)}, u32[]{:S(2)}) %copy-start) | copy-done | bytes 2097176
  6.3 1.2 %copy-done.7 = bf16[512,1024]{1,0:T(8,128)(2,1)S(1)} copy-done((bf16[512,1024]{1,0:T(8,128)(2,1)S(1)}, bf16[512,1024]{1,0:T(8,128)(2,1)}, u32[]{:S(2)}) %copy-start.7) | copy-done | bytes 1048600
  7.6 2.8 %shard_map.106 = (bf16[512,1024]{1,0:T(8,128)(2,1)S(1)}, bf16[128,1024]{1,0:T(8,128)(2,1)S(1)}, f32[2,128]{1,0:T(2,128)S(1)}, f32[512,128]{1,0:T(8,128)S(1)}, bf16[128,1024]{1,0:T(8,128)(2,1)S(1)}) custom-call(bf16[136,1024]{1,0:T(8,128)(2,1)S(1)} %shard_map.105.refs_0_, bf16[512,1024]{1,0:T(8,128)(2,1)S(1)} %copy-done.7, bf16[1024,1024]{1,0:T(8,128)(2,1)S(1)} %copy-done), custom_call_target="tpu_custom_call" | custom-call | flops 1610612736 | bytes 5260288 | tf_op jit(solution)/shard_map/pallas_call | solution.py:265
  10.4 2.0 %collective-permute-done.4.refs_1_ = bf16[136,1024]{1,0:T(8,128)(2,1)S(1)} collective-permute-done((bf16[136,1024]{1,0:T(8,128)(2,1)S(1)}, bf16[136,1024]{1,0:T(8,128)(2,1)S(1)}, u32[]{:S(2)}, u32[]{:S(2)}) %collective-permute-start.4) | collective-permute-done | bytes 278560 | tf_op jit(solution)/shard_map/ppermute | solution.py:296
  12.4 0.8 %collective-permute-start.5 = (bf16[136,1024]{1,0:T(8,128)(2,1)S(1)}, bf16[136,1024]{1,0:T(8,128)(2,1)S(1)}, u32[]{:S(2)}, u32[]{:S(2)}) collective-permute-start(bf16[136,1024]{1,0:T(8,128)(2,1)S(1)} %collective-permute-done.4.refs_1_), channel_id=1, source_target_pairs={{0,1},{1,3},{3,2},{2,0},{4,5},{5,7},{7,6},{6,4},{8,9},{9,11},{11,1... | collective-permute-start | bytes 835592 | tf_op jit(solution)/shard_map/ppermute | solution.py:296
  13.3 0.6 shard_map.107
  13.8 7.3 %collective-permute-done.5.refs_1_ = bf16[136,1024]{1,0:T(8,128)(2,1)S(1)} collective-permute-done((bf16[136,1024]{1,0:T(8,128)(2,1)S(1)}, bf16[136,1024]{1,0:T(8,128)(2,1)S(1)}, u32[]{:S(2)}, u32[]{:S(2)}) %collective-permute-start.5) | collective-permute-done | bytes 278560 | tf_op jit(solution)/shard_map/ppermute | solution.py:296
  21.1 1.0 %collective-permute-start.6 = (bf16[136,1024]{1,0:T(8,128)(2,1)S(1)}, bf16[136,1024]{1,0:T(8,128)(2,1)S(1)}, u32[]{:S(2)}, u32[]{:S(2)}) collective-permute-start(bf16[136,1024]{1,0:T(8,128)(2,1)S(1)} %collective-permute-done.5.refs_1_), channel_id=1, source_target_pairs={{0,1},{1,3},{3,2},{2,0},{4,5},{5,7},{7,6},{6,4},{8,9},{9,11},{11,1... | collective-permute-start | bytes 835592 | tf_op jit(solution)/shard_map/ppermute | solution.py:296
  22.1 0.6 shard_map.108
  23.0 3.0 %collective-permute-start.15 = (bf16[136,1024]{1,0:T(8,128)(2,1)S(1)}, bf16[136,1024]{1,0:T(8,128)(2,1)S(1)}, u32[]{:S(2)}, u32[]{:S(2)}) collective-permute-start(bf16[136,1024]{1,0:T(8,128)(2,1)S(1)} %shard_map.117), channel_id=1, source_target_pairs={{0,1},{1,3},{3,2},{2,0},{4,5},{5,7},{7,6},{6,4},{8,9},{9,11},{11,1... | collective-permute-start | bytes 835592 | tf_op jit(solution)/shard_map/ppermute | solution.py:296
  26.0 2.4 %collective-permute-start.3 = (bf16[2,16,1024]{2,1,0:T(8,128)(2,1)S(1)}, bf16[2,16,1024]{2,1,0:T(8,128)(2,1)S(1)}, u32[]{:S(2)}, u32[]{:S(2)}) collective-permute-start(bf16[2,16,1024]{2,1,0:T(8,128)(2,1)S(1)} %shard_map.103.refs_4_), channel_id=1, source_target_pairs={{0,24},{4,28},{8,0},{12,4},{16,8},{20,12},{24,16},{28,20},{1,25},{... | collective-permute-start | bytes 196616 | tf_op jit(solution)/shard_map/ppermute | solution.py:305
  29.0 0.6 %collective-permute-start.1 = (bf16[2,16,1024]{2,1,0:T(8,128)(2,1)S(1)}, bf16[2,16,1024]{2,1,0:T(8,128)(2,1)S(1)}, u32[]{:S(2)}, u32[]{:S(2)}) collective-permute-start(bf16[2,16,1024]{2,1,0:T(8,128)(2,1)S(1)} %shard_map.103.refs_4_), channel_id=1, source_target_pairs={{0,8},{4,12},{8,16},{12,20},{16,24},{20,28},{24,0},{28,4},{1,9},{5... | collective-permute-start | bytes 196616 | tf_op jit(solution)/shard_map/ppermute | solution.py:305
  29.6 1.4 %collective-permute-done.3.refs_7_ = bf16[2,16,1024]{2,1,0:T(8,128)(2,1)S(1)} collective-permute-done((bf16[2,16,1024]{2,1,0:T(8,128)(2,1)S(1)}, bf16[2,16,1024]{2,1,0:T(8,128)(2,1)S(1)}, u32[]{:S(2)}, u32[]{:S(2)}) %collective-permute-start.3) | collective-permute-done | bytes 65568 | tf_op jit(solution)/shard_map/ppermute | solution.py:305
  31.0 1.8 %collective-permute-done.2.refs_6_ = bf16[2,16,1024]{2,1,0:T(8,128)(2,1)S(1)} collective-permute-done((bf16[2,16,1024]{2,1,0:T(8,128)(2,1)S(1)}, bf16[2,16,1024]{2,1,0:T(8,128)(2,1)S(1)}, u32[]{:S(2)}, u32[]{:S(2)}) %collective-permute-start.2) | collective-permute-done | bytes 65568 | tf_op jit(solution)/shard_map/ppermute | solution.py:305
  32.8 1.4 %collective-permute-done.1.refs_5_ = bf16[2,16,1024]{2,1,0:T(8,128)(2,1)S(1)} collective-permute-done((bf16[2,16,1024]{2,1,0:T(8,128)(2,1)S(1)}, bf16[2,16,1024]{2,1,0:T(8,128)(2,1)S(1)}, u32[]{:S(2)}, u32[]{:S(2)}) %collective-permute-start.1) | collective-permute-done | bytes 65568 | tf_op jit(solution)/shard_map/ppermute | solution.py:305
  34.2 1.0 %shard_map.104 = (bf16[128,1024]{1,0:T(8,128)(2,1)S(1)}, f32[128,128]{1,0:T(8,128)S(1)}, f32[128,128]{1,0:T(8,128)S(1)}, f32[2,128]{1,0:T(2,128)S(1)}) custom-call(bf16[128,1024]{1,0:T(8,128)(2,1)S(1)} %copy-done.2, bf16[1024,1024]{1,0:T(8,128)(2,1)S(1)} %copy-done.1, s32[1,128]{1,0:T(1,128)S(1)} %bitcast.5, s32[64,64]{1,0:T(8,128)S(1)} %copy-done.3, ...), custom_call_target="tpu_custom_call" | custom-call | flops 301989888 | bytes 3032576 | tf_op jit(solution)/shard_map/pallas_call | solution.py:265
  35.5 0.8 %shard_map.109.refs_2_.refs_9_ = bf16[128,1024]{1,0:T(8,128)(2,1)S(1)} custom-call(bf16[1024,1024]{1,0:T(8,128)(2,1)S(1)} %copy-done.1, bf16[136,1024]{1,0:T(8,128)(2,1)S(1)} %collective-permute-done.4.refs_1_, f32[2,128]{1,0:T(2,128)S(1)} %get-tuple-element.38.refs_2_.refs_1_), custom_call_target="tpu_custom_call" | custom-call | flops 268435456 | bytes 2637824 | tf_op jit(solution)/shard_map/pallas_call | solution.py:265
  36.4 0.8 %shard_map.110.refs_3_.refs_10_ = bf16[128,1024]{1,0:T(8,128)(2,1)S(1)} custom-call(bf16[1024,1024]{1,0:T(8,128)(2,1)S(1)} %copy-done.1, bf16[136,1024]{1,0:T(8,128)(2,1)S(1)} %collective-permute-done.5.refs_1_, f32[2,128]{1,0:T(2,128)S(1)} %get-tuple-element.40.refs_2_.refs_1_), custom_call_target="tpu_custom_call" | custom-call | flops 268435456 | bytes 2637824 | tf_op jit(solution)/shard_map/pallas_call | solution.py:265
  37.2 0.6 shard_map.111
  38.2 2.1 %collective-permute-start.16 = (bf16[128,1024]{1,0:T(8,128)(2,1)S(1)}, bf16[128,1024]{1,0:T(8,128)(2,1)S(1)}, u32[]{:S(2)}, u32[]{:S(2)}) collective-permute-start(bf16[128,1024]{1,0:T(8,128)(2,1)S(1)} %shard_map.118), channel_id=1, source_target_pairs={{0,1},{1,3},{3,2},{2,0},{4,5},{5,7},{7,6},{6,4},{8,9},{9,11},{11,1... | collective-permute-start | bytes 786440 | tf_op jit(solution)/shard_map/ppermute | solution.py:296
  40.3 0.9 %collective-permute-start.9 = (f32[10,128]{1,0:T(8,128)S(1)}, f32[10,128]{1,0:T(8,128)S(1)}, u32[]{:S(2)}, u32[]{:S(2)}) collective-permute-start(f32[10,128]{1,0:T(8,128)S(1)} %shard_map.112.refs_2_.refs_6_.refs_0_), channel_id=1, source_target_pairs={{0,2},{1,0},{3,1},{2,3},{4,6},{5,4},{7,5},{6,7},{8,10},{9,8},{11,9... | collective-permute-start | bytes 15368 | tf_op jit(solution)/shard_map/ppermute | solution.py:296
  41.2 2.4 %collective-permute-start.8 = (f32[10,128]{1,0:T(8,128)S(1)}, f32[10,128]{1,0:T(8,128)S(1)}, u32[]{:S(2)}, u32[]{:S(2)}) collective-permute-start(f32[10,128]{1,0:T(8,128)S(1)} %shard_map.112.refs_2_.refs_6_.refs_0_), channel_id=1, source_target_pairs={{0,3},{1,2},{3,0},{2,1},{4,7},{5,6},{7,4},{6,5},{8,11},{9,10},{11,... | collective-permute-start | bytes 15368 | tf_op jit(solution)/shard_map/ppermute | solution.py:296
  43.6 0.8 %shard_map.113.refs_10_.refs_11_ = bf16[128,1024]{1,0:T(8,128)(2,1)S(1)} custom-call(bf16[1024,1024]{1,0:T(8,128)(2,1)S(1)} %copy-done.1, bf16[136,1024]{1,0:T(8,128)(2,1)S(1)} %collective-permute-done.6.refs_1_, f32[10,128]{1,0:T(8,128)S(1)} %shard_map.112.refs_2_.refs_6_.refs_0_), custom_call_target="tpu_custom_call" | custom-call | flops 268435456 | bytes 2637824 | tf_op jit(solution)/shard_map/pallas_call | solution.py:265
  44.4 2.8 %collective-permute-done.9.refs_9_.refs_3_ = f32[10,128]{1,0:T(8,128)S(1)} collective-permute-done((f32[10,128]{1,0:T(8,128)S(1)}, f32[10,128]{1,0:T(8,128)S(1)}, u32[]{:S(2)}, u32[]{:S(2)}) %collective-permute-start.9) | collective-permute-done | bytes 5152 | tf_op jit(solution)/shard_map/ppermute | solution.py:296
  47.2 1.5 %collective-permute-done.8.refs_8_.refs_2_ = f32[10,128]{1,0:T(8,128)S(1)} collective-permute-done((f32[10,128]{1,0:T(8,128)S(1)}, f32[10,128]{1,0:T(8,128)S(1)}, u32[]{:S(2)}, u32[]{:S(2)}) %collective-permute-start.8) | collective-permute-done | bytes 5152 | tf_op jit(solution)/shard_map/ppermute | solution.py:296
  49.3 1.3 %collective-permute-done.10 = bf16[64,1024]{1,0:T(8,128)(2,1)S(1)} collective-permute-done((bf16[64,1024]{1,0:T(8,128)(2,1)S(1)}, bf16[64,1024]{1,0:T(8,128)(2,1)S(1)}, u32[]{:S(2)}, u32[]{:S(2)}) %collective-permute-start.10) | collective-permute-done | bytes 131104 | tf_op jit(solution)/shard_map/ppermute | solution.py:302
  51.1 2.8 %collective-permute-start.12 = (bf16[16,1024]{1,0:T(8,128)(2,1)S(1)}, bf16[16,1024]{1,0:T(8,128)(2,1)S(1)}, u32[]{:S(2)}, u32[]{:S(2)}) collective-permute-start(bf16[16,1024]{1,0:T(8,128)(2,1)S(1)} %get-tuple-element.50), channel_id=1, source_target_pairs={{0,16},{4,20},{8,24},{12,28},{16,0},{20,4},{24,8},{28,12},{1,17},{... | collective-permute-start | bytes 98312 | tf_op jit(solution)/shard_map/ppermute | solution.py:305
  54.0 1.7 %collective-permute-start.13 = (bf16[16,1024]{1,0:T(8,128)(2,1)S(1)}, bf16[16,1024]{1,0:T(8,128)(2,1)S(1)}, u32[]{:S(2)}, u32[]{:S(2)}) collective-permute-start(bf16[16,1024]{1,0:T(8,128)(2,1)S(1)} %get-tuple-element.51), channel_id=1, source_target_pairs={{0,24},{4,28},{8,0},{12,4},{16,8},{20,12},{24,16},{28,20},{1,25},{... | collective-permute-start | bytes 98312 | tf_op jit(solution)/shard_map/ppermute | solution.py:305
  55.7 2.2 %shard_map.120 = bf16[512,1024]{1,0:T(8,128)(2,1)} custom-call(f32[10,128]{1,0:T(8,128)S(1)} %shard_map.112.refs_2_.refs_6_.refs_0_, f32[10,128]{1,0:T(8,128)S(1)} %collective-permute-done.7.refs_7_.refs_1_, f32[10,128]{1,0:T(8,128)S(1)} %collective-permute-done.8.refs_8_.refs_2_, f32[10,128]{1,0:T(8,128)S(1)} %collective-permute-done.9.refs_9_.refs_3_, ...), custom_call_target="tpu_custom_call" | custom-call | flops 536870912 | bytes 3166208 | tf_op jit(solution)/shard_map/pallas_call | solution.py:265
  58.0 0.9 %shard_map.119 = (bf16[128,1024]{1,0:T(8,128)(2,1)}, bf16[16,1024]{1,0:T(8,128)(2,1)}) custom-call(f32[128,1024]{1,0:T(8,128)S(1)} %get-tuple-element.44.refs_0_, f32[128,128]{1,0:T(8,128)S(1)} %get-tuple-element.45.refs_1_, f32[16,1024]{1,0:T(8,128)S(1)} %get-tuple-element.48.refs_2_, bf16[16,1024]{1,0:T(8,128)(2,1)S(1)} %collective-permute-done.11.refs_3_, ...), custom_call_target="tpu_custom_call" | custom-call | flops 2097152 | bytes 1572864 | tf_op jit(solution)/shard_map/pallas_call | solution.py:265
  (36 shorter events, 2.7 us)
Async XLA Ops:
  0.6 9.7 %copy-start.4 = (bf16[16,1024]{1,0:T(8,128)(2,1)S(1)}, bf16[16,1024]{1,0:T(8,128)(2,1)}, u32[]{:S(2)}) copy-start(bf16[16,1024]{1,0:T(8,128)(2,1)} %refs_0_.5) | copy-start | bytes 98308
  1.6 10.8 %collective-permute-start.4 = (bf16[136,1024]{1,0:T(8,128)(2,1)S(1)}, bf16[136,1024]{1,0:T(8,128)(2,1)S(1)}, u32[]{:S(2)}, u32[]{:S(2)}) collective-permute-start(bf16[136,1024]{1,0:T(8,128)(2,1)S(1)} %shard_map.105.refs_0_), channel_id=1, source_target_pairs={{0,1},{1,3},{3,2},{2,0},{4,5},{5,7},{7,6},{6,4},{8,9},{9,11},{11,1... | collective-permute-start | bytes 835592 | tf_op jit(solution)/shard_map/ppermute | solution.py:296
  4.7 5.6 %collective-permute-start = (bf16[16,1024]{1,0:T(8,128)(2,1)}, bf16[16,1024]{1,0:T(8,128)(2,1)S(1)}, u32[]{:S(2)}, u32[]{:S(2)}) collective-permute-start(bf16[16,1024]{1,0:T(8,128)(2,1)} %refs_0_.5), channel_id=1, source_target_pairs={{0,4},{4,0},{8,12},{12,8},{16,20},{20,16},{24,28},{28,24},{1,5},{5... | collective-permute-start | bytes 98312 | tf_op jit(solution)/shard_map/ppermute | solution.py:302
  4.7 1.6 %copy-start = (bf16[1024,1024]{1,0:T(8,128)(2,1)S(1)}, bf16[1024,1024]{1,0:T(8,128)(2,1)}, u32[]{:S(2)}) copy-start(bf16[1024,1024]{1,0:T(8,128)(2,1)} %refs_0_.9) | copy-start | bytes 6291460
  6.3 1.2 %copy-start.7 = (bf16[512,1024]{1,0:T(8,128)(2,1)S(1)}, bf16[512,1024]{1,0:T(8,128)(2,1)}, u32[]{:S(2)}) copy-start(bf16[512,1024]{1,0:T(8,128)(2,1)} %refs_1_.5) | copy-start | bytes 3145732
  12.4 8.7 %collective-permute-start.5 = (bf16[136,1024]{1,0:T(8,128)(2,1)S(1)}, bf16[136,1024]{1,0:T(8,128)(2,1)S(1)}, u32[]{:S(2)}, u32[]{:S(2)}) collective-permute-start(bf16[136,1024]{1,0:T(8,128)(2,1)S(1)} %collective-permute-done.4.refs_1_), channel_id=1, source_target_pairs={{0,1},{1,3},{3,2},{2,0},{4,5},{5,7},{7,6},{6,4},{8,9},{9,11},{11,1... | collective-permute-start | bytes 835592 | tf_op jit(solution)/shard_map/ppermute | solution.py:296
  13.2 20.9 %copy-start.1 = (bf16[1024,1024]{1,0:T(8,128)(2,1)S(1)}, bf16[1024,1024]{1,0:T(8,128)(2,1)}, u32[]{:S(2)}) copy-start(bf16[1024,1024]{1,0:T(8,128)(2,1)} %refs_0_.9) | copy-start | bytes 6291460
  13.3 20.9 %copy-start.2 = (bf16[128,1024]{1,0:T(8,128)(2,1)S(1)}, bf16[128,1024]{1,0:T(8,128)(2,1)}, u32[]{:S(2)}) copy-start(bf16[128,1024]{1,0:T(8,128)(2,1)} %refs_1_.4) | copy-start | bytes 786436
  13.3 20.9 %copy-start.3 = (s32[64,64]{1,0:T(8,128)S(1)}, s32[64,64]{1,0:T(8,128)}, u32[]{:S(2)}) copy-start(s32[64,64]{1,0:T(8,128)} %refs_3_.1) | copy-start | bytes 49156
  13.3 20.9 %copy-start.5 = (s32[128]{0:T(128)S(1)}, s32[128]{0:T(128)}, u32[]{:S(2)}) copy-start(s32[128]{0:T(128)} %param.13) | copy-start | bytes 1540
  21.1 16.0 %collective-permute-start.6 = (bf16[136,1024]{1,0:T(8,128)(2,1)S(1)}, bf16[136,1024]{1,0:T(8,128)(2,1)S(1)}, u32[]{:S(2)}, u32[]{:S(2)}) collective-permute-start(bf16[136,1024]{1,0:T(8,128)(2,1)S(1)} %collective-permute-done.5.refs_1_), channel_id=1, source_target_pairs={{0,1},{1,3},{3,2},{2,0},{4,5},{5,7},{7,6},{6,4},{8,9},{9,11},{11,1... | collective-permute-start | bytes 835592 | tf_op jit(solution)/shard_map/ppermute | solution.py:296
  23.0 14.8 %collective-permute-start.15 = (bf16[136,1024]{1,0:T(8,128)(2,1)S(1)}, bf16[136,1024]{1,0:T(8,128)(2,1)S(1)}, u32[]{:S(2)}, u32[]{:S(2)}) collective-permute-start(bf16[136,1024]{1,0:T(8,128)(2,1)S(1)} %shard_map.117), channel_id=1, source_target_pairs={{0,1},{1,3},{3,2},{2,0},{4,5},{5,7},{7,6},{6,4},{8,9},{9,11},{11,1... | collective-permute-start | bytes 835592 | tf_op jit(solution)/shard_map/ppermute | solution.py:296
  26.0 4.9 %collective-permute-start.3 = (bf16[2,16,1024]{2,1,0:T(8,128)(2,1)S(1)}, bf16[2,16,1024]{2,1,0:T(8,128)(2,1)S(1)}, u32[]{:S(2)}, u32[]{:S(2)}) collective-permute-start(bf16[2,16,1024]{2,1,0:T(8,128)(2,1)S(1)} %shard_map.103.refs_4_), channel_id=1, source_target_pairs={{0,24},{4,28},{8,0},{12,4},{16,8},{20,12},{24,16},{28,20},{1,25},{... | collective-permute-start | bytes 196616 | tf_op jit(solution)/shard_map/ppermute | solution.py:305
  28.5 4.3 %collective-permute-start.2 = (bf16[2,16,1024]{2,1,0:T(8,128)(2,1)S(1)}, bf16[2,16,1024]{2,1,0:T(8,128)(2,1)S(1)}, u32[]{:S(2)}, u32[]{:S(2)}) collective-permute-start(bf16[2,16,1024]{2,1,0:T(8,128)(2,1)S(1)} %shard_map.103.refs_4_), channel_id=1, source_target_pairs={{0,16},{4,20},{8,24},{12,28},{16,0},{20,4},{24,8},{28,12},{1,17},{... | collective-permute-start | bytes 196616 | tf_op jit(solution)/shard_map/ppermute | solution.py:305
  29.0 5.2 %collective-permute-start.1 = (bf16[2,16,1024]{2,1,0:T(8,128)(2,1)S(1)}, bf16[2,16,1024]{2,1,0:T(8,128)(2,1)S(1)}, u32[]{:S(2)}, u32[]{:S(2)}) collective-permute-start(bf16[2,16,1024]{2,1,0:T(8,128)(2,1)S(1)} %shard_map.103.refs_4_), channel_id=1, source_target_pairs={{0,8},{4,12},{8,16},{12,20},{16,24},{20,28},{24,0},{28,4},{1,9},{5... | collective-permute-start | bytes 196616 | tf_op jit(solution)/shard_map/ppermute | solution.py:305
  37.8 20.1 %collective-permute-start.14 = (bf16[128,1024]{1,0:T(8,128)(2,1)S(1)}, bf16[128,1024]{1,0:T(8,128)(2,1)S(1)}, u32[]{:S(2)}, u32[]{:S(2)}) collective-permute-start(bf16[128,1024]{1,0:T(8,128)(2,1)S(1)} %shard_map.116), channel_id=1, source_target_pairs={{0,2},{1,0},{3,1},{2,3},{4,6},{5,4},{7,5},{6,7},{8,10},{9,8},{11,9... | collective-permute-start | bytes 786440 | tf_op jit(solution)/shard_map/ppermute | solution.py:296
  37.9 11.0 %copy-start.6 = (s32[128]{0:T(128)S(1)}, s32[128]{0:T(128)}, u32[]{:S(2)}) copy-start(s32[128]{0:T(128)} %param.14) | copy-start | bytes 1540
  38.2 19.7 %collective-permute-start.16 = (bf16[128,1024]{1,0:T(8,128)(2,1)S(1)}, bf16[128,1024]{1,0:T(8,128)(2,1)S(1)}, u32[]{:S(2)}, u32[]{:S(2)}) collective-permute-start(bf16[128,1024]{1,0:T(8,128)(2,1)S(1)} %shard_map.118), channel_id=1, source_target_pairs={{0,1},{1,3},{3,2},{2,0},{4,5},{5,7},{7,6},{6,4},{8,9},{9,11},{11,1... | collective-permute-start | bytes 786440 | tf_op jit(solution)/shard_map/ppermute | solution.py:296
  40.3 6.9 %collective-permute-start.9 = (f32[10,128]{1,0:T(8,128)S(1)}, f32[10,128]{1,0:T(8,128)S(1)}, u32[]{:S(2)}, u32[]{:S(2)}) collective-permute-start(f32[10,128]{1,0:T(8,128)S(1)} %shard_map.112.refs_2_.refs_6_.refs_0_), channel_id=1, source_target_pairs={{0,2},{1,0},{3,1},{2,3},{4,6},{5,4},{7,5},{6,7},{8,10},{9,8},{11,9... | collective-permute-start | bytes 15368 | tf_op jit(solution)/shard_map/ppermute | solution.py:296
  41.2 7.5 %collective-permute-start.8 = (f32[10,128]{1,0:T(8,128)S(1)}, f32[10,128]{1,0:T(8,128)S(1)}, u32[]{:S(2)}, u32[]{:S(2)}) collective-permute-start(f32[10,128]{1,0:T(8,128)S(1)} %shard_map.112.refs_2_.refs_6_.refs_0_), channel_id=1, source_target_pairs={{0,3},{1,2},{3,0},{2,1},{4,7},{5,6},{7,4},{6,5},{8,11},{9,10},{11,... | collective-permute-start | bytes 15368 | tf_op jit(solution)/shard_map/ppermute | solution.py:296
  43.6 5.3 %collective-permute-start.7 = (f32[10,128]{1,0:T(8,128)S(1)}, f32[10,128]{1,0:T(8,128)S(1)}, u32[]{:S(2)}, u32[]{:S(2)}) collective-permute-start(f32[10,128]{1,0:T(8,128)S(1)} %shard_map.112.refs_2_.refs_6_.refs_0_), channel_id=1, source_target_pairs={{0,1},{1,3},{3,2},{2,0},{4,5},{5,7},{7,6},{6,4},{8,9},{9,11},{11,1... | collective-permute-start | bytes 15368 | tf_op jit(solution)/shard_map/ppermute | solution.py:296
  49.3 1.4 %collective-permute-start.10 = (bf16[64,1024]{1,0:T(8,128)(2,1)S(1)}, bf16[64,1024]{1,0:T(8,128)(2,1)S(1)}, u32[]{:S(2)}, u32[]{:S(2)}) collective-permute-start(bf16[64,1024]{1,0:T(8,128)(2,1)S(1)} %get-tuple-element.47), channel_id=1, source_target_pairs={{0,4},{4,0},{8,12},{12,8},{16,20},{20,16},{24,28},{28,24},{1,5},{5... | collective-permute-start | bytes 393224 | tf_op jit(solution)/shard_map/ppermute | solution.py:302
  50.7 7.2 %collective-permute-start.11 = (bf16[16,1024]{1,0:T(8,128)(2,1)S(1)}, bf16[16,1024]{1,0:T(8,128)(2,1)S(1)}, u32[]{:S(2)}, u32[]{:S(2)}) collective-permute-start(bf16[16,1024]{1,0:T(8,128)(2,1)S(1)} %get-tuple-element.49), channel_id=1, source_target_pairs={{0,8},{4,12},{8,16},{12,20},{16,24},{20,28},{24,0},{28,4},{1,9},{5... | collective-permute-start | bytes 98312 | tf_op jit(solution)/shard_map/ppermute | solution.py:305
  51.1 6.8 %collective-permute-start.12 = (bf16[16,1024]{1,0:T(8,128)(2,1)S(1)}, bf16[16,1024]{1,0:T(8,128)(2,1)S(1)}, u32[]{:S(2)}, u32[]{:S(2)}) collective-permute-start(bf16[16,1024]{1,0:T(8,128)(2,1)S(1)} %get-tuple-element.50), channel_id=1, source_target_pairs={{0,16},{4,20},{8,24},{12,28},{16,0},{20,4},{24,8},{28,12},{1,17},{... | collective-permute-start | bytes 98312 | tf_op jit(solution)/shard_map/ppermute | solution.py:305
  54.0 4.0 %collective-permute-start.13 = (bf16[16,1024]{1,0:T(8,128)(2,1)S(1)}, bf16[16,1024]{1,0:T(8,128)(2,1)S(1)}, u32[]{:S(2)}, u32[]{:S(2)}) collective-permute-start(bf16[16,1024]{1,0:T(8,128)(2,1)S(1)} %get-tuple-element.51), channel_id=1, source_target_pairs={{0,24},{4,28},{8,0},{12,4},{16,8},{20,12},{24,16},{28,20},{1,25},{... | collective-permute-start | bytes 98312 | tf_op jit(solution)/shard_map/ppermute | solution.py:305

commit v6 on v5

--- a/solution.py
+++ b/solution.py
@@ -28,16 +28,13 @@
     return lax.dot_general(a, b, (((0,), (0,)), ((), ())), preferred_element_type=F32)
 
 
-def pack_kernel(owners, pool_count, ids_hbm, query_ref, packed_ref, sem, ids_ref, ids_sem):
-    rows, depth = query_ref.shape
-    hard_count = ids_ref.shape[0]
+def tail_kernel(owners, pool_count, ids_hbm, tail_ref, ids_ref, ids_sem):
+    hard_count, rows = ids_ref.shape
     per = hard_count // owners
-    copy = pltpu.make_async_copy(query_ref, packed_ref.at[:rows, :], sem)
     ids_copy = pltpu.make_async_copy(ids_hbm, ids_ref, ids_sem)
     ids_copy.start()
-    copy.start()
+    tail_ref[...] = jnp.zeros(tail_ref.shape, BF16)
     ids_copy.wait()
-    packed_ref[rows:, :] = jnp.zeros((SUB, depth), BF16)
     for block in range(hard_count // SUB):
         lines = []
         for place in range(block * SUB, (block + 1) * SUB):
@@ -48,20 +45,26 @@
         high = jnp.right_shift(ids, LOW_BITS)
         low = ids - jnp.left_shift(high, LOW_BITS)
         start = 2 * block * rows
-        packed_ref[rows:, start : start + rows] = high.astype(F32).astype(BF16)
-        packed_ref[rows:, start + rows : start + 2 * rows] = low.astype(F32).astype(BF16)
-    copy.wait()
-
-
-def local_ids(packed_ref, me, rows, owners, per):
+        tail_ref[:, start : start + rows] = high.astype(F32).astype(BF16)
+        tail_ref[:, start + rows : start + 2 * rows] = low.astype(F32).astype(BF16)
+
+
+def pack_kernel(query_ref, tail_ref, packed_ref):
+    rows = query_ref.shape[0]
+    packed_ref[:rows, :] = query_ref[...]
+    packed_ref[rows:, :] = tail_ref[...]
+
+
+def local_ids(tail_ref, me, rows, owners, per):
+    base = tail_ref.shape[0] - SUB
     found = None
     for owner in range(owners):
         parts = []
         for j in range(per):
             block, sub = divmod(owner * per + j, SUB)
             start = 2 * block * rows
-            high = packed_ref[rows:, start : start + rows].astype(F32)
-            low = packed_ref[rows:, start + rows : start + 2 * rows].astype(F32)
+            high = tail_ref[base:, start : start + rows].astype(F32)
+            low = tail_ref[base:, start + rows : start + 2 * rows].astype(F32)
             ids = high * float(1 << LOW_BITS) + low
             parts.append(ids[sub : sub + 1, :])
         if found is None:
@@ -71,10 +74,10 @@
     return found
 
 
-def score_block(me, packed_ref, table_ref, rows, owners, per, scale):
+def score_block(me, query_ref, tail_ref, table_ref, rows, owners, per, scale):
     count = table_ref.shape[0]
-    ids = local_ids(packed_ref, me, rows, owners, per)
-    dense = nt(table_ref[...], packed_ref[:rows, :])
+    ids = local_ids(tail_ref, me, rows, owners, per)
+    dense = nt(table_ref[...], query_ref[:rows, :])
     row_iota = lax.broadcasted_iota(jnp.int32, (count, rows), 0).astype(F32)
     hits = [row_iota == one for one in ids]
     scores = [jnp.sum(jnp.where(hit, dense, 0.0), axis=0, keepdims=True) * scale for hit in hits]
@@ -86,13 +89,18 @@
     return weight, top, functools.reduce(jnp.add, powers)
 
 
-def own_kernel(owners, per, scale, packed_ref, hidden_ref, projection_ref, *outs):
-    table_ref, turned_ref, stat_ref, weight_ref, term_ref = outs
+def table_kernel(hidden_ref, projection_ref, table_ref):
+    table_ref[...] = nn(hidden_ref[...], projection_ref[...]).astype(BF16)
+
+
+def own_kernel(owners, per, scale, query_ref, tail_ref, table_ref, projection_ref, *outs):
+    turned_ref, stat_ref, weight_ref, term_ref = outs
     me = lax.axis_index("pb")
-    rows = packed_ref.shape[0] - SUB
-    table_ref[...] = nn(hidden_ref[...], projection_ref[...]).astype(BF16)
-    turned_ref[...] = nt(packed_ref[:rows, :], projection_ref[...]).astype(BF16)
-    weight, top, total = score_block(me, packed_ref, table_ref, rows, owners, per, scale)
+    rows = query_ref.shape[0]
+    turned_ref[...] = nt(query_ref[...], projection_ref[...]).astype(BF16)
+    weight, top, total = score_block(
+        me, query_ref, tail_ref, table_ref, rows, owners, per, scale
+    )
     stat_ref[0:1, :] = top
     stat_ref[1:2, :] = total
     weight_ref[...] = weight
@@ -102,7 +110,7 @@
 def score_kernel(owners, per, scale, table_ref, packed_ref, stat_ref, weight_ref):
     rows = packed_ref.shape[0] - SUB
     me = lax.axis_index("pb")
-    weight, top, total = score_block(me, packed_ref, table_ref, rows, owners, per, scale)
+    weight, top, total = score_block(me, packed_ref, packed_ref, table_ref, rows, owners, per, scale)
     stat_ref[0:1, :] = top
     stat_ref[1:2, :] = total
     weight_ref[...] = weight
@@ -304,27 +312,30 @@
     def pass_on(x, step):
         return lax.ppermute(x, "pa", [(i, (i + 2 * step) % members) for i in range(members)])
 
-    (packed,) = call(
-        functools.partial(pack_kernel, owners, pool_count),
-        [((rows + SUB, depth), BF16)],
+    first = shift(queries, 1)
+    (tail,) = call(
+        functools.partial(tail_kernel, owners, pool_count),
+        [((SUB, depth), BF16)],
         [],
-        in_place=[
-            pltpu.with_memory_space_constraint(hard_ids.T, pltpu.HBM),
-            pltpu.with_memory_space_constraint(queries, pltpu.HBM),
-        ],
-        scratch=[
-            pltpu.SemaphoreType.DMA,
-            pltpu.VMEM(hard_ids.shape[::-1], jnp.int32),
-            pltpu.SemaphoreType.DMA,
-        ],
-    )
-    block = shift(packed, 1)
+        in_place=[pltpu.with_memory_space_constraint(hard_ids.T, pltpu.HBM)],
+        scratch=[pltpu.VMEM(hard_ids.shape[::-1], jnp.int32), pltpu.SemaphoreType.DMA],
+    )
+    first_tail = shift(tail, 1)
+    (block,) = call(
+        pack_kernel, [((rows + SUB, depth), BF16)], [first, first_tail], flops=rows * depth
+    )
     other = swap(batch_hidden)
-    table, turned, own_stat, own_weight, own_term = call(
+    (table,) = call(
+        table_kernel,
+        [((pool_count, depth), BF16)],
+        [pool_hidden, projection],
+        flops=2 * depth * pool_count * depth,
+    )
+    turned, own_stat, own_weight, own_term = call(
         functools.partial(own_kernel, owners, per, scale),
-        [((pool_count, depth), BF16), term, ((2, rows), F32), weight, term],
-        [packed, pool_hidden, projection],
-        flops=2 * depth * (pool_count * depth + rows * depth + 2 * rows * pool_count),
+        [term, ((2, rows), F32), weight, term],
+        [queries, tail, table, projection],
+        flops=2 * depth * (rows * depth + 2 * rows * pool_count),
     )
     (chip,) = call(pair_kernel, [((2, size, depth), BF16)], [batch_hidden, other], flops=size * depth)
     chips = [chip] + [pass_on(chip, step) for step in range(1, pairs)]
@@ -342,7 +353,7 @@
     )
     stats, weights, terms, turned = [own_stat], [own_weight], [], [turned]
     direct = owners // 2 - 1
-    waits, chain = [own_stat, chip], None
+    waits, chain = [chip, table], None
     for slot in range(1, owners):
         last = slot + 1 == owners
         later = None if last else shift(hold(block, waits), 1)

time: 59.1 us -> 58.7 us (level)
  waiting for transfers between devices: 19.7 us -> 18.4 us
  starting transfers between devices: 22 us -> 22.8 us
    ppermute x9 -> x10, starting transfers between devices: 13.4 us -> 15.2 us  [shift(): return lax.ppermute(x, 'pb', to)]
    ppermute x6, waiting for transfers between devices: 4.58 us -> 3.06 us  [pass_on(): lax.ppermute(x, 'pa', [(i, (i + 2 * step) % members) for i in range(membe...]
    ppermute x6, starting transfers between devices: 8.52 us -> 7.54 us  [pass_on(): lax.ppermute(x, 'pa', [(i, (i + 2 * step) % members) for i in range(membe...]
    ppermute x9 -> x10, waiting for transfers between devices: 13.8 us -> 14 us  [shift(): return lax.ppermute(x, 'pb', to)]
    pallas_call x18 -> x20, Pallas kernels: 13.5 us -> 13.5 us  [call(): pl.pallas_call(body, out_shape=outs, in_specs=[vmem] * (len(arrays) - len...]
  transfers between devices with their start and end apart: 17 -> 18, of which waited for: 9 -> 9; matrix products, arithmetic and copies ran while one was open for 0% -> 0% of each run, Pallas kernels for 20% -> 21%
where the time goes in v6:
time: 58.7 us; the launch traced here: 58.4 us
  starting transfers between devices  22.8 us (39%)
  waiting for transfers between devices  18.4 us (31%)
  Pallas kernels  13.5 us (23%)
  local copies, waits for them, and re-layouts  2.85 us (5%)
  between operations  0.87 us (1%)
    ppermute x10, starting transfers between devices, shift(): return lax.ppermute(x, 'pb', to)  15.2 us
    ppermute x10, waiting for transfers between devices, shift(): return lax.ppermute(x, 'pb', to)  14 us
    pallas_call x20, Pallas kernels, call(): pl.pallas_call(body, out_shape=outs, in_specs=[vmem] * (len(arrays) - len...  13.5 us
    ppermute x6, starting transfers between devices, pass_on(): lax.ppermute(x, 'pa', [(i, (i + 2 * step) % members) for i in range(membe...  7.54 us
    ppermute x6, waiting for transfers between devices, pass_on(): lax.ppermute(x, 'pa', [(i, (i + 2 * step) % members) for i in range(membe...  3.06 us
    unnamed x16, local copies, waits for them, and re-layouts  2.85 us
    ppermute x2, waiting for transfers between devices, swap(): return lax.ppermute(x, 'pa', [(i, i ^ 1) for i in range(members)])  1.34 us
  transfers between devices with their start and end apart: 18, of which 9 were waited for; matrix products, arithmetic and copies ran while one was open for 0% of the time, Pallas kernels for 21%

profile of v6, /device:TPU:0, one launch (start us, length us, event | category | flops | bytes accessed | tf_op | source)
XLA Modules:
  0.0 58.4 jit_solution(4266633119841273731)
XLA Ops:
  0.6 3.1 %collective-permute-start.4 = (bf16[128,1024]{1,0:T(8,128)(2,1)}, bf16[128,1024]{1,0:T(8,128)(2,1)S(1)}, u32[]{:S(2)}, u32[]{:S(2)}) collective-permute-start(bf16[128,1024]{1,0:T(8,128)(2,1)} %refs_0_.10), channel_id=1, source_target_pairs={{0,1},{1,3},{3,2},{2,0},{4,5},{5,7},{7,6},{6,4},{8,9},{9,11},{11,1... | collective-permute-start | bytes 786440 | tf_op jit(solution)/shard_map/ppermute | solution.py:304
  3.7 0.7 %shard_map.105.refs_1_ = bf16[8,1024]{1,0:T(8,128)(2,1)S(1)} custom-call(s32[16,128]{1,0:T(8,128)} %bitcast.7), custom_call_target="tpu_custom_call" | custom-call | bytes 24576 | tf_op jit(solution)/shard_map/pallas_call | solution.py:273
  4.5 2.6 %collective-permute-start.5 = (bf16[8,1024]{1,0:T(8,128)(2,1)S(1)}, bf16[8,1024]{1,0:T(8,128)(2,1)S(1)}, u32[]{:S(2)}, u32[]{:S(2)}) collective-permute-start(bf16[8,1024]{1,0:T(8,128)(2,1)S(1)} %shard_map.105.refs_1_), channel_id=1, source_target_pairs={{0,1},{1,3},{3,2},{2,0},{4,5},{5,7},{7,6},{6,4},{8,9},{9,11},{11,1... | collective-permute-start | bytes 49160 | tf_op jit(solution)/shard_map/ppermute | solution.py:304
  7.1 1.6 %copy-done = bf16[1024,1024]{1,0:T(8,128)(2,1)S(1)} copy-done((bf16[1024,1024]{1,0:T(8,128)(2,1)S(1)}, bf16[1024,1024]{1,0:T(8,128)(2,1)}, u32[]{:S(2)}) %copy-start) | copy-done | bytes 2097176
  8.7 1.2 %copy-done.2 = bf16[512,1024]{1,0:T(8,128)(2,1)S(1)} copy-done((bf16[512,1024]{1,0:T(8,128)(2,1)S(1)}, bf16[512,1024]{1,0:T(8,128)(2,1)}, u32[]{:S(2)}) %copy-start.2) | copy-done | bytes 1048600
  9.9 1.2 %shard_map.106.refs_2_.refs_0_ = bf16[512,1024]{1,0:T(8,128)(2,1)S(1)} custom-call(bf16[512,1024]{1,0:T(8,128)(2,1)S(1)} %copy-done.2, bf16[1024,1024]{1,0:T(8,128)(2,1)S(1)} %copy-done), custom_call_target="tpu_custom_call" | custom-call | flops 1073741824 | bytes 4194304 | tf_op jit(solution)/shard_map/pallas_call | solution.py:273
  11.7 0.9 %collective-permute-start.6 = (bf16[136,1024]{1,0:T(8,128)(2,1)S(1)}, bf16[136,1024]{1,0:T(8,128)(2,1)S(1)}, u32[]{:S(2)}, u32[]{:S(2)}) collective-permute-start(bf16[136,1024]{1,0:T(8,128)(2,1)S(1)} %shard_map.108.refs_1_), channel_id=1, source_target_pairs={{0,1},{1,3},{3,2},{2,0},{4,5},{5,7},{7,6},{6,4},{8,9},{9,11},{11,1... | collective-permute-start | bytes 835592 | tf_op jit(solution)/shard_map/ppermute | solution.py:304
  12.6 0.6 shard_map.109
  13.1 8.2 %collective-permute-done.6.refs_1_ = bf16[136,1024]{1,0:T(8,128)(2,1)S(1)} collective-permute-done((bf16[136,1024]{1,0:T(8,128)(2,1)S(1)}, bf16[136,1024]{1,0:T(8,128)(2,1)S(1)}, u32[]{:S(2)}, u32[]{:S(2)}) %collective-permute-start.6) | collective-permute-done | bytes 278560 | tf_op jit(solution)/shard_map/ppermute | solution.py:304
  21.3 0.6 shard_map.110
  22.3 3.1 %collective-permute-start.16 = (bf16[136,1024]{1,0:T(8,128)(2,1)S(1)}, bf16[136,1024]{1,0:T(8,128)(2,1)S(1)}, u32[]{:S(2)}, u32[]{:S(2)}) collective-permute-start(bf16[136,1024]{1,0:T(8,128)(2,1)S(1)} %shard_map.119), channel_id=1, source_target_pairs={{0,1},{1,3},{3,2},{2,0},{4,5},{5,7},{7,6},{6,4},{8,9},{9,11},{11,1... | collective-permute-start | bytes 835592 | tf_op jit(solution)/shard_map/ppermute | solution.py:304
  25.4 2.4 %collective-permute-start.3 = (bf16[2,16,1024]{2,1,0:T(8,128)(2,1)S(1)}, bf16[2,16,1024]{2,1,0:T(8,128)(2,1)S(1)}, u32[]{:S(2)}, u32[]{:S(2)}) collective-permute-start(bf16[2,16,1024]{2,1,0:T(8,128)(2,1)S(1)} %shard_map.103.refs_4_), channel_id=1, source_target_pairs={{0,24},{4,28},{8,0},{12,4},{16,8},{20,12},{24,16},{28,20},{1,25},{... | collective-permute-start | bytes 196616 | tf_op jit(solution)/shard_map/ppermute | solution.py:313
  28.3 0.6 %collective-permute-start.1 = (bf16[2,16,1024]{2,1,0:T(8,128)(2,1)S(1)}, bf16[2,16,1024]{2,1,0:T(8,128)(2,1)S(1)}, u32[]{:S(2)}, u32[]{:S(2)}) collective-permute-start(bf16[2,16,1024]{2,1,0:T(8,128)(2,1)S(1)} %shard_map.103.refs_4_), channel_id=1, source_target_pairs={{0,8},{4,12},{8,16},{12,20},{16,24},{20,28},{24,0},{28,4},{1,9},{5... | collective-permute-start | bytes 196616 | tf_op jit(solution)/shard_map/ppermute | solution.py:313
  28.9 1.7 %shard_map.107 = (bf16[128,1024]{1,0:T(8,128)(2,1)S(1)}, f32[2,128]{1,0:T(2,128)S(1)}, f32[512,128]{1,0:T(8,128)S(1)}, bf16[128,1024]{1,0:T(8,128)(2,1)S(1)}) custom-call(bf16[128,1024]{1,0:T(8,128)(2,1)S(1)} %copy-done.3, bf16[8,1024]{1,0:T(8,128)(2,1)S(1)} %shard_map.105.refs_1_, bf16[512,1024]{1,0:T(8,128)(2,1)S(1)} %shard_map.106.refs_2_.refs_0_, ...), custom_call_target="tpu_custom_call" | custom-call | flops 536870912 | bytes 4211712 | tf_op jit(solution)/shard_map/pallas_call | solution.py:273
  30.7 1.4 %collective-permute-done.2.refs_6_ = bf16[2,16,1024]{2,1,0:T(8,128)(2,1)S(1)} collective-permute-done((bf16[2,16,1024]{2,1,0:T(8,128)(2,1)S(1)}, bf16[2,16,1024]{2,1,0:T(8,128)(2,1)S(1)}, u32[]{:S(2)}, u32[]{:S(2)}) %collective-permute-start.2) | collective-permute-done | bytes 65568 | tf_op jit(solution)/shard_map/ppermute | solution.py:313
  32.1 1.4 %collective-permute-done.1.refs_5_ = bf16[2,16,1024]{2,1,0:T(8,128)(2,1)S(1)} collective-permute-done((bf16[2,16,1024]{2,1,0:T(8,128)(2,1)S(1)}, bf16[2,16,1024]{2,1,0:T(8,128)(2,1)S(1)}, u32[]{:S(2)}, u32[]{:S(2)}) %collective-permute-start.1) | collective-permute-done | bytes 65568 | tf_op jit(solution)/shard_map/ppermute | solution.py:313
  33.5 1.0 %shard_map.104 = (bf16[128,1024]{1,0:T(8,128)(2,1)S(1)}, f32[128,128]{1,0:T(8,128)S(1)}, f32[128,128]{1,0:T(8,128)S(1)}, f32[2,128]{1,0:T(2,128)S(1)}) custom-call(bf16[128,1024]{1,0:T(8,128)(2,1)S(1)} %copy-done.3, bf16[1024,1024]{1,0:T(8,128)(2,1)S(1)} %copy-done.1, s32[1,128]{1,0:T(1,128)S(1)} %bitcast.5, s32[64,64]{1,0:T(8,128)S(1)} %copy-done.4, ...), custom_call_target="tpu_custom_call" | custom-call | flops 301989888 | bytes 3032576 | tf_op jit(solution)/shard_map/pallas_call | solution.py:273
  34.9 0.8 %shard_map.111.refs_2_.refs_9_ = bf16[128,1024]{1,0:T(8,128)(2,1)S(1)} custom-call(bf16[1024,1024]{1,0:T(8,128)(2,1)S(1)} %copy-done.1, bf16[136,1024]{1,0:T(8,128)(2,1)S(1)} %shard_map.108.refs_1_, f32[2,128]{1,0:T(2,128)S(1)} %get-tuple-element.36.refs_2_.refs_1_), custom_call_target="tpu_custom_call" | custom-call | flops 268435456 | bytes 2637824 | tf_op jit(solution)/shard_map/pallas_call | solution.py:273
  35.7 0.8 %shard_map.112.refs_3_.refs_10_ = bf16[128,1024]{1,0:T(8,128)(2,1)S(1)} custom-call(bf16[1024,1024]{1,0:T(8,128)(2,1)S(1)} %copy-done.1, bf16[136,1024]{1,0:T(8,128)(2,1)S(1)} %collective-permute-done.6.refs_1_, f32[2,128]{1,0:T(2,128)S(1)} %get-tuple-element.38.refs_2_.refs_1_), custom_call_target="tpu_custom_call" | custom-call | flops 268435456 | bytes 2637824 | tf_op jit(solution)/shard_map/pallas_call | solution.py:273
  36.5 0.6 %shard_map.113 = (f32[2,128]{1,0:T(2,128)S(1)}, f32[512,128]{1,0:T(8,128)S(1)}) custom-call(bf16[512,1024]{1,0:T(8,128)(2,1)S(1)} %shard_map.106.refs_2_.refs_0_, bf16[136,1024]{1,0:T(8,128)(2,1)S(1)} %collective-permute-done.7.refs_1_, bf16[128,1024]{1,0:T(8,128)(2,1)S(1)} %shard_map.111.refs_2_.refs_9_, bf16[128,1024]{1,0:T(8,128)(2,1)S(1)} %shard_map.112.refs_3_.refs_10_), custom_call_target="tpu_custom_call" | custom-call | flops 134217728 | bytes 1590272 | tf_op jit(solution)/shard_map/pallas_call | solution.py:273
  37.6 2.0 %collective-permute-start.17 = (bf16[128,1024]{1,0:T(8,128)(2,1)S(1)}, bf16[128,1024]{1,0:T(8,128)(2,1)S(1)}, u32[]{:S(2)}, u32[]{:S(2)}) collective-permute-start(bf16[128,1024]{1,0:T(8,128)(2,1)S(1)} %shard_map.120), channel_id=1, source_target_pairs={{0,1},{1,3},{3,2},{2,0},{4,5},{5,7},{7,6},{6,4},{8,9},{9,11},{11,1... | collective-permute-start | bytes 786440 | tf_op jit(solution)/shard_map/ppermute | solution.py:304
  39.6 0.9 %collective-permute-start.10 = (f32[10,128]{1,0:T(8,128)S(1)}, f32[10,128]{1,0:T(8,128)S(1)}, u32[]{:S(2)}, u32[]{:S(2)}) collective-permute-start(f32[10,128]{1,0:T(8,128)S(1)} %shard_map.114.refs_2_.refs_6_.refs_0_), channel_id=1, source_target_pairs={{0,2},{1,0},{3,1},{2,3},{4,6},{5,4},{7,5},{6,7},{8,10},{9,8},{11,9... | collective-permute-start | bytes 15368 | tf_op jit(solution)/shard_map/ppermute | solution.py:304
  40.6 2.4 %collective-permute-start.9 = (f32[10,128]{1,0:T(8,128)S(1)}, f32[10,128]{1,0:T(8,128)S(1)}, u32[]{:S(2)}, u32[]{:S(2)}) collective-permute-start(f32[10,128]{1,0:T(8,128)S(1)} %shard_map.114.refs_2_.refs_6_.refs_0_), channel_id=1, source_target_pairs={{0,3},{1,2},{3,0},{2,1},{4,7},{5,6},{7,4},{6,5},{8,11},{9,10},{11,... | collective-permute-start | bytes 15368 | tf_op jit(solution)/shard_map/ppermute | solution.py:304
  43.0 0.8 %shard_map.115.refs_10_.refs_11_ = bf16[128,1024]{1,0:T(8,128)(2,1)S(1)} custom-call(bf16[1024,1024]{1,0:T(8,128)(2,1)S(1)} %copy-done.1, bf16[136,1024]{1,0:T(8,128)(2,1)S(1)} %collective-permute-done.7.refs_1_, f32[10,128]{1,0:T(8,128)S(1)} %shard_map.114.refs_2_.refs_6_.refs_0_), custom_call_target="tpu_custom_call" | custom-call | flops 268435456 | bytes 2637824 | tf_op jit(solution)/shard_map/pallas_call | solution.py:273
  43.8 2.7 %collective-permute-done.10.refs_9_.refs_3_ = f32[10,128]{1,0:T(8,128)S(1)} collective-permute-done((f32[10,128]{1,0:T(8,128)S(1)}, f32[10,128]{1,0:T(8,128)S(1)}, u32[]{:S(2)}, u32[]{:S(2)}) %collective-permute-start.10) | collective-permute-done | bytes 5152 | tf_op jit(solution)/shard_map/ppermute | solution.py:304
  46.5 2.6 %collective-permute-done.9.refs_8_.refs_2_ = f32[10,128]{1,0:T(8,128)S(1)} collective-permute-done((f32[10,128]{1,0:T(8,128)S(1)}, f32[10,128]{1,0:T(8,128)S(1)}, u32[]{:S(2)}, u32[]{:S(2)}) %collective-permute-start.9) | collective-permute-done | bytes 5152 | tf_op jit(solution)/shard_map/ppermute | solution.py:304
  49.7 1.3 %collective-permute-done.11 = bf16[64,1024]{1,0:T(8,128)(2,1)S(1)} collective-permute-done((bf16[64,1024]{1,0:T(8,128)(2,1)S(1)}, bf16[64,1024]{1,0:T(8,128)(2,1)S(1)}, u32[]{:S(2)}, u32[]{:S(2)}) %collective-permute-start.11) | collective-permute-done | bytes 131104 | tf_op jit(solution)/shard_map/ppermute | solution.py:310
  51.0 0.5 collective-permute-start.12
  51.6 2.0 %collective-permute-start.13 = (bf16[16,1024]{1,0:T(8,128)(2,1)S(1)}, bf16[16,1024]{1,0:T(8,128)(2,1)S(1)}, u32[]{:S(2)}, u32[]{:S(2)}) collective-permute-start(bf16[16,1024]{1,0:T(8,128)(2,1)S(1)} %get-tuple-element.48), channel_id=1, source_target_pairs={{0,16},{4,20},{8,24},{12,28},{16,0},{20,4},{24,8},{28,12},{1,17},{... | collective-permute-start | bytes 98312 | tf_op jit(solution)/shard_map/ppermute | solution.py:313
  53.6 1.4 %collective-permute-start.14 = (bf16[16,1024]{1,0:T(8,128)(2,1)S(1)}, bf16[16,1024]{1,0:T(8,128)(2,1)S(1)}, u32[]{:S(2)}, u32[]{:S(2)}) collective-permute-start(bf16[16,1024]{1,0:T(8,128)(2,1)S(1)} %get-tuple-element.49), channel_id=1, source_target_pairs={{0,24},{4,28},{8,0},{12,4},{16,8},{20,12},{24,16},{28,20},{1,25},{... | collective-permute-start | bytes 98312 | tf_op jit(solution)/shard_map/ppermute | solution.py:313
  55.0 2.2 %shard_map.122 = bf16[512,1024]{1,0:T(8,128)(2,1)} custom-call(f32[10,128]{1,0:T(8,128)S(1)} %shard_map.114.refs_2_.refs_6_.refs_0_, f32[10,128]{1,0:T(8,128)S(1)} %collective-permute-done.8.refs_7_.refs_1_, f32[10,128]{1,0:T(8,128)S(1)} %collective-permute-done.9.refs_8_.refs_2_, f32[10,128]{1,0:T(8,128)S(1)} %collective-permute-done.10.refs_9_.refs_3_, ...), custom_call_target="tpu_custom_call" | custom-call | flops 536870912 | bytes 3166208 | tf_op jit(solution)/shard_map/pallas_call | solution.py:273
  57.5 0.9 %shard_map.121 = (bf16[128,1024]{1,0:T(8,128)(2,1)}, bf16[16,1024]{1,0:T(8,128)(2,1)}) custom-call(f32[128,1024]{1,0:T(8,128)S(1)} %get-tuple-element.42.refs_0_, f32[128,128]{1,0:T(8,128)S(1)} %get-tuple-element.43.refs_1_, f32[16,1024]{1,0:T(8,128)S(1)} %get-tuple-element.46.refs_2_, bf16[16,1024]{1,0:T(8,128)(2,1)S(1)} %collective-permute-done.12.refs_3_, ...), custom_call_target="tpu_custom_call" | custom-call | flops 2097152 | bytes 1572864 | tf_op jit(solution)/shard_map/pallas_call | solution.py:273
  (40 shorter events, 2.9 us)
Async XLA Ops:
  0.6 11.0 %collective-permute-start.4 = (bf16[128,1024]{1,0:T(8,128)(2,1)}, bf16[128,1024]{1,0:T(8,128)(2,1)S(1)}, u32[]{:S(2)}, u32[]{:S(2)}) collective-permute-start(bf16[128,1024]{1,0:T(8,128)(2,1)} %refs_0_.10), channel_id=1, source_target_pairs={{0,1},{1,3},{3,2},{2,0},{4,5},{5,7},{7,6},{6,4},{8,9},{9,11},{11,1... | collective-permute-start | bytes 786440 | tf_op jit(solution)/shard_map/ppermute | solution.py:304
  4.5 7.2 %collective-permute-start.5 = (bf16[8,1024]{1,0:T(8,128)(2,1)S(1)}, bf16[8,1024]{1,0:T(8,128)(2,1)S(1)}, u32[]{:S(2)}, u32[]{:S(2)}) collective-permute-start(bf16[8,1024]{1,0:T(8,128)(2,1)S(1)} %shard_map.105.refs_1_), channel_id=1, source_target_pairs={{0,1},{1,3},{3,2},{2,0},{4,5},{5,7},{7,6},{6,4},{8,9},{9,11},{11,1... | collective-permute-start | bytes 49160 | tf_op jit(solution)/shard_map/ppermute | solution.py:304
  7.1 4.1 %collective-permute-start = (bf16[16,1024]{1,0:T(8,128)(2,1)}, bf16[16,1024]{1,0:T(8,128)(2,1)S(1)}, u32[]{:S(2)}, u32[]{:S(2)}) collective-permute-start(bf16[16,1024]{1,0:T(8,128)(2,1)} %refs_0_.7), channel_id=1, source_target_pairs={{0,4},{4,0},{8,12},{12,8},{16,20},{20,16},{24,28},{28,24},{1,5},{5... | collective-permute-start | bytes 98312 | tf_op jit(solution)/shard_map/ppermute | solution.py:310
  7.1 1.6 %copy-start = (bf16[1024,1024]{1,0:T(8,128)(2,1)S(1)}, bf16[1024,1024]{1,0:T(8,128)(2,1)}, u32[]{:S(2)}) copy-start(bf16[1024,1024]{1,0:T(8,128)(2,1)} %refs_0_.13) | copy-start | bytes 6291460
  8.7 1.2 %copy-start.2 = (bf16[512,1024]{1,0:T(8,128)(2,1)S(1)}, bf16[512,1024]{1,0:T(8,128)(2,1)}, u32[]{:S(2)}) copy-start(bf16[512,1024]{1,0:T(8,128)(2,1)} %refs_0_.9) | copy-start | bytes 3145732
  9.9 1.3 %copy-start.5 = (bf16[16,1024]{1,0:T(8,128)(2,1)S(1)}, bf16[16,1024]{1,0:T(8,128)(2,1)}, u32[]{:S(2)}) copy-start(bf16[16,1024]{1,0:T(8,128)(2,1)} %refs_0_.7) | copy-start | bytes 98308
  11.6 17.3 %copy-start.1 = (bf16[1024,1024]{1,0:T(8,128)(2,1)S(1)}, bf16[1024,1024]{1,0:T(8,128)(2,1)}, u32[]{:S(2)}) copy-start(bf16[1024,1024]{1,0:T(8,128)(2,1)} %refs_0_.13) | copy-start | bytes 6291460
  11.7 17.3 %copy-start.3 = (bf16[128,1024]{1,0:T(8,128)(2,1)S(1)}, bf16[128,1024]{1,0:T(8,128)(2,1)}, u32[]{:S(2)}) copy-start(bf16[128,1024]{1,0:T(8,128)(2,1)} %refs_0_.10) | copy-start | bytes 786436
  11.7 9.7 %collective-permute-start.6 = (bf16[136,1024]{1,0:T(8,128)(2,1)S(1)}, bf16[136,1024]{1,0:T(8,128)(2,1)S(1)}, u32[]{:S(2)}, u32[]{:S(2)}) collective-permute-start(bf16[136,1024]{1,0:T(8,128)(2,1)S(1)} %shard_map.108.refs_1_), channel_id=1, source_target_pairs={{0,1},{1,3},{3,2},{2,0},{4,5},{5,7},{7,6},{6,4},{8,9},{9,11},{11,1... | collective-permute-start | bytes 835592 | tf_op jit(solution)/shard_map/ppermute | solution.py:304
  21.3 15.2 %collective-permute-start.7 = (bf16[136,1024]{1,0:T(8,128)(2,1)S(1)}, bf16[136,1024]{1,0:T(8,128)(2,1)S(1)}, u32[]{:S(2)}, u32[]{:S(2)}) collective-permute-start(bf16[136,1024]{1,0:T(8,128)(2,1)S(1)} %collective-permute-done.6.refs_1_), channel_id=1, source_target_pairs={{0,1},{1,3},{3,2},{2,0},{4,5},{5,7},{7,6},{6,4},{8,9},{9,11},{11,1... | collective-permute-start | bytes 835592 | tf_op jit(solution)/shard_map/ppermute | solution.py:304
  22.3 11.2 %copy-start.4 = (s32[64,64]{1,0:T(8,128)S(1)}, s32[64,64]{1,0:T(8,128)}, u32[]{:S(2)}) copy-start(s32[64,64]{1,0:T(8,128)} %refs_3_.2) | copy-start | bytes 49156
  22.3 11.2 %copy-start.6 = (s32[128]{0:T(128)S(1)}, s32[128]{0:T(128)}, u32[]{:S(2)}) copy-start(s32[128]{0:T(128)} %param.13) | copy-start | bytes 1540
  22.3 14.9 %collective-permute-start.16 = (bf16[136,1024]{1,0:T(8,128)(2,1)S(1)}, bf16[136,1024]{1,0:T(8,128)(2,1)S(1)}, u32[]{:S(2)}, u32[]{:S(2)}) collective-permute-start(bf16[136,1024]{1,0:T(8,128)(2,1)S(1)} %shard_map.119), channel_id=1, source_target_pairs={{0,1},{1,3},{3,2},{2,0},{4,5},{5,7},{7,6},{6,4},{8,9},{9,11},{11,1... | collective-permute-start | bytes 835592 | tf_op jit(solution)/shard_map/ppermute | solution.py:304
  25.4 5.3 %collective-permute-start.3 = (bf16[2,16,1024]{2,1,0:T(8,128)(2,1)S(1)}, bf16[2,16,1024]{2,1,0:T(8,128)(2,1)S(1)}, u32[]{:S(2)}, u32[]{:S(2)}) collective-permute-start(bf16[2,16,1024]{2,1,0:T(8,128)(2,1)S(1)} %shard_map.103.refs_4_), channel_id=1, source_target_pairs={{0,24},{4,28},{8,0},{12,4},{16,8},{20,12},{24,16},{28,20},{1,25},{... | collective-permute-start | bytes 196616 | tf_op jit(solution)/shard_map/ppermute | solution.py:313
  27.8 4.3 %collective-permute-start.2 = (bf16[2,16,1024]{2,1,0:T(8,128)(2,1)S(1)}, bf16[2,16,1024]{2,1,0:T(8,128)(2,1)S(1)}, u32[]{:S(2)}, u32[]{:S(2)}) collective-permute-start(bf16[2,16,1024]{2,1,0:T(8,128)(2,1)S(1)} %shard_map.103.refs_4_), channel_id=1, source_target_pairs={{0,16},{4,20},{8,24},{12,28},{16,0},{20,4},{24,8},{28,12},{1,17},{... | collective-permute-start | bytes 196616 | tf_op jit(solution)/shard_map/ppermute | solution.py:313
  28.3 5.2 %collective-permute-start.1 = (bf16[2,16,1024]{2,1,0:T(8,128)(2,1)S(1)}, bf16[2,16,1024]{2,1,0:T(8,128)(2,1)S(1)}, u32[]{:S(2)}, u32[]{:S(2)}) collective-permute-start(bf16[2,16,1024]{2,1,0:T(8,128)(2,1)S(1)} %shard_map.103.refs_4_), channel_id=1, source_target_pairs={{0,8},{4,12},{8,16},{12,20},{16,24},{20,28},{24,0},{28,4},{1,9},{5... | collective-permute-start | bytes 196616 | tf_op jit(solution)/shard_map/ppermute | solution.py:313
  37.1 20.4 %collective-permute-start.15 = (bf16[128,1024]{1,0:T(8,128)(2,1)S(1)}, bf16[128,1024]{1,0:T(8,128)(2,1)S(1)}, u32[]{:S(2)}, u32[]{:S(2)}) collective-permute-start(bf16[128,1024]{1,0:T(8,128)(2,1)S(1)} %shard_map.118), channel_id=1, source_target_pairs={{0,2},{1,0},{3,1},{2,3},{4,6},{5,4},{7,5},{6,7},{8,10},{9,8},{11,9... | collective-permute-start | bytes 786440 | tf_op jit(solution)/shard_map/ppermute | solution.py:304
  37.2 12.0 %copy-start.7 = (s32[128]{0:T(128)S(1)}, s32[128]{0:T(128)}, u32[]{:S(2)}) copy-start(s32[128]{0:T(128)} %param.14) | copy-start | bytes 1540
  37.6 19.9 %collective-permute-start.17 = (bf16[128,1024]{1,0:T(8,128)(2,1)S(1)}, bf16[128,1024]{1,0:T(8,128)(2,1)S(1)}, u32[]{:S(2)}, u32[]{:S(2)}) collective-permute-start(bf16[128,1024]{1,0:T(8,128)(2,1)S(1)} %shard_map.120), channel_id=1, source_target_pairs={{0,1},{1,3},{3,2},{2,0},{4,5},{5,7},{7,6},{6,4},{8,9},{9,11},{11,1... | collective-permute-start | bytes 786440 | tf_op jit(solution)/shard_map/ppermute | solution.py:304
  39.6 6.8 %collective-permute-start.10 = (f32[10,128]{1,0:T(8,128)S(1)}, f32[10,128]{1,0:T(8,128)S(1)}, u32[]{:S(2)}, u32[]{:S(2)}) collective-permute-start(f32[10,128]{1,0:T(8,128)S(1)} %shard_map.114.refs_2_.refs_6_.refs_0_), channel_id=1, source_target_pairs={{0,2},{1,0},{3,1},{2,3},{4,6},{5,4},{7,5},{6,7},{8,10},{9,8},{11,9... | collective-permute-start | bytes 15368 | tf_op jit(solution)/shard_map/ppermute | solution.py:304
  40.6 8.5 %collective-permute-start.9 = (f32[10,128]{1,0:T(8,128)S(1)}, f32[10,128]{1,0:T(8,128)S(1)}, u32[]{:S(2)}, u32[]{:S(2)}) collective-permute-start(f32[10,128]{1,0:T(8,128)S(1)} %shard_map.114.refs_2_.refs_6_.refs_0_), channel_id=1, source_target_pairs={{0,3},{1,2},{3,0},{2,1},{4,7},{5,6},{7,4},{6,5},{8,11},{9,10},{11,... | collective-permute-start | bytes 15368 | tf_op jit(solution)/shard_map/ppermute | solution.py:304
  43.0 6.3 %collective-permute-start.8 = (f32[10,128]{1,0:T(8,128)S(1)}, f32[10,128]{1,0:T(8,128)S(1)}, u32[]{:S(2)}, u32[]{:S(2)}) collective-permute-start(f32[10,128]{1,0:T(8,128)S(1)} %shard_map.114.refs_2_.refs_6_.refs_0_), channel_id=1, source_target_pairs={{0,1},{1,3},{3,2},{2,0},{4,5},{5,7},{7,6},{6,4},{8,9},{9,11},{11,1... | collective-permute-start | bytes 15368 | tf_op jit(solution)/shard_map/ppermute | solution.py:304
  49.6 1.4 %collective-permute-start.11 = (bf16[64,1024]{1,0:T(8,128)(2,1)S(1)}, bf16[64,1024]{1,0:T(8,128)(2,1)S(1)}, u32[]{:S(2)}, u32[]{:S(2)}) collective-permute-start(bf16[64,1024]{1,0:T(8,128)(2,1)S(1)} %get-tuple-element.45), channel_id=1, source_target_pairs={{0,4},{4,0},{8,12},{12,8},{16,20},{20,16},{24,28},{28,24},{1,5},{5... | collective-permute-start | bytes 393224 | tf_op jit(solution)/shard_map/ppermute | solution.py:310
  51.0 6.2 %collective-permute-start.12 = (bf16[16,1024]{1,0:T(8,128)(2,1)S(1)}, bf16[16,1024]{1,0:T(8,128)(2,1)S(1)}, u32[]{:S(2)}, u32[]{:S(2)}) collective-permute-start(bf16[16,1024]{1,0:T(8,128)(2,1)S(1)} %get-tuple-element.47), channel_id=1, source_target_pairs={{0,8},{4,12},{8,16},{12,20},{16,24},{20,28},{24,0},{28,4},{1,9},{5... | collective-permute-start | bytes 98312 | tf_op jit(solution)/shard_map/ppermute | solution.py:313
  51.6 5.7 %collective-permute-start.13 = (bf16[16,1024]{1,0:T(8,128)(2,1)S(1)}, bf16[16,1024]{1,0:T(8,128)(2,1)S(1)}, u32[]{:S(2)}, u32[]{:S(2)}) collective-permute-start(bf16[16,1024]{1,0:T(8,128)(2,1)S(1)} %get-tuple-element.48), channel_id=1, source_target_pairs={{0,16},{4,20},{8,24},{12,28},{16,0},{20,4},{24,8},{28,12},{1,17},{... | collective-permute-start | bytes 98312 | tf_op jit(solution)/shard_map/ppermute | solution.py:313
  53.6 3.9 %collective-permute-start.14 = (bf16[16,1024]{1,0:T(8,128)(2,1)S(1)}, bf16[16,1024]{1,0:T(8,128)(2,1)S(1)}, u32[]{:S(2)}, u32[]{:S(2)}) collective-permute-start(bf16[16,1024]{1,0:T(8,128)(2,1)S(1)} %get-tuple-element.49), channel_id=1, source_target_pairs={{0,24},{4,28},{8,0},{12,4},{16,8},{20,12},{24,16},{28,20},{1,25},{... | collective-permute-start | bytes 98312 | tf_op jit(solution)/shard_map/ppermute | solution.py:313
